TPU v7x, 32 devices: a whole 2x2x4 slice. The times are simulated.
32 devices in a mesh: section: 4 (over x, core), dp: 8 (over z, y).
Axes of the slice: x: 2, y: 2, z: 4, core: 2. Of those that a mesh axis runs over, the one named last changes fastest.
Arguments:
- text_ids: int32 [24, 77], P('dp'), may hold values from 0 to 12351
- seed_ids: int32 [24], P('dp'), may hold values from 0 to 1023
- text_table: bfloat16 [12352, 512], P('dp'), may hold values from -16 to 16
- latent_table: float32 [1024, 512], replicated, may hold values from -6 to 6
- start_map: bfloat16 [512, 256], replicated, may hold values from -6 to 6
- style_weight: bfloat16 [4, 512, 512], P('section'), may hold values from -0.25 to 0.25
- conv_weight: bfloat16 [4, 512, 9, 512], P('section'), may hold values from -1 to 1
- score_head: float32 [512], replicated, may hold values from -6 to 6
Outputs:
- conv_grad: float32 [4, 512, 9, 512], P('section', 'dp')
All inputs are finite; a program needn't handle non-finite values.
Results may differ from a plain program's by a relative error of at most 0.01.
Values may be sent and summed in bfloat16 or wider, within the bound.
No kernel may reach another device: no remote copies, remote signals or barrier semaphores. Data moves between devices by JAX's collectives and lax.ppermute only.
A program may use at most 128 MiB of HBM per device.

v0:
```python
import math

import jax
import jax.numpy as jnp
from jax import lax
from jax.sharding import PartitionSpec as P

RES = 16
TXT_LEN = 77


OFFSETS = tuple(((index_k // 3 - 1, index_k % 3 - 1) for index_k in range(9)))


def from_behind(x, axis, by):
    devices = lax.axis_size(axis)
    pairs = [(i, i + by) for i in range(devices) if 0 <= i + by < devices]
    return lax.ppermute(x, axis, pairs)


def spread(feature, side_len):
    pixels = side_len * side_len
    column = lax.broadcasted_iota(jnp.int32, (1, pixels), 1) % side_len
    padded = jnp.pad(feature, ((0, 0), (side_len + 1, side_len + 1)))
    pieces = []
    for shift_down, shift_right in OFFSETS:
        offset = side_len + 1 + shift_down * side_len + shift_right
        inside = ((column + shift_right >= 0) & (column + shift_right < side_len)).astype(
            feature.dtype
        )
        pieces.append(lax.slice_in_dim(padded, offset, offset + pixels, axis=1) * inside)
    return jnp.concatenate(pieces, axis=0)


def spread_back(pieces, channels, side_len):
    pixels = side_len * side_len
    column = lax.broadcasted_iota(jnp.int32, (1, pixels), 1) % side_len
    result = jnp.zeros((channels, pixels), pieces.dtype)
    for index_k, (shift_down, shift_right) in enumerate(OFFSETS):
        inside = ((column + shift_right >= 0) & (column + shift_right < side_len)).astype(
            pieces.dtype
        )
        masked = pieces[index_k * channels : (index_k + 1) * channels] * inside
        padded = jnp.pad(masked, ((0, 0), (side_len + 1, side_len + 1)))
        begin_at = side_len + 1 - shift_down * side_len - shift_right
        result = result + lax.slice_in_dim(padded, begin_at, begin_at + pixels, axis=1)
    return result


def on_device(
    text_ids, seed_ids, text_table, latent_table, start_map, style_weight, conv_weight, score_head
):
    sections = lax.axis_size("section")
    gen_count = sections - sections // 4
    section_at = lax.axis_index("section")
    is_gen = section_at < gen_count
    is_last = section_at == sections - 1
    at_border = section_at == gen_count - 1
    micro_count = seed_ids.shape[0]
    channels = start_map.shape[0]
    pixels = start_map.shape[1]
    side_len = RES
    vocab_rows = text_table.shape[0]
    norm_div = pixels * math.sqrt(channels)
    whole_ids = lax.all_gather(text_ids, "dp", axis=0, tiled=True)
    first_row = lax.axis_index("dp") * vocab_rows
    wanted = whole_ids - first_row
    inside = (wanted >= 0) & (wanted < vocab_rows)
    picked = jnp.take(text_table, jnp.clip(wanted, 0, vocab_rows - 1), axis=0)
    picked = jnp.where(inside[:, :, None], picked, jnp.zeros((), picked.dtype))
    text_mean = lax.psum_scatter(
        (jnp.sum(picked.astype(jnp.float32), axis=1) / TXT_LEN).astype(jnp.bfloat16),
        "dp",
        scatter_dimension=0,
        tiled=True,
    ).astype(jnp.float32)
    latent = jnp.take(latent_table, seed_ids, axis=0) + text_mean
    code_now = jnp.where(is_gen, latent, text_mean).astype(jnp.bfloat16)
    styles = 1.0 + lax.dot_general(
        code_now, style_weight[0], (((1,), (1,)), ((), ())), preferred_element_type=jnp.float32
    )
    weight = conv_weight[0]
    flat_weight = weight.reshape(channels, 9 * channels)
    squares = jnp.sum(jnp.square(weight.astype(jnp.float32)), axis=1)
    demods = lax.rsqrt(jnp.dot(styles * styles, squares.T, precision=lax.Precision.HIGHEST) + 1e-08)
    demods = jnp.where(is_gen, demods, jnp.ones_like(demods))
    blank_map = jnp.zeros((channels, pixels), jnp.bfloat16)
    ticks = micro_count + sections - 1

    def forward_step(state_in, tick_no):
        outgoing, kept_input, kept_conv, scores = state_in
        received = from_behind(outgoing, "section", 1)
        position = tick_no - section_at
        active = (position >= 0) & (position < micro_count)
        position = jnp.clip(position, 0, micro_count - 1)
        source = jnp.where(section_at == 0, start_map, received)

        def forward_compute(kept_all):
            kept_input, kept_conv, scores = kept_all
            mod_input = (styles[position][:, None] * source.astype(jnp.float32)).astype(
                jnp.bfloat16
            )
            conv_out = jnp.dot(
                flat_weight, spread(mod_input, side_len), preferred_element_type=jnp.float32
            )
            result_map = jax.nn.silu(demods[position][:, None] * conv_out).astype(jnp.bfloat16)
            sample_score = (
                jnp.sum(jnp.sum(result_map.astype(jnp.float32), axis=1) * score_head) / norm_div
            )
            kept_input = lax.dynamic_update_index_in_dim(kept_input, mod_input, position, 0)
            kept_conv = lax.dynamic_update_index_in_dim(kept_conv, conv_out, position, 0)
            scores = lax.dynamic_update_index_in_dim(scores, sample_score, position, 0)
            return (result_map, kept_input, kept_conv, scores)

        def forward_skipped(kept_all):
            return (blank_map,) + kept_all

        return (
            lax.cond(active, forward_compute, forward_skipped, (kept_input, kept_conv, scores)),
            None,
        )

    start_state = (
        blank_map,
        jnp.zeros((micro_count, channels, pixels), jnp.bfloat16),
        jnp.zeros((micro_count, channels, pixels), jnp.float32),
        jnp.zeros((micro_count,), jnp.float32),
    )
    forward_done = lax.scan(forward_step, start_state, jnp.arange(ticks))[0]
    kept_input = forward_done[1]
    kept_conv = forward_done[2]
    scores = forward_done[3]
    d_all = jax.nn.sigmoid(scores).astype(jnp.bfloat16)
    g_all = (-jax.nn.sigmoid(-scores)).astype(jnp.bfloat16)
    unit_cot = jnp.broadcast_to(
        (score_head / norm_div).astype(jnp.bfloat16)[:, None], (channels, pixels)
    )
    grad_store = jnp.zeros((channels, 9 * channels), jnp.float32)

    def backward_step(state_in, tick_no):
        outgoing, outgoing_factors, mixture, grad_store = state_in
        received, received_factors = from_behind((outgoing, outgoing_factors), "section", -1)
        position = tick_no - (sections - 1 - section_at)
        active = (position >= 0) & (position < micro_count)
        position = jnp.clip(position, 0, micro_count - 1)
        own_factors = jnp.stack([d_all[position], g_all[position]])
        factors_now = jnp.where(is_last, own_factors, received_factors)
        arriving = jnp.where(is_last, unit_cot, received)

        def backward_compute(kept_all):
            mixture, grad_store = kept_all
            mod_input = kept_input[position]
            conv_out = kept_conv[position]
            style_row = styles[position]
            demod_row = demods[position]
            boost = jnp.where(at_border, factors_now[1].astype(jnp.float32), 1.0)
            incoming = arriving.astype(jnp.float32) * boost
            pre_act = demod_row[:, None] * conv_out
            sigmas = jax.nn.sigmoid(pre_act)
            grad_pre = incoming * sigmas * (1.0 + pre_act * (1.0 - sigmas))
            grad_conv = (demod_row[:, None] * grad_pre).astype(jnp.bfloat16)
            grad_demod = jnp.sum(grad_pre * conv_out, axis=1)
            demod_term = jnp.where(is_gen, grad_demod * demod_row * demod_row * demod_row, 0.0)
            mixture = mixture + demod_term[:, None] * (style_row * style_row)[None, :]
            weight_scale = jnp.where(is_gen, 1.0, factors_now[0].astype(jnp.float32))
            term_now = lax.dot_general(
                grad_conv,
                spread(mod_input, side_len),
                (((1,), (1,)), ((), ())),
                preferred_element_type=jnp.float32,
            )
            grad_store = grad_store + weight_scale * term_now
            back_prod = lax.dot_general(
                flat_weight, grad_conv, (((0,), (0,)), ((), ())), preferred_element_type=jnp.float32
            )
            sent_map = (style_row[:, None] * spread_back(back_prod, channels, side_len)).astype(
                jnp.bfloat16
            )
            return (sent_map, factors_now, mixture, grad_store)

        def backward_skipped(kept_all):
            return (blank_map, factors_now) + kept_all

        return (lax.cond(active, backward_compute, backward_skipped, (mixture, grad_store)), None)

    back_state = (
        blank_map,
        jnp.zeros((2,), jnp.bfloat16),
        jnp.zeros((channels, channels), jnp.float32),
        grad_store,
    )
    back_done = lax.scan(backward_step, back_state, jnp.arange(ticks))[0]
    mixture = back_done[2]
    grad_store = back_done[3]
    full_grad = (
        grad_store.reshape(channels, 9, channels) - weight.astype(jnp.float32) * mixture[:, None, :]
    )
    share = lax.psum_scatter(
        full_grad.astype(jnp.bfloat16), "dp", scatter_dimension=0, tiled=True
    ).astype(jnp.float32)
    return share[None]


def solution(mesh):
    placed = (
        P("dp", None),
        P("dp"),
        P("dp", None),
        P(),
        P(),
        P("section", None, None),
        P("section", None, None, None),
        P(),
    )
    return jax.shard_map(
        on_device,
        mesh=mesh,
        in_specs=placed,
        out_specs=P("section", "dp", None, None),
        check_vma=False,
    )
```

profile of v0, /device:TPU:0, one launch (start us, length us, event | category | flops | bytes accessed | tf_op | source)
XLA Modules:
  0.0 556.0 jit_solution(12567117041173258758)
XLA Ops:
  6.5 28.2 %all-gather = s32[8,3,77]{2,1,0:T(4,128)S(1)} all-gather(s32[1,3,77]{2,1,0:T(4,128)} %bitcast.78), channel_id=1, replica_groups=mesh['section'=4,'dp'=8] {'dp'}, dimensions={0}, use_global_device_ids=true | all-gather | bytes 8316 | tf_op jit(solution)/shard_map/all_gather | solution.py:65
  36.2 8.5 %gather_fusion.1 = bf16[1848,512]{1,0:T(8,128)(2,1)} fusion(bf16[1544,512]{1,0:T(8,128)(2,1)} %param.18, s32[2048]{0:T(1024)S(1)} %pad_clamp_fusion), kind=kCustom, calls=%fused_computation.1 | custom fusion | bytes 3792096 | tf_op jit(solution)/shard_map/jit(_take)/gather | solution.py:69
  44.7 3.8 reshape.155
  48.6 2.2 convert_reduce_fusion.1
  50.8 35.4 %all-reduce.10 = bf16[24,512]{1,0:T(8,128)(2,1)S(1)} all-reduce(bf16[24,512]{1,0:T(8,128)(2,1)S(1)} %multiply_convert_fusion.5), channel_id=2, replica_groups=mesh['section'=4,'dp'=8] {'dp'}, use_global_device_ids=true, to_apply=%region_1.2.clone | all-reduce | flops 12288 | bytes 49152
  86.3 6.7 %copy.25 = bf16[1,512,9,512]{1,3,2,0:T(8,128)(2,1)} copy(bf16[1,512,9,512]{3,1,2,0:T(8,128)(2,1)} %param.22) | data formatting | bytes 9437184 | tf_op args[6]
  93.0 3.4 fusion.52
  96.4 6.7 %copy.27 = bf16[512,4608]{1,0:T(8,128)(2,1)} copy(bf16[512,4608]{0,1:T(8,128)(2,1)} %bitcast.68) | data formatting | bytes 9437184 | tf_op jit(solution)/shard_map/while | solution.py:129
  107.8 65.5 %while.36 = (s32[]{:T(128)}, bf16[512,256]{0,1:T(8,128)(2,1)}, bf16[3,512,256]{2,1,0:T(8,128)(2,1)S(1)}, f32[3,512,256]{1,2,0:T(8,128)S(1)}, f32[3]{0:T(128)S(1)...) while((s32[]{:T(128)}, bf16[512,256]{0,1:T(8,128)(2,1)}, ...), condition=%wide.region_8.9_spmd, body=%wide.region_3.8_spmd.sunk | while | flops 1214258176 | bytes 35152344 | solution.py:129
  108.9 1.3 collective-permute-start
  111.5 6.2 %conditional.5 = (bf16[512,256]{0,1:T(8,128)(2,1)}, bf16[3,512,256]{2,1,0:T(8,128)(2,1)S(1)}, f32[3,512,256]{1,2,0:T(8,128)S(1)}, f32[3]{0:T(128)S(1)}) conditional(s32[]{:T(128)} %convert_element_type.275, (bf16[3,512,256]{2,1,0:T(8,128)(2,1)S(1)}, f32[3,512,256]{1,2,0:T(8,128)S(1)}, f32[3]{0:T(128)S(1)}) %tuple.99, (s32[]{:T(128)}, ...), branch_computations={%region_4.4_spmd, %region_5.7_spmd} | conditional | flops 1214258176 | bytes 33579132 | solution.py:119
  114.0 2.2 convert_reduce_fusion
  118.8 1.3 collective-permute-start
  121.3 6.2 %conditional.5 = (bf16[512,256]{0,1:T(8,128)(2,1)}, bf16[3,512,256]{2,1,0:T(8,128)(2,1)S(1)}, f32[3,512,256]{1,2,0:T(8,128)S(1)}, f32[3]{0:T(128)S(1)}) conditional(s32[]{:T(128)} %convert_element_type.275, (bf16[3,512,256]{2,1,0:T(8,128)(2,1)S(1)}, f32[3,512,256]{1,2,0:T(8,128)S(1)}, f32[3]{0:T(128)S(1)}) %tuple.99, (s32[]{:T(128)}, ...), branch_computations={%region_4.4_spmd, %region_5.7_spmd} | conditional | flops 1214258176 | bytes 33579132 | solution.py:119
  123.9 2.2 convert_reduce_fusion
  128.6 5.8 %collective-permute-start = (bf16[512,256]{1,0:T(8,128)(2,1)S(1)}, bf16[512,256]{1,0:T(8,128)(2,1)S(1)}, u32[]{:S(2)}, u32[]{:S(2)}) collective-permute-start(bf16[512,256]{1,0:T(8,128)(2,1)S(1)} %copy.36), channel_id=1, source_target_pairs={{0,8},{8,16},{16,24},{1,9},{9,17},{17,25},{2,10},{10,18},{18,26},{... | collective-permute-start | bytes 786440 | tf_op jit(solution)/shard_map/while/body/eval_jaxpr/ppermute | solution.py:18
  135.7 6.2 %conditional.5 = (bf16[512,256]{0,1:T(8,128)(2,1)}, bf16[3,512,256]{2,1,0:T(8,128)(2,1)S(1)}, f32[3,512,256]{1,2,0:T(8,128)S(1)}, f32[3]{0:T(128)S(1)}) conditional(s32[]{:T(128)} %convert_element_type.275, (bf16[3,512,256]{2,1,0:T(8,128)(2,1)S(1)}, f32[3,512,256]{1,2,0:T(8,128)S(1)}, f32[3]{0:T(128)S(1)}) %tuple.99, (s32[]{:T(128)}, ...), branch_computations={%region_4.4_spmd, %region_5.7_spmd} | conditional | flops 1214258176 | bytes 33579132 | solution.py:119
  138.2 2.2 convert_reduce_fusion
  143.0 3.9 collective-permute-start
  150.0 11.9 %collective-permute-start = (bf16[512,256]{1,0:T(8,128)(2,1)S(1)}, bf16[512,256]{1,0:T(8,128)(2,1)S(1)}, u32[]{:S(2)}, u32[]{:S(2)}) collective-permute-start(bf16[512,256]{1,0:T(8,128)(2,1)S(1)} %copy.36), channel_id=1, source_target_pairs={{0,8},{8,16},{16,24},{1,9},{9,17},{17,25},{2,10},{10,18},{18,26},{... | collective-permute-start | bytes 786440 | tf_op jit(solution)/shard_map/while/body/eval_jaxpr/ppermute | solution.py:18
  164.9 6.4 %collective-permute-start = (bf16[512,256]{1,0:T(8,128)(2,1)S(1)}, bf16[512,256]{1,0:T(8,128)(2,1)S(1)}, u32[]{:S(2)}, u32[]{:S(2)}) collective-permute-start(bf16[512,256]{1,0:T(8,128)(2,1)S(1)} %copy.36), channel_id=1, source_target_pairs={{0,8},{8,16},{16,24},{1,9},{9,17},{17,25},{2,10},{10,18},{18,26},{... | collective-permute-start | bytes 786440 | tf_op jit(solution)/shard_map/while/body/eval_jaxpr/ppermute | solution.py:18
  174.5 1.9 copy.28
  176.4 4.8 broadcast_in_dim.94
  183.0 184.8 %while.37 = (s32[]{:T(128)}, bf16[512,256]{0,1:T(8,128)(2,1)}, bf16[2]{0:T(256)(128)(2,1)S(1)}, f32[512,512]{1,0:T(8,128)}, f32[512,4608]{1,0:T(8,128)}, /*index...) while((s32[]{:T(128)}, bf16[512,256]{0,1:T(8,128)(2,1)}, ...), condition=%wide.region_13.14_spmd.clone, body=%wide.region_9.13_spmd.clone.sunk | while | flops 2433886976 | bytes 78953192 | solution.py:192
  184.1 1.3 collective-permute-start.1
  185.4 1.3 collective-permute-start.2
  189.3 9.2 %collective-permute-done.2 = bf16[2]{0:T(256)(128)(2,1)S(1)} collective-permute-done((bf16[2]{0:T(256)(128)(2,1)S(1)}, bf16[2]{0:T(256)(128)(2,1)S(1)}, u32[]{:S(2)}, u32[]{:S(2)}) %collective-permute-start.2) | collective-permute-done | bytes 36 | tf_op jit(solution)/shard_map/while/body/eval_jaxpr/ppermute | solution.py:18
  198.6 1.3 broadcast_select_fusion.5
  201.7 1.3 collective-permute-start.1
  206.9 3.3 collective-permute-done.2
  210.2 1.3 broadcast_select_fusion.5
  213.3 1.3 collective-permute-start.1
  218.6 2.6 collective-permute-done.2
  221.1 1.3 broadcast_select_fusion.5
  229.5 55.9 %collective-permute-done.2 = bf16[2]{0:T(256)(128)(2,1)S(1)} collective-permute-done((bf16[2]{0:T(256)(128)(2,1)S(1)}, bf16[2]{0:T(256)(128)(2,1)S(1)}, u32[]{:S(2)}, u32[]{:S(2)}) %collective-permute-start.2) | collective-permute-done | bytes 36 | tf_op jit(solution)/shard_map/while/body/eval_jaxpr/ppermute | solution.py:18
  285.3 1.3 broadcast_select_fusion.5
  286.6 20.3 %conditional.6 = (bf16[512,256]{0,1:T(8,128)(2,1)}, f32[512,512]{1,0:T(8,128)}, f32[512,4608]{1,0:T(8,128)}) conditional(s32[]{:T(128)} %convert_element_type.276, (f32[512,512]{1,0:T(8,128)}, f32[512,4608]{1,0:T(8,128)}) %tuple.102, (s32[]{:T(128)}, f32[3,512]{1,0:T(4,128)S(1)}, f32[3,512]{1,0:T(4,128)S(1)}, pred[]{:T(512)}, ...), branch_computations={%region_10.10_spmd, %region_11.12_spmd} | conditional | flops 2433886976 | bytes 77379784 | solution.py:184
  288.0 1.4 copy-done.3
  291.3 9.8 %multiply_add_fusion = f32[512,4608]{1,0:T(8,128)} fusion(f32[512,4608]{1,0:T(8,128)} %get-tuple-element.430, bf16[4608,256]{1,0:T(8,128)(2,1)} %copy-done.3, f32[]{:T(128)S(6)} %select_n.184, f32[512]{0:T(512)S(1)} %bitcast.70, f32[3,512,256]{2,1,0:T(8,128)S(1)} %get-tuple-element.426, s32[]{:T(128)S(6)} %select_n.169, f32[]{:T(128)S(6)} %select_n.172, ...), kind=kOutput, calls=%fused_computation.41 | convolution fusion | flops 1214513152 | bytes 22023180 | tf_op jit(solution)/shard_map/while/body/eval_jaxpr/cond/branch_1_fun/dot_general | solution.py:166
  301.0 1.6 convolution_bitcast_fusion
  304.6 2.4 multiply_add_fusion.1
  308.0 1.3 collective-permute-start.1
  313.2 2.6 collective-permute-done.2
  315.8 1.3 broadcast_select_fusion.5
  317.1 20.3 %conditional.6 = (bf16[512,256]{0,1:T(8,128)(2,1)}, f32[512,512]{1,0:T(8,128)}, f32[512,4608]{1,0:T(8,128)}) conditional(s32[]{:T(128)} %convert_element_type.276, (f32[512,512]{1,0:T(8,128)}, f32[512,4608]{1,0:T(8,128)}) %tuple.102, (s32[]{:T(128)}, f32[3,512]{1,0:T(4,128)S(1)}, f32[3,512]{1,0:T(4,128)S(1)}, pred[]{:T(512)}, ...), branch_computations={%region_10.10_spmd, %region_11.12_spmd} | conditional | flops 2433886976 | bytes 77379784 | solution.py:184
  318.5 1.4 copy-done.3
  321.7 9.8 %multiply_add_fusion = f32[512,4608]{1,0:T(8,128)} fusion(f32[512,4608]{1,0:T(8,128)} %get-tuple-element.430, bf16[4608,256]{1,0:T(8,128)(2,1)} %copy-done.3, f32[]{:T(128)S(6)} %select_n.184, f32[512]{0:T(512)S(1)} %bitcast.70, f32[3,512,256]{2,1,0:T(8,128)S(1)} %get-tuple-element.426, s32[]{:T(128)S(6)} %select_n.169, f32[]{:T(128)S(6)} %select_n.172, ...), kind=kOutput, calls=%fused_computation.41 | convolution fusion | flops 1214513152 | bytes 22023180 | tf_op jit(solution)/shard_map/while/body/eval_jaxpr/cond/branch_1_fun/dot_general | solution.py:166
  331.5 1.6 convolution_bitcast_fusion
  335.0 2.4 multiply_add_fusion.1
  338.5 1.3 collective-permute-start.1
  343.7 2.6 collective-permute-done.2
  346.2 1.3 broadcast_select_fusion.5
  347.6 20.3 %conditional.6 = (bf16[512,256]{0,1:T(8,128)(2,1)}, f32[512,512]{1,0:T(8,128)}, f32[512,4608]{1,0:T(8,128)}) conditional(s32[]{:T(128)} %convert_element_type.276, (f32[512,512]{1,0:T(8,128)}, f32[512,4608]{1,0:T(8,128)}) %tuple.102, (s32[]{:T(128)}, f32[3,512]{1,0:T(4,128)S(1)}, f32[3,512]{1,0:T(4,128)S(1)}, pred[]{:T(512)}, ...), branch_computations={%region_10.10_spmd, %region_11.12_spmd} | conditional | flops 2433886976 | bytes 77379784 | solution.py:184
  348.9 1.4 copy-done.3
  352.2 9.8 %multiply_add_fusion = f32[512,4608]{1,0:T(8,128)} fusion(f32[512,4608]{1,0:T(8,128)} %get-tuple-element.430, bf16[4608,256]{1,0:T(8,128)(2,1)} %copy-done.3, f32[]{:T(128)S(6)} %select_n.184, f32[512]{0:T(512)S(1)} %bitcast.70, f32[3,512,256]{2,1,0:T(8,128)S(1)} %get-tuple-element.426, s32[]{:T(128)S(6)} %select_n.169, f32[]{:T(128)S(6)} %select_n.172, ...), kind=kOutput, calls=%fused_computation.41 | convolution fusion | flops 1214513152 | bytes 22023180 | tf_op jit(solution)/shard_map/while/body/eval_jaxpr/cond/branch_1_fun/dot_general | solution.py:166
  362.0 1.6 convolution_bitcast_fusion
  365.5 2.4 multiply_add_fusion.1
  367.8 9.6 %copy.30 = f32[512,4608]{0,1:T(8,128)} copy(f32[512,4608]{1,0:T(8,128)} %get-tuple-element.462) | data formatting | bytes 18874368 | tf_op jit(solution)/shard_map/while | solution.py:192
  377.4 1.6 copy.31
  379.0 9.2 %fusion.54 = bf16[512,9,512]{0,2,1:T(8,128)(2,1)} fusion(f32[512,9,512]{0,2,1:T(8,128)} %bitcast.69, bf16[1,512,9,512]{1,3,2,0:T(8,128)(2,1)} %copy.25, f32[512,512]{0,1:T(8,128)S(1)} %copy.31), kind=kLoop, calls=%fused_computation.122 | loop fusion | flops 9437184 | bytes 19922944 | tf_op jit(solution)/shard_map/convert_element_type | solution.py:199
  388.2 14.1 %copy.32 = bf16[512,9,512]{2,1,0:T(8,128)(2,1)} copy(bf16[512,9,512]{0,2,1:T(8,128)(2,1)} %fusion.54) | data formatting | bytes 9437184 | tf_op jit(solution)/shard_map/convert_element_type | solution.py:199
  402.3 143.5 %reduce-scatter.2.cloned.1.call-done = bf16[64,9,512]{2,1,0:T(8,128)(2,1)} async-done(((bf16[512,9,512]{2,1,0:T(8,128)(2,1)}), bf16[64,9,512]{2,1,0:T(8,128)(2,1)}) %reduce-scatter.2.cloned.1.call-update) | async-done | bytes 589840 | tf_op jit(solution)/shard_map/reduce_scatter | solution.py:198
  545.8 1.6 bitcast_convert_fusion
  547.4 1.7 copy.33
  (242 shorter events, 73.8 us)
Async XLA Ops:
  6.5 96.6 %copy-start = (f32[1024,512]{1,0:T(8,128)S(1)}, f32[1024,512]{1,0:T(8,128)}, u32[]{:S(2)}) copy-start(f32[1024,512]{1,0:T(8,128)} %param.19) | copy-start | bytes 6291460
  6.5 539.2 %reduce-scatter.2.cloned.1.call-start = ((), (), s32[]{:S(2)}) async-start(), calls=%async_computation.1 | async-start | bytes 9437184 | tf_op jit(solution)/shard_map/reduce_scatter | solution.py:198
  96.3 6.7 %copy-start.6 = (f32[512]{0:T(512)S(1)}, f32[512]{0:T(512)}, u32[]{:S(2)}) copy-start(f32[512]{0:T(512)} %param.23) | copy-start | bytes 6148
  96.3 7.3 %copy-start.7 = (u32[32]{0:T(128)S(1)}, u32[32]{0:T(128)}, u32[]{:S(2)}) copy-start(u32[32]{0:T(128)} %constant.236) | copy-start | bytes 388
  103.1 4.7 copy-start.4
  108.9 2.6 collective-permute-start
  111.7 2.3 copy-start.2
  118.8 2.6 collective-permute-start
  121.5 2.3 copy-start.2
  128.6 7.0 %collective-permute-start = (bf16[512,256]{1,0:T(8,128)(2,1)S(1)}, bf16[512,256]{1,0:T(8,128)(2,1)S(1)}, u32[]{:S(2)}, u32[]{:S(2)}) collective-permute-start(bf16[512,256]{1,0:T(8,128)(2,1)S(1)} %copy.36), channel_id=1, source_target_pairs={{0,8},{8,16},{16,24},{1,9},{9,17},{17,25},{2,10},{10,18},{18,26},{... | collective-permute-start | bytes 786440 | tf_op jit(solution)/shard_map/while/body/eval_jaxpr/ppermute | solution.py:18
  135.9 2.3 copy-start.2
  143.0 5.2 collective-permute-start
  150.0 13.1 %collective-permute-start = (bf16[512,256]{1,0:T(8,128)(2,1)S(1)}, bf16[512,256]{1,0:T(8,128)(2,1)S(1)}, u32[]{:S(2)}, u32[]{:S(2)}) collective-permute-start(bf16[512,256]{1,0:T(8,128)(2,1)S(1)} %copy.36), channel_id=1, source_target_pairs={{0,8},{8,16},{16,24},{1,9},{9,17},{17,25},{2,10},{10,18},{18,26},{... | collective-permute-start | bytes 786440 | tf_op jit(solution)/shard_map/while/body/eval_jaxpr/ppermute | solution.py:18
  164.9 7.7 %collective-permute-start = (bf16[512,256]{1,0:T(8,128)(2,1)S(1)}, bf16[512,256]{1,0:T(8,128)(2,1)S(1)}, u32[]{:S(2)}, u32[]{:S(2)}) collective-permute-start(bf16[512,256]{1,0:T(8,128)(2,1)S(1)} %copy.36), channel_id=1, source_target_pairs={{0,8},{8,16},{16,24},{1,9},{9,17},{17,25},{2,10},{10,18},{18,26},{... | collective-permute-start | bytes 786440 | tf_op jit(solution)/shard_map/while/body/eval_jaxpr/ppermute | solution.py:18
  173.3 1.1 copy-start.5
  184.1 15.8 %collective-permute-start.1 = (bf16[512,256]{1,0:T(8,128)(2,1)S(1)}, bf16[512,256]{1,0:T(8,128)(2,1)S(1)}, u32[]{:S(2)}, u32[]{:S(2)}) collective-permute-start(bf16[512,256]{1,0:T(8,128)(2,1)S(1)} %copy.37), channel_id=1, source_target_pairs={{8,0},{16,8},{24,16},{9,1},{17,9},{25,17},{10,2},{18,10},{26,18},{... | collective-permute-start | bytes 786440 | tf_op jit(solution)/shard_map/while/body/eval_jaxpr/ppermute | solution.py:18
  185.4 13.1 %collective-permute-start.2 = (bf16[2]{0:T(256)(128)(2,1)S(1)}, bf16[2]{0:T(256)(128)(2,1)S(1)}, u32[]{:S(2)}, u32[]{:S(2)}) collective-permute-start(bf16[2]{0:T(256)(128)(2,1)S(1)} %broadcast_select_fusion.4), channel_id=1, source_target_pairs={{8,0},{16,8},{24,16},{9,1},{17,9},{25,17},{10,2},{18,10},{26,18},{... | collective-permute-start | bytes 20 | tf_op jit(solution)/shard_map/while/body/eval_jaxpr/ppermute | solution.py:18
  201.7 9.8 %collective-permute-start.1 = (bf16[512,256]{1,0:T(8,128)(2,1)S(1)}, bf16[512,256]{1,0:T(8,128)(2,1)S(1)}, u32[]{:S(2)}, u32[]{:S(2)}) collective-permute-start(bf16[512,256]{1,0:T(8,128)(2,1)S(1)} %copy.37), channel_id=1, source_target_pairs={{8,0},{16,8},{24,16},{9,1},{17,9},{25,17},{10,2},{18,10},{26,18},{... | collective-permute-start | bytes 786440 | tf_op jit(solution)/shard_map/while/body/eval_jaxpr/ppermute | solution.py:18
  203.0 7.2 %collective-permute-start.2 = (bf16[2]{0:T(256)(128)(2,1)S(1)}, bf16[2]{0:T(256)(128)(2,1)S(1)}, u32[]{:S(2)}, u32[]{:S(2)}) collective-permute-start(bf16[2]{0:T(256)(128)(2,1)S(1)} %broadcast_select_fusion.4), channel_id=1, source_target_pairs={{8,0},{16,8},{24,16},{9,1},{17,9},{25,17},{10,2},{18,10},{26,18},{... | collective-permute-start | bytes 20 | tf_op jit(solution)/shard_map/while/body/eval_jaxpr/ppermute | solution.py:18
  213.3 9.1 %collective-permute-start.1 = (bf16[512,256]{1,0:T(8,128)(2,1)S(1)}, bf16[512,256]{1,0:T(8,128)(2,1)S(1)}, u32[]{:S(2)}, u32[]{:S(2)}) collective-permute-start(bf16[512,256]{1,0:T(8,128)(2,1)S(1)} %copy.37), channel_id=1, source_target_pairs={{8,0},{16,8},{24,16},{9,1},{17,9},{25,17},{10,2},{18,10},{26,18},{... | collective-permute-start | bytes 786440 | tf_op jit(solution)/shard_map/while/body/eval_jaxpr/ppermute | solution.py:18
  214.7 6.5 %collective-permute-start.2 = (bf16[2]{0:T(256)(128)(2,1)S(1)}, bf16[2]{0:T(256)(128)(2,1)S(1)}, u32[]{:S(2)}, u32[]{:S(2)}) collective-permute-start(bf16[2]{0:T(256)(128)(2,1)S(1)} %broadcast_select_fusion.4), channel_id=1, source_target_pairs={{8,0},{16,8},{24,16},{9,1},{17,9},{25,17},{10,2},{18,10},{26,18},{... | collective-permute-start | bytes 20 | tf_op jit(solution)/shard_map/while/body/eval_jaxpr/ppermute | solution.py:18
  224.3 62.4 %collective-permute-start.1 = (bf16[512,256]{1,0:T(8,128)(2,1)S(1)}, bf16[512,256]{1,0:T(8,128)(2,1)S(1)}, u32[]{:S(2)}, u32[]{:S(2)}) collective-permute-start(bf16[512,256]{1,0:T(8,128)(2,1)S(1)} %copy.37), channel_id=1, source_target_pairs={{8,0},{16,8},{24,16},{9,1},{17,9},{25,17},{10,2},{18,10},{26,18},{... | collective-permute-start | bytes 786440 | tf_op jit(solution)/shard_map/while/body/eval_jaxpr/ppermute | solution.py:18
  225.6 59.8 %collective-permute-start.2 = (bf16[2]{0:T(256)(128)(2,1)S(1)}, bf16[2]{0:T(256)(128)(2,1)S(1)}, u32[]{:S(2)}, u32[]{:S(2)}) collective-permute-start(bf16[2]{0:T(256)(128)(2,1)S(1)} %broadcast_select_fusion.4), channel_id=1, source_target_pairs={{8,0},{16,8},{24,16},{9,1},{17,9},{25,17},{10,2},{18,10},{26,18},{... | collective-permute-start | bytes 20 | tf_op jit(solution)/shard_map/while/body/eval_jaxpr/ppermute | solution.py:18
  287.8 13.2 %slice-start = ((s8[4718592]{0:T(1024)(128)(4,1)}), s8[524288]{0:T(1024)(128)(4,1)S(1)}, s32[]{:S(2)}) async-start(s8[4718592]{0:T(1024)(128)(4,1)} %bitcast.66), calls=%async_computation.2 | async-start | bytes 1048576 | tf_op jit(solution)/shard_map/while/body/eval_jaxpr/cond
  288.0 1.4 copy-start.3
  291.3 9.8 %slice-start.1 = ((s8[4718592]{0:T(1024)(128)(4,1)}), s8[4194304]{0:T(1024)(128)(4,1)S(1)}, s32[]{:S(2)}) async-start(s8[4718592]{0:T(1024)(128)(4,1)} %bitcast.66), calls=%async_computation.3 | async-start | bytes 8388608 | tf_op jit(solution)/shard_map/while/body/eval_jaxpr/cond
  308.0 9.1 %collective-permute-start.1 = (bf16[512,256]{1,0:T(8,128)(2,1)S(1)}, bf16[512,256]{1,0:T(8,128)(2,1)S(1)}, u32[]{:S(2)}, u32[]{:S(2)}) collective-permute-start(bf16[512,256]{1,0:T(8,128)(2,1)S(1)} %copy.37), channel_id=1, source_target_pairs={{8,0},{16,8},{24,16},{9,1},{17,9},{25,17},{10,2},{18,10},{26,18},{... | collective-permute-start | bytes 786440 | tf_op jit(solution)/shard_map/while/body/eval_jaxpr/ppermute | solution.py:18
  309.3 6.5 %collective-permute-start.2 = (bf16[2]{0:T(256)(128)(2,1)S(1)}, bf16[2]{0:T(256)(128)(2,1)S(1)}, u32[]{:S(2)}, u32[]{:S(2)}) collective-permute-start(bf16[2]{0:T(256)(128)(2,1)S(1)} %broadcast_select_fusion.4), channel_id=1, source_target_pairs={{8,0},{16,8},{24,16},{9,1},{17,9},{25,17},{10,2},{18,10},{26,18},{... | collective-permute-start | bytes 20 | tf_op jit(solution)/shard_map/while/body/eval_jaxpr/ppermute | solution.py:18
  318.3 13.2 %slice-start = ((s8[4718592]{0:T(1024)(128)(4,1)}), s8[524288]{0:T(1024)(128)(4,1)S(1)}, s32[]{:S(2)}) async-start(s8[4718592]{0:T(1024)(128)(4,1)} %bitcast.66), calls=%async_computation.2 | async-start | bytes 1048576 | tf_op jit(solution)/shard_map/while/body/eval_jaxpr/cond
  318.5 1.4 copy-start.3
  321.7 9.8 %slice-start.1 = ((s8[4718592]{0:T(1024)(128)(4,1)}), s8[4194304]{0:T(1024)(128)(4,1)S(1)}, s32[]{:S(2)}) async-start(s8[4718592]{0:T(1024)(128)(4,1)} %bitcast.66), calls=%async_computation.3 | async-start | bytes 8388608 | tf_op jit(solution)/shard_map/while/body/eval_jaxpr/cond
  338.5 9.1 %collective-permute-start.1 = (bf16[512,256]{1,0:T(8,128)(2,1)S(1)}, bf16[512,256]{1,0:T(8,128)(2,1)S(1)}, u32[]{:S(2)}, u32[]{:S(2)}) collective-permute-start(bf16[512,256]{1,0:T(8,128)(2,1)S(1)} %copy.37), channel_id=1, source_target_pairs={{8,0},{16,8},{24,16},{9,1},{17,9},{25,17},{10,2},{18,10},{26,18},{... | collective-permute-start | bytes 786440 | tf_op jit(solution)/shard_map/while/body/eval_jaxpr/ppermute | solution.py:18
  339.8 6.5 %collective-permute-start.2 = (bf16[2]{0:T(256)(128)(2,1)S(1)}, bf16[2]{0:T(256)(128)(2,1)S(1)}, u32[]{:S(2)}, u32[]{:S(2)}) collective-permute-start(bf16[2]{0:T(256)(128)(2,1)S(1)} %broadcast_select_fusion.4), channel_id=1, source_target_pairs={{8,0},{16,8},{24,16},{9,1},{17,9},{25,17},{10,2},{18,10},{26,18},{... | collective-permute-start | bytes 20 | tf_op jit(solution)/shard_map/while/body/eval_jaxpr/ppermute | solution.py:18
  348.7 13.2 %slice-start = ((s8[4718592]{0:T(1024)(128)(4,1)}), s8[524288]{0:T(1024)(128)(4,1)S(1)}, s32[]{:S(2)}) async-start(s8[4718592]{0:T(1024)(128)(4,1)} %bitcast.66), calls=%async_computation.2 | async-start | bytes 1048576 | tf_op jit(solution)/shard_map/while/body/eval_jaxpr/cond
  348.9 1.4 copy-start.3
  352.2 9.8 %slice-start.1 = ((s8[4718592]{0:T(1024)(128)(4,1)}), s8[4194304]{0:T(1024)(128)(4,1)S(1)}, s32[]{:S(2)}) async-start(s8[4718592]{0:T(1024)(128)(4,1)} %bitcast.66), calls=%async_computation.3 | async-start | bytes 8388608 | tf_op jit(solution)/shard_map/while/body/eval_jaxpr/cond
  545.8 3.4 copy-start.1
Sparse Core Ops, SparseCore 0:
  402.4 143.3 reduce-scatter.1
where the time goes:
time: 558 us; the launch traced here: 556 us
  waiting for transfers between devices  220 us (39%)
  local copies, waits for them, and re-layouts  106 us (19%)
  blocking collectives  63.6 us (11%)
  other arithmetic  48.2 us (9%)
  starting transfers between devices  46.1 us (8%)
  matrix products  42.7 us (8%)
  loops' own time  15 us (3%)
  between operations  14.2 us (3%)
    reduce_scatter x1, waiting for transfers between devices, on_device(): lax.psum_scatter(full_grad.astype(jnp.bfloat16), 'dp', scatter_dimension=...  144 us
    ppermute x18, waiting for transfers between devices, from_behind(): return lax.ppermute(x, axis, pairs)  76.2 us
    ppermute x18, starting transfers between devices, from_behind(): return lax.ppermute(x, axis, pairs)  46.1 us
    unnamed x1, blocking collectives  35.4 us
    dot_general x3, matrix products, backward_compute(): lax.dot_general(grad_conv, spread(mod_input, side_len), (((1,), (1,)), ((...  29.3 us
    all_gather x1, blocking collectives, on_device(): whole_ids = lax.all_gather(text_ids, 'dp', axis=0, tiled=True)  28.2 us
    convert_element_type x1, local copies, waits for them, and re-layouts, on_device(): full_grad.astype(jnp.bfloat16)  14.1 us
    gather x2, local copies, waits for them, and re-layouts, on_device(): picked = jnp.take(text_table, jnp.clip(wanted, 0, vocab_rows - 1), axis=0)  12.3 us
  transfers between devices with their start and end apart: 19, of which 7 were waited for; matrix products, arithmetic and copies ran while one was open for 4% of the time, Pallas kernels for 0%

commit v1 on v0

v1 whole, which is shorter than its diff:
```python
import functools
import math

import jax
import jax.numpy as jnp
from jax import lax
from jax.experimental import pallas as pl
from jax.experimental.pallas import tpu as pltpu
from jax.sharding import PartitionSpec as P

TXT_LEN = 77
RES = 16
F32 = jnp.float32
BF16 = jnp.bfloat16
VMEM = pltpu.VMEM
LIMIT = 30 * 1024 * 1024


def params(limit=LIMIT):
    return pltpu.CompilerParams(vmem_limit_bytes=limit)


def swap(x, bit, count):
    return lax.ppermute(x, "dp", [(i, i ^ bit) for i in range(count)])


def column_masks(rows, side):
    column = lax.broadcasted_iota(jnp.int32, (rows, 1), 0) % side
    return column != 0, column != side - 1


def put_shifts(pieces, value, side, at, rows, pad):
    not_first, not_last = column_masks(rows, side)
    left = jnp.where(not_first, pltpu.roll(value, 1, 0), 0.0)
    right = jnp.where(not_last, pltpu.roll(value, rows - 1, 0), 0.0)
    for index, shifted in enumerate((left, value, right)):
        pieces[index, pl.ds(at, rows), :] = shifted.astype(BF16)


def blank_edges(pieces, rows, pad):
    blank = jnp.zeros((pad, pieces.shape[2]), BF16)
    for index in range(3):
        pieces[index, pl.ds(0, pad), :] = blank
        pieces[index, pl.ds(pad + rows, pad), :] = blank


def conv_of(pieces, spread, weight, sign, side, rows):
    channels = pieces.shape[2]
    for tap in range(9):
        down, across = sign * (tap // 3 - 1), sign * (tap % 3 - 1)
        spread[:, pl.ds(tap * channels, channels)] = pieces[
            across + 1, pl.ds(side + down * side, rows), :
        ]
    return jnp.dot(spread[...], weight[...], preferred_element_type=F32)


def forward_kernel(
    side, where, received, start, styles, demods, head, weight, kept_in, kept_conv,
    out, kept_in_out, kept_conv_out, score, pieces, spread, mod_box, conv_box, sems,
):
    rows = received.shape[0]
    position, slot, is_first = where[0], where[1], where[2]
    blank_edges(pieces, rows, side)
    style = styles[pl.ds(position, 1), :]
    source = jnp.where(is_first == 1, start[...].astype(F32), received[...].astype(F32))
    mod = (style * source).astype(BF16)
    mod_box[...] = mod
    first = pltpu.make_async_copy(mod_box, kept_in_out.at[slot], sems.at[0])
    first.start()
    put_shifts(pieces, mod.astype(F32), side, side, rows, side)
    conv = conv_of(pieces, spread, weight, 1, side, rows)
    conv_box[...] = conv
    second = pltpu.make_async_copy(conv_box, kept_conv_out.at[slot], sems.at[1])
    second.start()
    pre = demods[pl.ds(position, 1), :] * conv
    result = (pre / (1.0 + jnp.exp(-pre))).astype(BF16)
    out[...] = result
    sums = jnp.sum(result.astype(F32), axis=0, keepdims=True) * head[...]
    score[...] = jnp.broadcast_to(jnp.sum(sums, axis=1, keepdims=True), score.shape)
    first.wait()
    second.wait()


def backward_kernel(
    side, where, received, unit, styles, demods, scales, boosts, kept_conv, weight, kept_grad, kept_term,
    out, kept_grad_out, kept_term_out, pieces, spread, conv_box, grad_box, term_box, sems,
):
    rows = received.shape[0]
    position, slot, is_last = where[0], where[1], where[2]
    load = pltpu.make_async_copy(kept_conv.at[position], conv_box, sems.at[0])
    load.start()
    blank_edges(pieces, rows, side)
    demod = demods[pl.ds(position, 1), :]
    incoming = jnp.where(is_last == 1, jnp.broadcast_to(unit[...], received.shape), received[...].astype(F32))
    load.wait()
    conv = conv_box[...]
    pre = demod * conv
    sigma = 1.0 / (1.0 + jnp.exp(-pre))
    grad_pre = incoming * sigma * (1.0 + pre * (1.0 - sigma))
    grad_conv = demod * grad_pre
    grad_box[...] = (scales[pl.ds(position, 1), :] * grad_conv).astype(BF16)
    first = pltpu.make_async_copy(grad_box, kept_grad_out.at[slot], sems.at[1])
    first.start()
    term = jnp.sum(grad_pre * conv, axis=0, keepdims=True) * demod * demod * demod
    term_box[...] = jnp.broadcast_to(term, term_box.shape)
    second = pltpu.make_async_copy(term_box, kept_term_out.at[slot], sems.at[2])
    second.start()
    put_shifts(pieces, grad_conv.astype(BF16).astype(F32), side, side, rows, side)
    back = conv_of(pieces, spread, weight, -1, side, rows)
    out[...] = (styles[pl.ds(position, 1), :] * boosts[pl.ds(position, 1), :] * back).astype(BF16)
    first.wait()
    second.wait()


def weight_grad_kernel(
    side, micro, count, orders, taps, where, kept_grad, kept_in, squares, terms, weight, *rest
):
    outs, (pieces, grad_rows, by_out, mixture, mod_f) = rest[:-5], rest[-5:]
    channels = kept_in.shape[2]
    pixels = kept_in.shape[1]
    part = channels // count
    band = micro * side
    here = where[0]
    blank = jnp.zeros((band, channels), BF16)
    for index in range(3):
        pieces[index, pl.ds(0, band), :] = blank
        pieces[index, pl.ds(band + micro * pixels, band), :] = blank
    for sample in range(micro):
        for line in range(side):
            at = line * band + sample * side
            grad_rows[pl.ds(at, side), :] = kept_grad[sample, pl.ds(line * side, side), :]
            mod_f[pl.ds(at, side), :] = kept_in[sample, pl.ds(line * side, side), :]
    put_shifts(pieces, mod_f[...].astype(F32), side, band, micro * pixels, band)
    turned = jnp.transpose(grad_rows[...].astype(F32)).astype(BF16)
    mixture[...] = lax.dot_general(
        terms[...], squares[...], (((0,), (0,)), ((), ())),
        preferred_element_type=F32, precision=lax.Precision.HIGHEST,
    )
    by_out[len(orders)] = turned
    for kind, order in enumerate(orders):
        for slot in range(count):
            flip = 0
            for stage, bit in enumerate(order):
                flip |= ((slot >> (len(order) - 1 - stage)) & 1) << bit
            source = pl.multiple_of((here ^ flip) * part, part)
            by_out[kind, pl.ds(slot * part, part), :] = by_out[len(orders), pl.ds(source, part), :]
    for chunk, (kind, tap_list) in enumerate(taps):
        keep, send = outs[2 * chunk], outs[2 * chunk + 1]
        order = orders[kind]
        for spot, tap in enumerate(tap_list):
            total = jnp.dot(
                by_out[kind], pieces[tap % 3, pl.ds((tap // 3) * band, micro * pixels), :],
                preferred_element_type=F32,
            )
            for slot in range(count):
                flip = 0
                for stage, bit in enumerate(order):
                    flip |= ((slot >> (len(order) - 1 - stage)) & 1) << bit
                source = pl.multiple_of((here ^ flip) * part, part)
                fixed = total[slot * part : (slot + 1) * part] - weight[
                    tap, pl.ds(source, part), :
                ].astype(F32) * mixture[pl.ds(source, part), :]
                target = keep if slot < count // 2 else send
                target[slot % (count // 2), spot] = fixed.astype(BF16)


def on_device(
    text_ids, seed_ids, text_table, latent_table, start_map, style_weight, conv_weight, score_head
):
    sections = lax.axis_size("section")
    count = lax.axis_size("dp")
    bits = count.bit_length() - 1
    gen_count = sections - sections // 4
    section_at = lax.axis_index("section")
    here = lax.axis_index("dp")
    is_gen = section_at < gen_count
    micro = seed_ids.shape[0]
    channels, pixels = start_map.shape
    side = RES
    vocab_rows = text_table.shape[0]
    norm_div = pixels * math.sqrt(channels)

    ids = text_ids[None]
    for stage in range(bits):
        ids = jnp.concatenate([ids, swap(ids, 1 << stage, count)], axis=0)
    wanted = ids.reshape(count * micro, TXT_LEN) - here * vocab_rows
    rows = lax.broadcasted_iota(jnp.int32, (1, 1, vocab_rows), 2)
    hits = jnp.sum((wanted[:, :, None] == rows).astype(F32), axis=1)
    sums = jnp.dot(hits.astype(BF16), text_table, preferred_element_type=F32)
    sums = sums.reshape(count, micro, channels)
    for stage in reversed(range(bits)):
        half = 1 << stage
        sums = sums[:half] + swap(sums[half:], half, count)
    text_mean = sums[0] / TXT_LEN

    weight = conv_weight[0]
    weight_out = jnp.transpose(weight, (1, 0, 2))
    weight_in = jnp.transpose(weight, (1, 2, 0)).reshape(9 * channels, channels)
    squares = jnp.sum(jnp.square(weight_out.astype(F32)), axis=0)

    latent = jnp.take(latent_table, seed_ids, axis=0) + text_mean
    code_now = jnp.where(is_gen, latent, text_mean).astype(BF16)
    styles = 1.0 + lax.dot_general(
        code_now, style_weight[0], (((1,), (1,)), ((), ())), preferred_element_type=F32
    )
    demods = lax.rsqrt(
        lax.dot_general(
            styles * styles, squares, (((1,), (1,)), ((), ())), precision=lax.Precision.HIGHEST
        )
        + 1e-08
    )
    demods = jnp.where(is_gen, demods, jnp.ones_like(demods))
    first_map = start_map.T
    head = score_head[None]
    ticks = micro + sections - 1

    whole = pl.BlockSpec(memory_space=VMEM)
    anywhere = pl.BlockSpec(memory_space=pl.ANY)
    smem = pl.BlockSpec(memory_space=pltpu.SMEM)
    flops = 2 * 9 * channels * channels * pixels
    conv_cost = pl.CostEstimate(
        flops=flops, bytes_accessed=9 * channels * channels * 2 + 5 * channels * pixels * 2,
        transcendentals=channels * pixels,
    )
    tall = 2 * side + pixels
    conv_scratch = [VMEM((3, tall, channels), BF16), VMEM((pixels, 9 * channels), BF16)]
    forward = pl.pallas_call(
        functools.partial(forward_kernel, side),
        in_specs=[smem] + [whole] * 6 + [anywhere] * 2,
        out_specs=[whole, anywhere, anywhere, whole],
        out_shape=[
            jax.ShapeDtypeStruct((pixels, channels), BF16),
            jax.ShapeDtypeStruct((micro + 1, pixels, channels), BF16),
            jax.ShapeDtypeStruct((micro + 1, pixels, channels), F32),
            jax.ShapeDtypeStruct((8, 128), F32),
        ],
        scratch_shapes=conv_scratch
        + [
            VMEM((pixels, channels), BF16),
            VMEM((pixels, channels), F32),
            pltpu.SemaphoreType.DMA((2,)),
        ],
        input_output_aliases={7: 1, 8: 2},
        cost_estimate=conv_cost,
        compiler_params=params(),
        name="forward_conv",
    )
    backward = pl.pallas_call(
        functools.partial(backward_kernel, side),
        in_specs=[smem] + [whole] * 6 + [anywhere, whole, anywhere, anywhere],
        out_specs=[whole, anywhere, anywhere],
        out_shape=[
            jax.ShapeDtypeStruct((pixels, channels), BF16),
            jax.ShapeDtypeStruct((micro + 1, pixels, channels), BF16),
            jax.ShapeDtypeStruct((micro + 1, 8, channels), F32),
        ],
        scratch_shapes=conv_scratch
        + [
            VMEM((pixels, channels), F32),
            VMEM((pixels, channels), BF16),
            VMEM((8, channels), F32),
            pltpu.SemaphoreType.DMA((3,)),
        ],
        input_output_aliases={9: 1, 10: 2},
        cost_estimate=conv_cost,
        compiler_params=params(),
        name="backward_conv",
    )

    kept_in = jnp.zeros((micro + 1, pixels, channels), BF16)
    kept_conv = jnp.zeros((micro + 1, pixels, channels), F32)
    outgoing = first_map
    scores = []
    for tick in range(ticks):
        received = (
            lax.ppermute(outgoing, "section", [(i, i + 1) for i in range(sections - 1) if 0 <= tick - 1 - i < micro])
            if tick
            else first_map
        )
        position = tick - section_at
        active = (position >= 0) & (position < micro)
        position = jnp.clip(position, 0, micro - 1)
        where = jnp.stack(
            [position, jnp.where(active, position, micro), (section_at == 0).astype(jnp.int32)]
        ).astype(jnp.int32)
        outgoing, kept_in, kept_conv, score = forward(
            where, received, first_map, styles, demods, head, weight_in, kept_in, kept_conv
        )
        scores.append(score[0, 0])
    scores = jnp.stack(scores[sections - 1 :])[:, None] / norm_div
    for hop in range(sections - gen_count - 1):
        target = sections - 2 - hop
        passed = lax.ppermute(scores, "section", [(target + 1, target)])
        scores = jnp.where(section_at == target, passed, scores)
    d_factor = jax.nn.sigmoid(scores).astype(BF16).astype(F32)
    g_factor = (-jax.nn.sigmoid(-scores)).astype(BF16).astype(F32)
    ones = jnp.ones((micro, channels), F32)
    scales = jnp.where(is_gen, ones, d_factor * ones)
    boosts = jnp.where(section_at == gen_count, g_factor * ones, ones)
    unit = (head / norm_div).astype(BF16).astype(F32)

    kept_grad = jnp.zeros((micro + 1, pixels, channels), BF16)
    kept_term = jnp.zeros((micro + 1, 8, channels), F32)
    outgoing = None
    for tick in range(ticks):
        received = (
            lax.ppermute(
                outgoing, "section",
                [(i, i - 1) for i in range(1, sections) if 0 <= tick - 1 - (sections - 1 - i) < micro],
            )
            if tick
            else first_map
        )
        position = tick - (sections - 1 - section_at)
        active = (position >= 0) & (position < micro)
        position = jnp.clip(position, 0, micro - 1)
        where = jnp.stack(
            [position, jnp.where(active, position, micro), (section_at == sections - 1).astype(jnp.int32)]
        ).astype(jnp.int32)
        outgoing, kept_grad, kept_term = backward(
            where, received, unit, styles, demods, scales, boosts, kept_conv,
            weight_out.reshape(9 * channels, channels), kept_grad, kept_term,
        )

    terms = jnp.where(is_gen, kept_term[:micro, 0, :], 0.0)
    pad = (-micro) % 8
    terms = jnp.pad(terms, ((0, pad), (0, 0)))
    style_squares = jnp.pad(styles * styles, ((0, pad), (0, 0)))
    part = channels // count
    orders = (tuple(range(bits)), (1, 0) + tuple(range(2, bits)))
    taps = ((0, (0, 1, 2)), (0, (3, 4)), (1, (7, 8)), (0, (5, 6)))
    shapes = []
    for kind, tap_list in taps:
        shapes += [jax.ShapeDtypeStruct((count // 2, len(tap_list), part, channels), BF16)] * 2
    tall = micro * (2 * side + pixels)
    pairs = pl.pallas_call(
        functools.partial(weight_grad_kernel, side, micro, count, orders, taps),
        in_specs=[smem] + [whole] * 5,
        out_specs=[whole] * len(shapes),
        out_shape=shapes,
        scratch_shapes=[
            VMEM((3, tall, channels), BF16),
            VMEM((micro * pixels, channels), BF16),
            VMEM((len(orders) + 1, channels, micro * pixels), BF16),
            VMEM((channels, channels), F32),
            VMEM((micro * pixels, channels), BF16),
        ],
        cost_estimate=pl.CostEstimate(flops=micro * flops, bytes_accessed=20 * 1024 * 1024, transcendentals=0),
        compiler_params=params(48 * 1024 * 1024),
        name="weight_grad",
    )(here[None].astype(jnp.int32), kept_grad, kept_in, style_squares, terms, weight_out)
    done = [None] * 9
    for chunk, (kind, tap_list) in enumerate(taps):
        keep, send = pairs[2 * chunk], pairs[2 * chunk + 1]
        for stage in range(bits):
            got = swap(send, 1 << orders[kind][stage], count)
            total = keep.astype(F32) + got.astype(F32)
            half = total.shape[0] // 2
            if half:
                keep = total[:half]
                send = total[half:].astype(BF16)
        for spot, tap in enumerate(tap_list):
            done[tap] = total[0, spot]
    return jnp.stack(done, axis=1)[None]


def solution(mesh):
    placed = (
        P("dp", None),
        P("dp"),
        P("dp", None),
        P(),
        P(),
        P("section", None, None),
        P("section", None, None, None),
        P(),
    )
    return jax.shard_map(
        on_device,
        mesh=mesh,
        in_specs=placed,
        out_specs=P("section", "dp", None, None),
        check_vma=False,
    )
```

time: 558 us -> 275 us (0.49)
  waiting for transfers between devices: 220 us -> 110 us
  blocking collectives: 63.6 us -> 0 us
  local copies, waits for them, and re-layouts: 106 us -> 56.9 us
  Pallas kernels: 0 us -> 45.9 us
  matrix products: 42.7 us -> 4.15 us
  other arithmetic: 48.2 us -> 9.72 us
  loops' own time: 15 us -> 0 us
  between operations: 14.2 us -> 0.73 us
    reduce_scatter x1 -> x0, waiting for transfers between devices: 144 us -> none  [on_device(): lax.psum_scatter(full_grad.astype(jnp.bfloat16), 'dp', scatter_dimension=...]
    pallas_call x0 -> x13, Pallas kernels: none -> 45.9 us  [the longest x6 19.4 us: on_device(): forward(where, received, first_map, styles, demods, head, weight_in, kept...]
    dot_general x10 -> x2, matrix products: 41.5 us -> 2.73 us  [the longest x1 1.72 us: on_device(): sums = jnp.dot(hits.astype(BF16), text_table, preferred_element_type=F32)]
    unnamed x15 -> x75, local copies, waits for them, and re-layouts: 10.3 us -> 47 us
    unnamed x1 -> x0, blocking collectives: 35.4 us -> none
    ppermute x18 -> x28, waiting for transfers between devices: 76.2 us -> 110 us  [the longest x18 71.4 us: swap(): return lax.ppermute(x, 'dp', [(i, i ^ bit) for i in range(count)])]
    all_gather x1 -> x0, blocking collectives: 28.2 us -> none  [on_device(): whole_ids = lax.all_gather(text_ids, 'dp', axis=0, tiled=True)]
    while x9 -> x0, local copies, waits for them, and re-layouts: 24.3 us -> none  [the longest x2 11.1 us: on_device(): back_done = lax.scan(backward_step, back_state, jnp.arange(ticks))[0]]
  transfers between devices with their start and end apart: 19 -> 28, of which waited for: 7 -> 18; matrix products, arithmetic and copies ran while one was open for 4% -> 6% of each run, Pallas kernels for 0% -> 0%
where the time goes in v1:
time: 275 us; the launch traced here: 273 us
  waiting for transfers between devices  110 us (40%)
  local copies, waits for them, and re-layouts  56.9 us (21%)
  starting transfers between devices  46.1 us (17%)
  Pallas kernels  45.9 us (17%)
  other arithmetic  9.72 us (4%)
  matrix products  4.15 us (2%)
    ppermute x18, waiting for transfers between devices, swap(): return lax.ppermute(x, 'dp', [(i, i ^ bit) for i in range(count)])  71.4 us
    unnamed x75, local copies, waits for them, and re-layouts  47 us
    ppermute x5, waiting for transfers between devices, on_device(): lax.ppermute(outgoing, 'section', [(i, i - 1) for i in range(1, sections)...  36.4 us
    ppermute x18, starting transfers between devices, swap(): return lax.ppermute(x, 'dp', [(i, i ^ bit) for i in range(count)])  28.7 us
    pallas_call x6, Pallas kernels, on_device(): forward(where, received, first_map, styles, demods, head, weight_in, kept...  19.4 us
    pallas_call x6, Pallas kernels, on_device(): backward(where, received, unit, styles, demods, scales, boosts, kept_conv...  19 us
    ppermute x5, starting transfers between devices, on_device(): lax.ppermute(outgoing, 'section', [(i, i + 1) for i in range(sections - 1...  11.9 us
    pallas_call x1, Pallas kernels, on_device(): pl.pallas_call(functools.partial(weight_grad_kernel, side, micro, count,...  7.5 us
  transfers between devices with their start and end apart: 28, of which 18 were waited for; matrix products, arithmetic and copies ran while one was open for 6% of the time, Pallas kernels for 0%

profile of v1, /device:TPU:0, one launch (start us, length us, event | category | flops | bytes accessed | tf_op | source)
XLA Modules:
  0.0 273.4 jit_solution(12883972840263037194)
XLA Ops:
  0.0 3.0 %collective-permute-start = (s32[1,3,77]{2,1,0:T(4,128)}, s32[1,3,77]{2,1,0:T(4,128)S(1)}, u32[]{:S(2)}, u32[]{:S(2)}) collective-permute-start(s32[1,3,77]{2,1,0:T(4,128)} %bitcast.140), channel_id=1, source_target_pairs={{0,1},{1,0},{2,3},{3,2},{4,5},{5,4},{6,7},{7,6},{8,9},{9,8},{10,11... | collective-permute-start | bytes 2780 | tf_op jit(solution)/shard_map/ppermute | solution.py:24
  3.0 1.8 collective-permute-done
  5.5 2.1 collective-permute-start.1
  7.5 3.4 %multiply_reduce_fusion = f32[512,512]{1,0:T(8,128)S(1)} fusion(bf16[1,512,9,512]{3,1,2,0:T(8,128)(2,1)} %param.14), kind=kLoop, calls=%fused_computation.3 | loop fusion | flops 6815744 | bytes 5767168 | tf_op jit(solution)/shard_map/reduce_sum | solution.py:199
  11.0 2.7 collective-permute-start.2
  13.6 2.0 collective-permute-done.2
  15.7 1.6 convert_reduce_fusion
  17.3 1.7 fusion.28
  19.1 2.7 collective-permute-start.3
  21.8 2.2 collective-permute-done.3
  24.3 3.5 %collective-permute-done.4 = f32[2,3,512]{2,1,0:T(4,128)S(1)} collective-permute-done((f32[2,3,512]{2,1,0:T(4,128)S(1)}, f32[2,3,512]{2,1,0:T(4,128)S(1)}, u32[]{:S(2)}, u32[]{:S(2)}) %collective-permute-start.4) | collective-permute-done | bytes 12320 | tf_op jit(solution)/shard_map/ppermute | solution.py:24
  27.8 1.8 collective-permute-start.5
  30.8 6.6 %copy.40 = bf16[9,512,512]{2,1,0:T(8,128)(2,1)} copy(bf16[9,512,512]{1,2,0:T(8,128)(2,1)} %bitcast.104) | data formatting | bytes 9437184 | tf_op jit(solution)/shard_map/transpose | solution.py:198
  41.2 3.1 %forward_conv.6 = (bf16[256,512]{1,0:T(8,128)(2,1)}, bf16[4,256,512]{2,1,0:T(8,128)(2,1)S(1)}, f32[4,256,512]{2,1,0:T(8,128)S(1)}, f32[8,128]{1,0:T(8,128)}) custom-call(s32[3]{0:T(128)S(1)} %add_add_fusion.9.where, bf16[256,512]{1,0:T(8,128)(2,1)S(1)} %bitcast.120, bf16[256,512]{1,0:T(8,128)(2,1)S(1)} %bitcast.121, ...), custom_call_target="tpu_custom_call", output_to_operand_aliasing={{1}: (7, {}), {2}: (8, {})} | custom-call | flops 1207959552 | bytes 6029312 | tf_op jit(solution)/shard_map/forward_conv/pallas_call | solution.py:286
  45.6 2.0 collective-permute-start.6
  48.3 1.6 copy-done.2
  49.9 2.3 copy-done.22
  52.3 3.5 %forward_conv.7 = (bf16[256,512]{1,0:T(8,128)(2,1)}, bf16[4,256,512]{2,1,0:T(8,128)(2,1)S(1)}, f32[4,256,512]{2,1,0:T(8,128)S(1)}, f32[8,128]{1,0:T(8,128)}) custom-call(s32[3]{0:T(128)S(1)} %add_add_fusion.8.where, bf16[256,512]{1,0:T(8,128)(2,1)} %collective-permute-done.6.received, ...), custom_call_target="tpu_custom_call", output_to_operand_aliasing={{1}: (7, {}), {2}: (8, {})} | custom-call | flops 1207959552 | bytes 6029312 | tf_op jit(solution)/shard_map/forward_conv/pallas_call | solution.py:286
  57.1 3.0 %collective-permute-start.7 = (bf16[256,512]{1,0:T(8,128)(2,1)}, bf16[256,512]{1,0:T(8,128)(2,1)}, u32[]{:S(2)}, u32[]{:S(2)}) collective-permute-start(bf16[256,512]{1,0:T(8,128)(2,1)} %get-tuple-element.53), channel_id=1, source_target_pairs={{0,8},{8,16},{1,9},{9,17},{2,10},{10,18},{3,11},{11,19},{4,12},{12... | collective-permute-start | bytes 786440 | tf_op jit(solution)/shard_map/ppermute | solution.py:276
  60.9 1.6 copy-done.4
  62.5 2.3 copy-done.23
  64.8 3.5 %forward_conv.8 = (bf16[256,512]{1,0:T(8,128)(2,1)}, bf16[4,256,512]{2,1,0:T(8,128)(2,1)S(1)}, f32[4,256,512]{2,1,0:T(8,128)S(1)}, f32[8,128]{1,0:T(8,128)}) custom-call(s32[3]{0:T(128)S(1)} %add_add_fusion.7.where, bf16[256,512]{1,0:T(8,128)(2,1)} %collective-permute-done.7.received, ...), custom_call_target="tpu_custom_call", output_to_operand_aliasing={{1}: (7, {}), {2}: (8, {})} | custom-call | flops 1207959552 | bytes 6029312 | tf_op jit(solution)/shard_map/forward_conv/pallas_call | solution.py:286
  69.6 4.7 %collective-permute-start.8 = (bf16[256,512]{1,0:T(8,128)(2,1)}, bf16[256,512]{1,0:T(8,128)(2,1)}, u32[]{:S(2)}, u32[]{:S(2)}) collective-permute-start(bf16[256,512]{1,0:T(8,128)(2,1)} %get-tuple-element.56), channel_id=1, source_target_pairs={{0,8},{8,16},{16,24},{1,9},{9,17},{17,25},{2,10},{10,18},{18,26},{... | collective-permute-start | bytes 786440 | tf_op jit(solution)/shard_map/ppermute | solution.py:276
  76.7 2.3 copy-done.24
  79.1 3.5 %forward_conv.9 = (bf16[256,512]{1,0:T(8,128)(2,1)}, bf16[4,256,512]{2,1,0:T(8,128)(2,1)S(1)}, f32[4,256,512]{2,1,0:T(8,128)S(1)}, f32[8,128]{1,0:T(8,128)S(1)}) custom-call(s32[3]{0:T(128)S(1)} %add_add_fusion.6.where, bf16[256,512]{1,0:T(8,128)(2,1)} %collective-permute-done.8.received, ...), custom_call_target="tpu_custom_call", output_to_operand_aliasing={{1}: (7, {}), {2}: (8, {})} | custom-call | flops 1207959552 | bytes 6029312 | tf_op jit(solution)/shard_map/forward_conv/pallas_call | solution.py:286
  85.4 1.6 copy-done.8
  87.0 2.3 copy-done.25
  89.3 2.8 %forward_conv.10 = (bf16[256,512]{1,0:T(8,128)(2,1)S(1)}, bf16[4,256,512]{2,1,0:T(8,128)(2,1)S(1)}, f32[4,256,512]{2,1,0:T(8,128)S(1)}, f32[8,128]{1,0:T(8,128)S(1)}) custom-call(s32[3]{0:T(128)S(1)} %add_add_fusion.10.where, bf16[256,512]{1,0:T(8,128)(2,1)} %collective-permute-done.9.received, ...), custom_call_target="tpu_custom_call", output_to_operand_aliasing={{1}: (7, {}), {2}: (8, {})} | custom-call | flops 1207959552 | bytes 6029312 | tf_op jit(solution)/shard_map/forward_conv/pallas_call | solution.py:286
  94.2 3.1 %forward_conv.11 = (bf16[256,512]{1,0:T(8,128)(2,1)}, bf16[4,256,512]{2,1,0:T(8,128)(2,1)S(1)}, f32[4,256,512]{2,1,0:T(8,128)S(1)}, f32[8,128]{1,0:T(8,128)S(1)}) custom-call(s32[3]{0:T(128)S(1)} %add_add_fusion.11.where, bf16[256,512]{1,0:T(8,128)(2,1)S(1)} %collective-permute-done.10.received, ...), custom_call_target="tpu_custom_call", output_to_operand_aliasing={{1}: (7, {}), {2}: (8, {})} | custom-call | flops 1207959552 | bytes 6029312 | tf_op jit(solution)/shard_map/forward_conv/pallas_call | solution.py:286
  100.1 1.9 broadcast_select_fusion
  103.9 3.1 %backward_conv.6 = (bf16[256,512]{1,0:T(8,128)(2,1)}, bf16[4,256,512]{2,1,0:T(8,128)(2,1)S(1)}, f32[4,8,512]{2,1,0:T(8,128)S(1)}) custom-call(s32[3]{0:T(128)S(1)} %add_add_fusion.5.where, bf16[256,512]{1,0:T(8,128)(2,1)S(1)} %bitcast.127, f32[1,512]{1,0:T(1,128)S(1)} %bitcast.134, ...), custom_call_target="tpu_custom_call", output_to_operand_aliasing={{1}: (9, {}), {2}: (10, {})} | custom-call | flops 1207959552 | bytes 6029312 | tf_op jit(solution)/shard_map/backward_conv/pallas_call | solution.py:320
  107.8 1.6 copy-done.11
  109.4 2.3 copy-done.16
  111.7 3.2 %backward_conv.7 = (bf16[256,512]{1,0:T(8,128)(2,1)}, bf16[4,256,512]{2,1,0:T(8,128)(2,1)S(1)}, f32[4,8,512]{2,1,0:T(8,128)S(1)}) custom-call(s32[3]{0:T(128)S(1)} %add_add_fusion.4.where, bf16[256,512]{1,0:T(8,128)(2,1)S(1)} %collective-permute-done.11.received, f32[1,512]{1,0:T(1,128)S(1)} %bitcast.135, ...), custom_call_target="tpu_custom_call", output_to_operand_aliasing={{1}: (9, {}), {2}: (10, {})} | custom-call | flops 1207959552 | bytes 6029312 | tf_op jit(solution)/shard_map/backward_conv/pallas_call | solution.py:320
  115.7 1.6 copy-done.12
  117.3 2.3 copy-done.17
  119.6 3.2 %backward_conv.8 = (bf16[256,512]{1,0:T(8,128)(2,1)}, bf16[4,256,512]{2,1,0:T(8,128)(2,1)S(1)}, f32[4,8,512]{2,1,0:T(8,128)S(1)}) custom-call(s32[3]{0:T(128)S(1)} %add_add_fusion.3.where, bf16[256,512]{1,0:T(8,128)(2,1)S(1)} %collective-permute-done.12.received, f32[1,512]{1,0:T(1,128)S(1)} %bitcast.136, ...), custom_call_target="tpu_custom_call", output_to_operand_aliasing={{1}: (9, {}), {2}: (10, {})} | custom-call | flops 1207959552 | bytes 6029312 | tf_op jit(solution)/shard_map/backward_conv/pallas_call | solution.py:320
  124.2 24.2 %collective-permute-done.13.received = bf16[256,512]{1,0:T(8,128)(2,1)S(1)} collective-permute-done((bf16[256,512]{1,0:T(8,128)(2,1)}, bf16[256,512]{1,0:T(8,128)(2,1)S(1)}, u32[]{:S(2)}, u32[]{:S(2)}) %collective-permute-start.13) | collective-permute-done | bytes 262176 | tf_op jit(solution)/shard_map/ppermute | solution.py:307
  148.4 1.6 copy-done.13
  150.0 2.3 copy-done.18
  152.3 3.2 %backward_conv.9 = (bf16[256,512]{1,0:T(8,128)(2,1)}, bf16[4,256,512]{2,1,0:T(8,128)(2,1)S(1)}, f32[4,8,512]{2,1,0:T(8,128)S(1)}) custom-call(s32[3]{0:T(128)S(1)} %add_add_fusion.2.where, bf16[256,512]{1,0:T(8,128)(2,1)S(1)} %collective-permute-done.13.received, f32[1,512]{1,0:T(1,128)S(1)} %bitcast.137, ...), custom_call_target="tpu_custom_call", output_to_operand_aliasing={{1}: (9, {}), {2}: (10, {})} | custom-call | flops 1207959552 | bytes 6029312 | tf_op jit(solution)/shard_map/backward_conv/pallas_call | solution.py:320
  156.9 6.5 %collective-permute-done.14.received = bf16[256,512]{1,0:T(8,128)(2,1)S(1)} collective-permute-done((bf16[256,512]{1,0:T(8,128)(2,1)}, bf16[256,512]{1,0:T(8,128)(2,1)S(1)}, u32[]{:S(2)}, u32[]{:S(2)}) %collective-permute-start.14) | collective-permute-done | bytes 262176 | tf_op jit(solution)/shard_map/ppermute | solution.py:307
  163.4 1.6 copy-done.14
  165.0 2.3 copy-done.19
  167.3 3.2 %backward_conv.10 = (bf16[256,512]{1,0:T(8,128)(2,1)}, bf16[4,256,512]{2,1,0:T(8,128)(2,1)S(1)}, f32[4,8,512]{2,1,0:T(8,128)S(1)}) custom-call(s32[3]{0:T(128)S(1)} %add_add_fusion.1.where, bf16[256,512]{1,0:T(8,128)(2,1)S(1)} %collective-permute-done.14.received, f32[1,512]{1,0:T(1,128)S(1)} %bitcast.138, ...), custom_call_target="tpu_custom_call", output_to_operand_aliasing={{1}: (9, {}), {2}: (10, {})} | custom-call | flops 1207959552 | bytes 6029312 | tf_op jit(solution)/shard_map/backward_conv/pallas_call | solution.py:320
  172.1 5.7 %collective-permute-done.15.received = bf16[256,512]{1,0:T(8,128)(2,1)S(1)} collective-permute-done((bf16[256,512]{1,0:T(8,128)(2,1)}, bf16[256,512]{1,0:T(8,128)(2,1)S(1)}, u32[]{:S(2)}, u32[]{:S(2)}) %collective-permute-start.15) | collective-permute-done | bytes 262176 | tf_op jit(solution)/shard_map/ppermute | solution.py:307
  177.8 1.6 copy-done.15
  179.4 2.3 copy-done.20
  181.7 3.2 %backward_conv.11 = (bf16[256,512]{1,0:T(8,128)(2,1)}, bf16[4,256,512]{2,1,0:T(8,128)(2,1)S(1)}, f32[4,8,512]{2,1,0:T(8,128)S(1)}) custom-call(s32[3]{0:T(128)S(1)} %add_add_fusion.where, bf16[256,512]{1,0:T(8,128)(2,1)S(1)} %collective-permute-done.15.received, f32[1,512]{1,0:T(1,128)S(1)} %bitcast.139, ...), custom_call_target="tpu_custom_call", output_to_operand_aliasing={{1}: (9, {}), {2}: (10, {})} | custom-call | flops 1207959552 | bytes 6029312 | tf_op jit(solution)/shard_map/backward_conv/pallas_call | solution.py:320
  185.0 7.5 %weight_grad.1 = (bf16[4,3,64,512]{3,2,1,0:T(8,128)(2,1)S(1)}, bf16[4,3,64,512]{3,2,1,0:T(8,128)(2,1)S(1)}, bf16[4,2,64,512]{3,2,1,0:T(8,128)(2,1)S(1)}, bf16[4,...) custom-call(s32[1]{0:T(128)} %bitcast.where, ...), custom_call_target="tpu_custom_call" | custom-call | flops 3623878656 | bytes 20971520 | tf_op jit(solution)/shard_map/weight_grad/pallas_call | solution.py:336
  193.2 1.6 collective-permute-start.19
  195.2 11.3 %collective-permute-done.25 = bf16[4,2,64,512]{3,2,1,0:T(8,128)(2,1)S(1)} collective-permute-done((bf16[4,2,64,512]{3,2,1,0:T(8,128)(2,1)S(1)}, bf16[4,2,64,512]{3,2,1,0:T(8,128)(2,1)S(1)}, u32[]{:S(2)}, u32[]{:S(2)}) %collective-permute-start.25) | collective-permute-done | bytes 524320 | tf_op jit(solution)/shard_map/ppermute | solution.py:24
  207.8 1.9 collective-permute-start.23
  209.6 9.2 %collective-permute-done.19 = bf16[4,2,64,512]{3,2,1,0:T(8,128)(2,1)S(1)} collective-permute-done((bf16[4,2,64,512]{3,2,1,0:T(8,128)(2,1)S(1)}, bf16[4,2,64,512]{3,2,1,0:T(8,128)(2,1)S(1)}, u32[]{:S(2)}, u32[]{:S(2)}) %collective-permute-start.19) | collective-permute-done | bytes 524320 | tf_op jit(solution)/shard_map/ppermute | solution.py:24
  219.0 1.9 collective-permute-start.20
  220.9 19.4 %collective-permute-done.26 = bf16[2,2,64,512]{3,2,1,0:T(8,128)(2,1)S(1)} collective-permute-done((bf16[2,2,64,512]{3,2,1,0:T(8,128)(2,1)S(1)}, bf16[2,2,64,512]{3,2,1,0:T(8,128)(2,1)S(1)}, u32[]{:S(2)}, u32[]{:S(2)}) %collective-permute-start.26) | collective-permute-done | bytes 262176 | tf_op jit(solution)/shard_map/ppermute | solution.py:24
  240.4 2.5 collective-permute-start.27
  243.7 2.5 collective-permute-start.21
  246.5 1.6 collective-permute-start.17
  248.1 7.4 %collective-permute-done.27 = bf16[1,2,64,512]{3,2,1,0:T(8,128)(2,1)S(1)} collective-permute-done((bf16[1,2,64,512]{3,2,1,0:T(8,128)(2,1)S(1)}, bf16[1,2,64,512]{3,2,1,0:T(8,128)(2,1)S(1)}, u32[]{:S(2)}, u32[]{:S(2)}) %collective-permute-start.27) | collective-permute-done | bytes 131104 | tf_op jit(solution)/shard_map/ppermute | solution.py:24
  255.5 2.8 %collective-permute-done.24 = bf16[1,2,64,512]{3,2,1,0:T(8,128)(2,1)S(1)} collective-permute-done((bf16[1,2,64,512]{3,2,1,0:T(8,128)(2,1)S(1)}, bf16[1,2,64,512]{3,2,1,0:T(8,128)(2,1)S(1)}, u32[]{:S(2)}, u32[]{:S(2)}) %collective-permute-start.24) | collective-permute-done | bytes 131104 | tf_op jit(solution)/shard_map/ppermute | solution.py:24
  258.3 4.8 %collective-permute-done.17 = bf16[2,3,64,512]{3,2,1,0:T(8,128)(2,1)S(1)} collective-permute-done((bf16[2,3,64,512]{3,2,1,0:T(8,128)(2,1)S(1)}, bf16[2,3,64,512]{3,2,1,0:T(8,128)(2,1)S(1)}, u32[]{:S(2)}, u32[]{:S(2)}) %collective-permute-start.17) | collective-permute-done | bytes 393248 | tf_op jit(solution)/shard_map/ppermute | solution.py:24
  263.4 2.2 collective-permute-start.18
  265.6 6.5 %collective-permute-done.18 = bf16[1,3,64,512]{3,2,1,0:T(8,128)(2,1)S(1)} collective-permute-done((bf16[1,3,64,512]{3,2,1,0:T(8,128)(2,1)S(1)}, bf16[1,3,64,512]{3,2,1,0:T(8,128)(2,1)S(1)}, u32[]{:S(2)}, u32[]{:S(2)}) %collective-permute-start.18) | collective-permute-done | bytes 196640 | tf_op jit(solution)/shard_map/ppermute | solution.py:24
  (152 shorter events, 34.4 us)
Async XLA Ops:
  0.0 37.5 %copy-start = (f32[1024,512]{1,0:T(8,128)S(1)}, f32[1024,512]{1,0:T(8,128)}, u32[]{:S(2)}) copy-start(f32[1024,512]{1,0:T(8,128)} %param.11) | copy-start | bytes 6291460
  0.0 4.8 %collective-permute-start = (s32[1,3,77]{2,1,0:T(4,128)}, s32[1,3,77]{2,1,0:T(4,128)S(1)}, u32[]{:S(2)}, u32[]{:S(2)}) collective-permute-start(s32[1,3,77]{2,1,0:T(4,128)} %bitcast.140), channel_id=1, source_target_pairs={{0,1},{1,0},{2,3},{3,2},{4,5},{5,4},{6,7},{7,6},{8,9},{9,8},{10,11... | collective-permute-start | bytes 2780 | tf_op jit(solution)/shard_map/ppermute | solution.py:24
  5.5 5.5 %copy-start.28 = (s32[3,77]{1,0:T(4,128)S(1)}, s32[3,77]{1,0:T(4,128)}, u32[]{:S(2)}) copy-start(s32[3,77]{1,0:T(4,128)} %param.8) | copy-start | bytes 2776
  5.5 8.2 %copy-start.30 = (s32[3]{0:T(128)S(1)}, s32[3]{0:T(128)}, u32[]{:S(2)}) copy-start(s32[3]{0:T(128)} %param.9) | copy-start | bytes 40
  5.5 5.5 %collective-permute-start.1 = (s32[2,3,77]{2,1,0:T(4,128)S(1)}, s32[2,3,77]{2,1,0:T(4,128)S(1)}, u32[]{:S(2)}, u32[]{:S(2)}) collective-permute-start(s32[2,3,77]{2,1,0:T(4,128)S(1)} %pad_add_fusion.1), channel_id=1, source_target_pairs={{0,2},{1,3},{2,0},{3,1},{4,6},{5,7},{6,4},{7,5},{8,10},{9,11},{10,... | collective-permute-start | bytes 5552 | tf_op jit(solution)/shard_map/ppermute | solution.py:24
  11.0 4.6 %collective-permute-start.2 = (s32[4,3,77]{2,1,0:T(4,128)S(1)}, s32[4,3,77]{2,1,0:T(4,128)S(1)}, u32[]{:S(2)}, u32[]{:S(2)}) collective-permute-start(s32[4,3,77]{2,1,0:T(4,128)S(1)} %pad_add_fusion), channel_id=1, source_target_pairs={{0,4},{1,5},{2,6},{3,7},{4,0},{5,1},{6,2},{7,3},{8,12},{9,13},{10,... | collective-permute-start | bytes 11096 | tf_op jit(solution)/shard_map/ppermute | solution.py:24
  19.1 4.9 %collective-permute-start.3 = (f32[4,3,512]{2,1,0:T(4,128)S(1)}, f32[4,3,512]{2,1,0:T(4,128)S(1)}, u32[]{:S(2)}, u32[]{:S(2)}) collective-permute-start(f32[4,3,512]{2,1,0:T(4,128)S(1)} %slice.122), channel_id=1, source_target_pairs={{0,4},{1,5},{2,6},{3,7},{4,0},{5,1},{6,2},{7,3},{8,12},{9,13},{10,... | collective-permute-start | bytes 73736 | tf_op jit(solution)/shard_map/ppermute | solution.py:24
  24.0 3.8 %collective-permute-start.4 = (f32[2,3,512]{2,1,0:T(4,128)S(1)}, f32[2,3,512]{2,1,0:T(4,128)S(1)}, u32[]{:S(2)}, u32[]{:S(2)}) collective-permute-start(f32[2,3,512]{2,1,0:T(4,128)S(1)} %slice.161), channel_id=1, source_target_pairs={{0,2},{1,3},{2,0},{3,1},{4,6},{5,7},{6,4},{7,5},{8,10},{9,11},{10,... | collective-permute-start | bytes 36872 | tf_op jit(solution)/shard_map/ppermute | solution.py:24
  27.8 10.2 %collective-permute-start.5 = (f32[1,3,512]{2,1,0:T(4,128)S(1)}, f32[1,3,512]{2,1,0:T(4,128)S(1)}, u32[]{:S(2)}, u32[]{:S(2)}) collective-permute-start(f32[1,3,512]{2,1,0:T(4,128)S(1)} %slice.163), channel_id=1, source_target_pairs={{0,1},{1,0},{2,3},{3,2},{4,5},{5,4},{6,7},{7,6},{8,9},{9,8},{10,11... | collective-permute-start | bytes 18440 | tf_op jit(solution)/shard_map/ppermute | solution.py:24
  38.0 2.8 %copy-start.21 = (bf16[9,512,512]{2,1,0:T(8,128)(2,1)S(1)}, bf16[9,512,512]{2,1,0:T(8,128)(2,1)}, u32[]{:S(2)}) copy-start(bf16[9,512,512]{2,1,0:T(8,128)(2,1)} %copy.40) | copy-start | bytes 14155780
  40.5 0.7 copy-start.27
  44.2 1.3 copy-start.1
  45.6 2.8 %collective-permute-start.6 = (bf16[256,512]{1,0:T(8,128)(2,1)}, bf16[256,512]{1,0:T(8,128)(2,1)}, u32[]{:S(2)}, u32[]{:S(2)}) collective-permute-start(bf16[256,512]{1,0:T(8,128)(2,1)} %get-tuple-element.50), channel_id=1, source_target_pairs={{0,8},{1,9},{2,10},{3,11},{4,12},{5,13},{6,14},{7,15}} | collective-permute-start | bytes 786440 | tf_op jit(solution)/shard_map/ppermute | solution.py:276
  48.3 1.6 copy-start.2
  49.9 2.3 copy-start.22
  55.8 1.3 copy-start.3
  57.1 3.8 %collective-permute-start.7 = (bf16[256,512]{1,0:T(8,128)(2,1)}, bf16[256,512]{1,0:T(8,128)(2,1)}, u32[]{:S(2)}, u32[]{:S(2)}) collective-permute-start(bf16[256,512]{1,0:T(8,128)(2,1)} %get-tuple-element.53), channel_id=1, source_target_pairs={{0,8},{8,16},{1,9},{9,17},{2,10},{10,18},{3,11},{11,19},{4,12},{12... | collective-permute-start | bytes 786440 | tf_op jit(solution)/shard_map/ppermute | solution.py:276
  60.9 1.6 copy-start.4
  62.5 2.3 copy-start.23
  68.3 1.3 copy-start.5
  69.6 5.5 %collective-permute-start.8 = (bf16[256,512]{1,0:T(8,128)(2,1)}, bf16[256,512]{1,0:T(8,128)(2,1)}, u32[]{:S(2)}, u32[]{:S(2)}) collective-permute-start(bf16[256,512]{1,0:T(8,128)(2,1)} %get-tuple-element.56), channel_id=1, source_target_pairs={{0,8},{8,16},{16,24},{1,9},{9,17},{17,25},{2,10},{10,18},{18,26},{... | collective-permute-start | bytes 786440 | tf_op jit(solution)/shard_map/ppermute | solution.py:276
  75.1 1.6 copy-start.6
  76.7 2.3 copy-start.24
  82.6 1.3 copy-start.7
  83.9 1.5 collective-permute-start.9
  85.4 1.6 copy-start.8
  87.0 2.3 copy-start.25
  92.1 2.0 collective-permute-start.10
  94.2 8.1 %slice-start = ((s8[4718592]{0:T(1024)(128)(4,1)}), s8[4194304]{0:T(1024)(128)(4,1)S(1)}, s32[]{:S(2)}) async-start(s8[4718592]{0:T(1024)(128)(4,1)} %bitcast.106), calls=%async_computation | async-start | bytes 8388608
  94.2 8.1 %slice-start.1 = ((s8[4718592]{0:T(1024)(128)(4,1)}), s8[524288]{0:T(1024)(128)(4,1)S(1)}, s32[]{:S(2)}) async-start(s8[4718592]{0:T(1024)(128)(4,1)} %bitcast.106), calls=%async_computation.1 | async-start | bytes 1048576
  97.2 1.3 copy-start.9
  98.6 1.0 copy-start.26
  102.3 1.6 copy-start.10
  107.0 0.8 collective-permute-start.11
  107.8 1.6 copy-start.11
  109.4 2.3 copy-start.16
  114.9 0.8 collective-permute-start.12
  115.7 1.6 copy-start.12
  117.3 2.3 copy-start.17
  122.8 25.6 %collective-permute-start.13 = (bf16[256,512]{1,0:T(8,128)(2,1)}, bf16[256,512]{1,0:T(8,128)(2,1)S(1)}, u32[]{:S(2)}, u32[]{:S(2)}) collective-permute-start(bf16[256,512]{1,0:T(8,128)(2,1)} %get-tuple-element.75), channel_id=1, source_target_pairs={{8,0},{16,8},{24,16},{9,1},{17,9},{25,17},{10,2},{18,10},{26,18},{... | collective-permute-start | bytes 786440 | tf_op jit(solution)/shard_map/ppermute | solution.py:307
  148.4 1.6 copy-start.13
  150.0 2.3 copy-start.18
  155.5 7.9 %collective-permute-start.14 = (bf16[256,512]{1,0:T(8,128)(2,1)}, bf16[256,512]{1,0:T(8,128)(2,1)S(1)}, u32[]{:S(2)}, u32[]{:S(2)}) collective-permute-start(bf16[256,512]{1,0:T(8,128)(2,1)} %get-tuple-element.78), channel_id=1, source_target_pairs={{8,0},{16,8},{9,1},{17,9},{10,2},{18,10},{11,3},{19,11},{12,4},{20... | collective-permute-start | bytes 786440 | tf_op jit(solution)/shard_map/ppermute | solution.py:307
  163.4 1.6 copy-start.14
  165.0 2.3 copy-start.19
  170.5 7.3 %collective-permute-start.15 = (bf16[256,512]{1,0:T(8,128)(2,1)}, bf16[256,512]{1,0:T(8,128)(2,1)S(1)}, u32[]{:S(2)}, u32[]{:S(2)}) collective-permute-start(bf16[256,512]{1,0:T(8,128)(2,1)} %get-tuple-element.81), channel_id=1, source_target_pairs={{8,0},{9,1},{10,2},{11,3},{12,4},{13,5},{14,6},{15,7}} | collective-permute-start | bytes 786440 | tf_op jit(solution)/shard_map/ppermute | solution.py:307
  177.8 1.6 copy-start.15
  179.4 2.3 copy-start.20
  192.5 14.0 %collective-permute-start.25 = (bf16[4,2,64,512]{3,2,1,0:T(8,128)(2,1)S(1)}, bf16[4,2,64,512]{3,2,1,0:T(8,128)(2,1)S(1)}, u32[]{:S(2)}, u32[]{:S(2)}) collective-permute-start(bf16[4,2,64,512]{3,2,1,0:T(8,128)(2,1)S(1)} %get-tuple-element.94), channel_id=1, source_target_pairs={{0,2},{1,3},{2,0},{3,1},{4,6},{5,7},{6,4},{7,5},{8,10},{9,11},{10,... | collective-permute-start | bytes 1572872 | tf_op jit(solution)/shard_map/ppermute | solution.py:24
  192.8 14.8 %collective-permute-start.22 = (bf16[4,2,64,512]{3,2,1,0:T(8,128)(2,1)S(1)}, bf16[4,2,64,512]{3,2,1,0:T(8,128)(2,1)S(1)}, u32[]{:S(2)}, u32[]{:S(2)}) collective-permute-start(bf16[4,2,64,512]{3,2,1,0:T(8,128)(2,1)S(1)} %get-tuple-element.92), channel_id=1, source_target_pairs={{0,1},{1,0},{2,3},{3,2},{4,5},{5,4},{6,7},{7,6},{8,9},{9,8},{10,11... | collective-permute-start | bytes 1572872 | tf_op jit(solution)/shard_map/ppermute | solution.py:24
  193.2 25.6 %collective-permute-start.19 = (bf16[4,2,64,512]{3,2,1,0:T(8,128)(2,1)S(1)}, bf16[4,2,64,512]{3,2,1,0:T(8,128)(2,1)S(1)}, u32[]{:S(2)}, u32[]{:S(2)}) collective-permute-start(bf16[4,2,64,512]{3,2,1,0:T(8,128)(2,1)S(1)} %get-tuple-element.90), channel_id=1, source_target_pairs={{0,1},{1,0},{2,3},{3,2},{4,5},{5,4},{6,7},{7,6},{8,9},{9,8},{10,11... | collective-permute-start | bytes 1572872 | tf_op jit(solution)/shard_map/ppermute | solution.py:24
  194.8 51.4 %collective-permute-start.16 = (bf16[4,3,64,512]{3,2,1,0:T(8,128)(2,1)S(1)}, bf16[4,3,64,512]{3,2,1,0:T(8,128)(2,1)S(1)}, u32[]{:S(2)}, u32[]{:S(2)}) collective-permute-start(bf16[4,3,64,512]{3,2,1,0:T(8,128)(2,1)S(1)} %get-tuple-element.88), channel_id=1, source_target_pairs={{0,1},{1,0},{2,3},{3,2},{4,5},{5,4},{6,7},{7,6},{8,9},{9,8},{10,11... | collective-permute-start | bytes 2359304 | tf_op jit(solution)/shard_map/ppermute | solution.py:24
  206.7 33.6 %collective-permute-start.26 = (bf16[2,2,64,512]{3,2,1,0:T(8,128)(2,1)S(1)}, bf16[2,2,64,512]{3,2,1,0:T(8,128)(2,1)S(1)}, u32[]{:S(2)}, u32[]{:S(2)}) collective-permute-start(bf16[2,2,64,512]{3,2,1,0:T(8,128)(2,1)S(1)} %slice.246), channel_id=1, source_target_pairs={{0,1},{1,0},{2,3},{3,2},{4,5},{5,4},{6,7},{7,6},{8,9},{9,8},{10,11... | collective-permute-start | bytes 786440 | tf_op jit(solution)/shard_map/ppermute | solution.py:24
  207.8 35.1 %collective-permute-start.23 = (bf16[2,2,64,512]{3,2,1,0:T(8,128)(2,1)S(1)}, bf16[2,2,64,512]{3,2,1,0:T(8,128)(2,1)S(1)}, u32[]{:S(2)}, u32[]{:S(2)}) collective-permute-start(bf16[2,2,64,512]{3,2,1,0:T(8,128)(2,1)S(1)} %slice.247), channel_id=1, source_target_pairs={{0,2},{1,3},{2,0},{3,1},{4,6},{5,7},{6,4},{7,5},{8,10},{9,11},{10,... | collective-permute-start | bytes 786440 | tf_op jit(solution)/shard_map/ppermute | solution.py:24
  219.0 24.6 %collective-permute-start.20 = (bf16[2,2,64,512]{3,2,1,0:T(8,128)(2,1)S(1)}, bf16[2,2,64,512]{3,2,1,0:T(8,128)(2,1)S(1)}, u32[]{:S(2)}, u32[]{:S(2)}) collective-permute-start(bf16[2,2,64,512]{3,2,1,0:T(8,128)(2,1)S(1)} %slice.248), channel_id=1, source_target_pairs={{0,2},{1,3},{2,0},{3,1},{4,6},{5,7},{6,4},{7,5},{8,10},{9,11},{10,... | collective-permute-start | bytes 786440 | tf_op jit(solution)/shard_map/ppermute | solution.py:24
  240.4 15.1 %collective-permute-start.27 = (bf16[1,2,64,512]{3,2,1,0:T(8,128)(2,1)S(1)}, bf16[1,2,64,512]{3,2,1,0:T(8,128)(2,1)S(1)}, u32[]{:S(2)}, u32[]{:S(2)}) collective-permute-start(bf16[1,2,64,512]{3,2,1,0:T(8,128)(2,1)S(1)} %slice.250), channel_id=1, source_target_pairs={{0,4},{1,5},{2,6},{3,7},{4,0},{5,1},{6,2},{7,3},{8,12},{9,13},{10,... | collective-permute-start | bytes 393224 | tf_op jit(solution)/shard_map/ppermute | solution.py:24
  243.0 15.3 %collective-permute-start.24 = (bf16[1,2,64,512]{3,2,1,0:T(8,128)(2,1)S(1)}, bf16[1,2,64,512]{3,2,1,0:T(8,128)(2,1)S(1)}, u32[]{:S(2)}, u32[]{:S(2)}) collective-permute-start(bf16[1,2,64,512]{3,2,1,0:T(8,128)(2,1)S(1)} %slice.251), channel_id=1, source_target_pairs={{0,4},{1,5},{2,6},{3,7},{4,0},{5,1},{6,2},{7,3},{8,12},{9,13},{10,... | collective-permute-start | bytes 393224 | tf_op jit(solution)/shard_map/ppermute | solution.py:24
  243.7 21.9 %collective-permute-start.21 = (bf16[1,2,64,512]{3,2,1,0:T(8,128)(2,1)S(1)}, bf16[1,2,64,512]{3,2,1,0:T(8,128)(2,1)S(1)}, u32[]{:S(2)}, u32[]{:S(2)}) collective-permute-start(bf16[1,2,64,512]{3,2,1,0:T(8,128)(2,1)S(1)} %slice.252), channel_id=1, source_target_pairs={{0,4},{1,5},{2,6},{3,7},{4,0},{5,1},{6,2},{7,3},{8,12},{9,13},{10,... | collective-permute-start | bytes 393224 | tf_op jit(solution)/shard_map/ppermute | solution.py:24
  246.5 16.7 %collective-permute-start.17 = (bf16[2,3,64,512]{3,2,1,0:T(8,128)(2,1)S(1)}, bf16[2,3,64,512]{3,2,1,0:T(8,128)(2,1)S(1)}, u32[]{:S(2)}, u32[]{:S(2)}) collective-permute-start(bf16[2,3,64,512]{3,2,1,0:T(8,128)(2,1)S(1)} %slice.245), channel_id=1, source_target_pairs={{0,2},{1,3},{2,0},{3,1},{4,6},{5,7},{6,4},{7,5},{8,10},{9,11},{10,... | collective-permute-start | bytes 1179656 | tf_op jit(solution)/shard_map/ppermute | solution.py:24
  263.4 8.7 %collective-permute-start.18 = (bf16[1,3,64,512]{3,2,1,0:T(8,128)(2,1)S(1)}, bf16[1,3,64,512]{3,2,1,0:T(8,128)(2,1)S(1)}, u32[]{:S(2)}, u32[]{:S(2)}) collective-permute-start(bf16[1,3,64,512]{3,2,1,0:T(8,128)(2,1)S(1)} %slice.249), channel_id=1, source_target_pairs={{0,4},{1,5},{2,6},{3,7},{4,0},{5,1},{6,2},{7,3},{8,12},{9,13},{10,... | collective-permute-start | bytes 589832 | tf_op jit(solution)/shard_map/ppermute | solution.py:24
  272.3 1.0 copy-start.29

commit v2 on v1

v2 whole, which is shorter than its diff:
```python
import functools
import math

import jax
import jax.numpy as jnp
from jax import lax
from jax.experimental import pallas as pl
from jax.experimental.pallas import tpu as pltpu
from jax.sharding import PartitionSpec as P

TXT_LEN = 77
RES = 16
F32 = jnp.float32
BF16 = jnp.bfloat16
VMEM = pltpu.VMEM
LIMIT = 48 * 1024 * 1024
SLOTS = 24


def params():
    return pltpu.CompilerParams(vmem_limit_bytes=LIMIT)


def swap(x, bit, count):
    return lax.ppermute(x, "dp", [(i, i ^ bit) for i in range(count)])


def column_masks(rows, side):
    column = lax.broadcasted_iota(jnp.int32, (rows, 1), 0) % side
    return column != 0, column != side - 1


def put_shifts(pieces, value, side, at, rows, pad):
    not_first, not_last = column_masks(rows, side)
    left = jnp.where(not_first, pltpu.roll(value, 1, 0), 0.0)
    right = jnp.where(not_last, pltpu.roll(value, rows - 1, 0), 0.0)
    for index, shifted in enumerate((left, value, right)):
        pieces[index, pl.ds(at, rows), :] = shifted.astype(BF16)


def blank_edges(pieces, rows, pad):
    blank = jnp.zeros((pad, pieces.shape[2]), BF16)
    for index in range(3):
        pieces[index, pl.ds(0, pad), :] = blank
        pieces[index, pl.ds(pad + rows, pad), :] = blank


def conv_of(pieces, weight, sign, side, rows):
    channels = pieces.shape[2]
    total = None
    for tap in range(9):
        down, across = sign * (tap // 3 - 1), sign * (tap % 3 - 1)
        term = jnp.dot(
            pieces[across + 1, pl.ds(side + down * side, rows), :],
            weight[pl.ds(tap * channels, channels), :],
            preferred_element_type=F32,
        )
        total = term if total is None else total + term
    return total


def forward_kernel(tick, side, micro, *refs):
    if tick:
        received, start, pack, head, weight = refs[:5]
        refs = refs[7:]
    else:
        start, pack, head, weight = refs[:4]
        received = start
        refs = refs[4:]
    out, kept_in, kept_conv, score, pieces, mod_box, conv_box, sems = refs
    rows = start.shape[0]
    section = lax.axis_index("section")
    position = tick - section

    @pl.when((position >= 0) & (position < micro))
    def _():
        blank_edges(pieces, rows, side)
        style = pack[pl.ds(position, 1), :]
        source = received[...]
        if tick:
            source = jnp.where(section == 0, start[...].astype(F32), source.astype(F32))
        mod = (style * source.astype(F32)).astype(BF16)
        mod_box[...] = mod.reshape(mod_box.shape)
        first = pltpu.make_async_copy(mod_box, kept_in.at[:, position], sems.at[0])
        first.start()
        put_shifts(pieces, mod.astype(F32), side, side, rows, side)
        conv = conv_of(pieces, weight, 1, side, rows)
        conv_box[...] = conv
        second = pltpu.make_async_copy(conv_box, kept_conv.at[position], sems.at[1])
        second.start()
        pre = pack[pl.ds(8 + position, 1), :] * conv
        result = (pre / (1.0 + jnp.exp(-pre))).astype(BF16)
        out[...] = result
        sums = jnp.sum(result.astype(F32), axis=0, keepdims=True) * head[...]
        score[...] = jnp.broadcast_to(jnp.sum(sums, axis=1, keepdims=True), score.shape)
        first.wait()
        second.wait()


def backward_kernel(tick, side, micro, norm_div, *refs):
    if tick:
        received = refs[0]
        refs = refs[1:]
    head, pack = refs[:2]
    scores, refs = refs[2 : 2 + micro], refs[2 + micro :]
    kept_conv, weight = refs[:2]
    refs = refs[4:] if tick else refs[2:]
    out, kept_grad, kept_term, pieces, conv_box, grad_box, term_box, sems = refs
    rows = conv_box.shape[0]
    section = lax.axis_index("section")
    sections = lax.axis_size("section")
    gen_count = sections - sections // 4
    position = tick - (sections - 1 - section)

    @pl.when((position >= 0) & (position < micro))
    def _():
        load = pltpu.make_async_copy(kept_conv.at[position], conv_box, sems.at[0])
        load.start()
        blank_edges(pieces, rows, side)
        raw = scores[0][...]
        for index in range(1, micro):
            raw = jnp.where(position == index, scores[index][...], raw)
        raw = raw[:1, :1] / norm_div
        d_factor = (1.0 / (1.0 + jnp.exp(-raw))).astype(BF16).astype(F32)
        g_factor = (-1.0 / (1.0 + jnp.exp(raw))).astype(BF16).astype(F32)
        scale = jnp.where(section < gen_count, jnp.ones_like(raw), d_factor)
        boost = jnp.where(section == gen_count, g_factor, jnp.ones_like(raw))
        demod = pack[pl.ds(8 + position, 1), :]
        unit = (head[...] / norm_div).astype(BF16).astype(F32)
        incoming = jnp.broadcast_to(unit, conv_box.shape)
        if tick:
            incoming = jnp.where(section == sections - 1, incoming, received[...].astype(F32))
        load.wait()
        conv = conv_box[...]
        pre = demod * conv
        sigma = 1.0 / (1.0 + jnp.exp(-pre))
        grad_pre = incoming * sigma * (1.0 + pre * (1.0 - sigma))
        grad_conv = demod * grad_pre
        grad_box[...] = (scale * grad_conv).astype(BF16).reshape(grad_box.shape)
        first = pltpu.make_async_copy(grad_box, kept_grad.at[:, position], sems.at[1])
        first.start()
        term = jnp.sum(grad_pre * conv, axis=0, keepdims=True) * demod * demod * demod
        term = jnp.where(section < gen_count, term, 0.0)
        term_box[...] = jnp.broadcast_to(term, term_box.shape)
        second = pltpu.make_async_copy(term_box, kept_term.at[position], sems.at[2])
        second.start()
        put_shifts(pieces, grad_conv.astype(BF16).astype(F32), side, side, rows, side)
        back = conv_of(pieces, weight, -1, side, rows)
        out[...] = (pack[pl.ds(position, 1), :] * boost * back).astype(BF16)
        first.wait()
        second.wait()


def slot_flip(slot, order):
    flip = 0
    for stage, bit in enumerate(order):
        flip |= ((slot >> (len(order) - 1 - stage)) & 1) << bit
    return flip


def weight_grad_kernel(
    side, micro, count, orders, taps, kept_grad, kept_in, kept_term, pack, weight, *rest
):
    outs, rest = rest[: 2 * len(taps)], rest[2 * len(taps) :]
    pieces, grad_rows, mod_rows, terms, by_out, mixture, sems = rest
    channels = kept_in.shape[3]
    total_rows = micro * side * side
    part = channels // count
    band = micro * side
    here = lax.axis_index("dp")
    chosen = pl.ds(0, micro)
    loads = [
        pltpu.make_async_copy(kept_grad.at[:, chosen], grad_rows, sems.at[0]),
        pltpu.make_async_copy(kept_in.at[:, chosen], mod_rows, sems.at[1]),
        pltpu.make_async_copy(kept_term.at[chosen], terms, sems.at[2]),
    ]
    for load in loads:
        load.start()
    blank = jnp.zeros((band, channels), BF16)
    for index in range(3):
        pieces[index, pl.ds(0, band), :] = blank
        pieces[index, pl.ds(band + total_rows, band), :] = blank
    loads[1].wait()
    put_shifts(
        pieces, mod_rows[...].reshape(total_rows, channels).astype(F32), side, band, total_rows, band
    )
    loads[0].wait()
    turned = jnp.transpose(grad_rows[...].reshape(total_rows, channels).astype(F32)).astype(BF16)
    by_out[len(orders)] = turned
    loads[2].wait()
    row = lax.broadcasted_iota(jnp.int32, (8, channels), 0)
    stacked = jnp.zeros((8, channels), F32)
    for sample in range(micro):
        stacked = jnp.where(row == sample, terms[sample], stacked)
    mixture[...] = lax.dot_general(
        stacked, pack[pl.ds(0, 8), :] * pack[pl.ds(0, 8), :], (((0,), (0,)), ((), ())),
        preferred_element_type=F32, precision=lax.Precision.HIGHEST,
    )
    for kind, order in enumerate(orders):
        for slot in range(count):
            source = pl.multiple_of((here ^ slot_flip(slot, order)) * part, part)
            by_out[kind, pl.ds(slot * part, part), :] = by_out[len(orders), pl.ds(source, part), :]
    for chunk, (kind, tap_list) in enumerate(taps):
        keep, send = outs[2 * chunk], outs[2 * chunk + 1]
        for spot, tap in enumerate(tap_list):
            total = jnp.dot(
                by_out[kind], pieces[tap % 3, pl.ds((tap // 3) * band, total_rows), :],
                preferred_element_type=F32,
            )
            for slot in range(count):
                source = pl.multiple_of((here ^ slot_flip(slot, orders[kind])) * part, part)
                fixed = total[slot * part : (slot + 1) * part] - weight[
                    pl.ds(tap * channels + source, part), :
                ].astype(F32) * mixture[pl.ds(source, part), :]
                target = keep if slot < count // 2 else send
                target[slot % (count // 2), spot] = fixed.astype(BF16)


def on_device(
    text_ids, seed_ids, text_table, latent_table, start_map, style_weight, conv_weight, score_head
):
    sections = lax.axis_size("section")
    count = lax.axis_size("dp")
    bits = count.bit_length() - 1
    gen_count = sections - sections // 4
    section_at = lax.axis_index("section")
    here = lax.axis_index("dp")
    is_gen = section_at < gen_count
    micro = seed_ids.shape[0]
    channels, pixels = start_map.shape
    side = RES
    vocab_rows = text_table.shape[0]
    norm_div = pixels * math.sqrt(channels)

    ids = text_ids[None]
    weight = conv_weight[0]
    weight_out = jnp.transpose(weight, (1, 0, 2))
    weight_in = jnp.transpose(weight, (1, 2, 0)).reshape(9 * channels, channels)
    first_map = start_map.T
    latent = jnp.take(latent_table, seed_ids, axis=0)
    for stage in range(bits):
        other = swap(ids, 1 << stage, count)
        if stage == 0:
            other, weight_in, first_map, latent = lax.optimization_barrier(
                (other, weight_in, first_map, latent)
            )
        ids = jnp.concatenate([ids, other], axis=0)
    wanted = ids.reshape(count * micro, TXT_LEN) - here * vocab_rows
    rows = lax.broadcasted_iota(jnp.int32, (1, 1, vocab_rows), 2)
    hits = jnp.sum((wanted[:, :, None] == rows).astype(F32), axis=1)
    sums = jnp.dot(hits.astype(BF16), text_table, preferred_element_type=F32)
    sums = sums.reshape(count, micro, channels)
    for stage in reversed(range(bits)):
        half = 1 << stage
        sums = sums[:half] + swap(sums[half:], half, count)
    text_mean = sums[0] / TXT_LEN

    squares = jnp.sum(jnp.square(weight_out.astype(F32)), axis=0)

    code_now = jnp.where(is_gen, latent + text_mean, text_mean).astype(BF16)
    styles = 1.0 + lax.dot_general(
        code_now, style_weight[0], (((1,), (1,)), ((), ())), preferred_element_type=F32
    )
    demods = lax.rsqrt(
        lax.dot_general(
            styles * styles, squares, (((1,), (1,)), ((), ())), precision=lax.Precision.HIGHEST
        )
        + 1e-08
    )
    demods = jnp.where(is_gen, demods, jnp.ones_like(demods))
    rest = ((0, 8 - micro), (0, 0))
    pack = jnp.concatenate([jnp.pad(styles, rest), jnp.pad(demods, rest)], axis=0)
    head = score_head[None]
    ticks = micro + sections - 1

    whole = pl.BlockSpec(memory_space=VMEM)
    far = pl.BlockSpec(memory_space=pltpu.HBM)
    flops = 2 * 9 * channels * channels * pixels
    conv_cost = pl.CostEstimate(
        flops=flops, bytes_accessed=9 * channels * channels * 2 + 5 * channels * pixels * 2,
        transcendentals=channels * pixels,
    )
    tall = 2 * side + pixels
    conv_scratch = [VMEM((3, tall, channels), BF16)]
    plain = jax.ShapeDtypeStruct((pixels, channels), BF16)
    lined = jax.ShapeDtypeStruct((side, SLOTS, side, channels), BF16)
    tower = jax.ShapeDtypeStruct((SLOTS, pixels, channels), F32)
    rows_kept = jax.ShapeDtypeStruct((1024, 8, channels), F32)

    def forward(tick, arrays):
        return pl.pallas_call(
            functools.partial(forward_kernel, tick, side, micro),
            in_specs=[whole] * 5 + [far] * 2 if tick else [whole] * 4,
            out_specs=[whole, far, far, whole],
            out_shape=[plain, lined, tower, jax.ShapeDtypeStruct((8, 128), F32)],
            scratch_shapes=conv_scratch
            + [
                VMEM((side, side, channels), BF16),
                VMEM((pixels, channels), F32),
                pltpu.SemaphoreType.DMA((2,)),
            ],
            input_output_aliases={5: 1, 6: 2} if tick else {},
            cost_estimate=conv_cost,
            compiler_params=params(),
            name="forward_conv",
        )(*arrays)

    def backward(tick, arrays):
        fixed = 3 + micro if tick else 2 + micro
        return pl.pallas_call(
            functools.partial(backward_kernel, tick, side, micro, norm_div),
            in_specs=[whole] * fixed + [far, whole] + [far] * (2 if tick else 0),
            out_specs=[whole, far, far],
            out_shape=[plain, lined, rows_kept],
            scratch_shapes=conv_scratch
            + [
                VMEM((pixels, channels), F32),
                VMEM((side, side, channels), BF16),
                VMEM((8, channels), F32),
                pltpu.SemaphoreType.DMA((3,)),
            ],
            input_output_aliases={fixed + 2: 1, fixed + 3: 2} if tick else {},
            cost_estimate=conv_cost,
            compiler_params=params(),
            name="backward_conv",
        )(*arrays)

    scores = []
    kept_in = kept_conv = outgoing = None
    for tick in range(ticks):
        if tick:
            received = lax.ppermute(
                outgoing, "section", [(i, i + 1) for i in range(sections - 1) if 0 <= tick - 1 - i < micro]
            )
            arrays = (received, first_map, pack, head, weight_in, kept_in, kept_conv)
        else:
            arrays = (first_map, pack, head, weight_in)
        outgoing, kept_in, kept_conv, score = forward(tick, arrays)
        scores.append(score)
    scores = scores[sections - 1 :]
    for hop in range(sections - gen_count - 1):
        target = sections - 2 - hop
        passed = lax.ppermute(scores, "section", [(target + 1, target)])
        scores = [jnp.where(section_at == target, new, old) for new, old in zip(passed, scores)]

    flat_out = weight_out.reshape(9 * channels, channels)
    kept_grad = kept_term = outgoing = None
    for tick in range(ticks):
        arrays = (head, pack, *scores, kept_conv, flat_out)
        if tick:
            received = lax.ppermute(
                outgoing, "section",
                [(i, i - 1) for i in range(1, sections) if 0 <= tick - 1 - (sections - 1 - i) < micro],
            )
            arrays = (received, *arrays, kept_grad, kept_term)
        outgoing, kept_grad, kept_term = backward(tick, arrays)

    part = channels // count
    orders = (tuple(range(bits)), (1, 0) + tuple(range(2, bits)))
    taps = ((0, (0, 1, 2)), (0, (3, 4)), (1, (7, 8)), (0, (5, 6)))
    shapes = []
    for kind, tap_list in taps:
        shapes += [jax.ShapeDtypeStruct((count // 2, len(tap_list), part, channels), BF16)] * 2
    pairs = pl.pallas_call(
        functools.partial(weight_grad_kernel, side, micro, count, orders, taps),
        in_specs=[far] * 3 + [whole] * 2,
        out_specs=[whole] * len(shapes),
        out_shape=shapes,
        scratch_shapes=[
            VMEM((3, micro * tall, channels), BF16),
            VMEM((side, micro, side, channels), BF16),
            VMEM((side, micro, side, channels), BF16),
            VMEM((micro, 8, channels), F32),
            VMEM((len(orders) + 1, channels, micro * pixels), BF16),
            VMEM((channels, channels), F32),
            pltpu.SemaphoreType.DMA((3,)),
        ],
        cost_estimate=pl.CostEstimate(flops=micro * flops, bytes_accessed=20 * 1024 * 1024, transcendentals=0),
        compiler_params=params(),
        name="weight_grad",
    )(kept_grad, kept_in, kept_term, pack, flat_out)
    done = [None] * 9
    for chunk, (kind, tap_list) in enumerate(taps):
        keep, send = pairs[2 * chunk], pairs[2 * chunk + 1]
        for stage in range(bits):
            got = swap(send, 1 << orders[kind][stage], count)
            total = keep.astype(F32) + got.astype(F32)
            half = total.shape[0] // 2
            if half:
                keep = total[:half]
                send = total[half:].astype(BF16)
        for spot, tap in enumerate(tap_list):
            done[tap] = total[0, spot]
    return jnp.stack(done, axis=1)[None]


def solution(mesh):
    placed = (
        P("dp", None),
        P("dp"),
        P("dp", None),
        P(),
        P(),
        P("section", None, None),
        P("section", None, None, None),
        P(),
    )
    return jax.shard_map(
        on_device,
        mesh=mesh,
        in_specs=placed,
        out_specs=P("section", "dp", None, None),
        check_vma=False,
    )
```

time: 275 us -> 209 us (0.76)
  local copies, waits for them, and re-layouts: 56.9 us -> 13.8 us
  Pallas kernels: 45.9 us -> 29.7 us
  waiting for transfers between devices: 110 us -> 105 us
  starting transfers between devices: 46.1 us -> 49.8 us
    unnamed x75 -> x29, local copies, waits for them, and re-layouts: 47 us -> 6.01 us
    ppermute x18, waiting for transfers between devices: 71.4 us -> 49.5 us  [swap(): return lax.ppermute(x, 'dp', [(i, i ^ bit) for i in range(count)])]
    pallas_call x12, Pallas kernels: 38.4 us -> 20.4 us  [the longest x6 10.9 us: backward(): pl.pallas_call(functools.partial(backward_kernel, tick, side, micro, norm...]
    ppermute x5, waiting for transfers between devices: 36.4 us -> 51.9 us  [on_device(): lax.ppermute(outgoing, 'section', [(i, i - 1) for i in range(1, sections)...]
    ppermute x18, starting transfers between devices: 28.7 us -> 35.6 us  [swap(): return lax.ppermute(x, 'dp', [(i, i ^ bit) for i in range(count)])]
    ppermute x5, starting transfers between devices: 11.9 us -> 9.03 us  [on_device(): lax.ppermute(outgoing, 'section', [(i, i + 1) for i in range(sections - 1...]
  transfers between devices with their start and end apart: 28 -> 28, of which waited for: 18 -> 16; matrix products, arithmetic and copies ran while one was open for 6% -> 7% of each run, Pallas kernels for 0% -> 0%
where the time goes in v2:
time: 209 us; the launch traced here: 208 us
  waiting for transfers between devices  105 us (50%)
  starting transfers between devices  49.8 us (24%)
  Pallas kernels  29.7 us (14%)
  local copies, waits for them, and re-layouts  13.8 us (7%)
  other arithmetic  7.61 us (4%)
    ppermute x5, waiting for transfers between devices, on_device(): lax.ppermute(outgoing, 'section', [(i, i - 1) for i in range(1, sections)...  51.9 us
    ppermute x18, waiting for transfers between devices, swap(): return lax.ppermute(x, 'dp', [(i, i ^ bit) for i in range(count)])  49.5 us
    ppermute x18, starting transfers between devices, swap(): return lax.ppermute(x, 'dp', [(i, i ^ bit) for i in range(count)])  35.6 us
    pallas_call x6, Pallas kernels, backward(): pl.pallas_call(functools.partial(backward_kernel, tick, side, micro, norm...  10.9 us
    pallas_call x6, Pallas kernels, forward(): pl.pallas_call(functools.partial(forward_kernel, tick, side, micro), in_s...  9.51 us
    pallas_call x1, Pallas kernels, on_device(): pl.pallas_call(functools.partial(weight_grad_kernel, side, micro, count,...  9.27 us
    ppermute x5, starting transfers between devices, on_device(): lax.ppermute(outgoing, 'section', [(i, i + 1) for i in range(sections - 1...  9.03 us
    transpose x1, local copies, waits for them, and re-layouts, on_device(): weight_in = jnp.transpose(weight, (1, 2, 0)).reshape(9 * channels, channels)  6.84 us
  transfers between devices with their start and end apart: 28, of which 16 were waited for; matrix products, arithmetic and copies ran while one was open for 7% of the time, Pallas kernels for 0%

profile of v2, /device:TPU:0, one launch (start us, length us, event | category | flops | bytes accessed | tf_op | source)
XLA Modules:
  0.0 207.9 jit_solution(16795029017991426707)
XLA Ops:
  0.0 3.0 %collective-permute-start = (s32[1,3,77]{2,1,0:T(4,128)}, s32[1,3,77]{2,1,0:T(4,128)S(1)}, u32[]{:S(2)}, u32[]{:S(2)}) collective-permute-start(s32[1,3,77]{2,1,0:T(4,128)} %bitcast.94), channel_id=1, source_target_pairs={{0,1},{1,0},{2,3},{3,2},{4,5},{5,4},{6,7},{7,6},{8,9},{9,8},{10,11... | collective-permute-start | bytes 2780 | tf_op jit(solution)/shard_map/ppermute | solution.py:25
  3.0 0.7 compare_and_fusion
  3.7 0.7 compare_select_fusion
  4.3 0.6 gather_fusion
  5.0 1.1 copy.34
  6.1 6.8 %copy.33 = bf16[9,512,512]{2,1,0:T(8,128)(2,1)} copy(bf16[9,512,512]{1,2,0:T(8,128)(2,1)} %bitcast.60) | data formatting | bytes 9437184 | tf_op jit(solution)/shard_map/transpose | solution.py:238
  12.9 1.6 collective-permute-start.1
  14.6 2.0 collective-permute-done.1
  16.6 2.6 %collective-permute-start.2 = (s32[4,3,77]{2,1,0:T(4,128)S(1)}, s32[4,3,77]{2,1,0:T(4,128)S(1)}, u32[]{:S(2)}, u32[]{:S(2)}) collective-permute-start(s32[4,3,77]{2,1,0:T(4,128)S(1)} %pad_add_fusion), channel_id=1, source_target_pairs={{0,4},{1,5},{2,6},{3,7},{4,0},{5,1},{6,2},{7,3},{8,12},{9,13},{10,... | collective-permute-start | bytes 11096 | tf_op jit(solution)/shard_map/ppermute | solution.py:25
  19.2 2.0 collective-permute-done.2
  21.3 1.6 convert_reduce_fusion
  22.9 0.3 fusion.23
  23.3 2.7 %collective-permute-start.3 = (f32[4,3,512]{2,1,0:T(4,128)S(1)}, f32[4,3,512]{2,1,0:T(4,128)S(1)}, u32[]{:S(2)}, u32[]{:S(2)}) collective-permute-start(f32[4,3,512]{2,1,0:T(4,128)S(1)} %slice.110), channel_id=1, source_target_pairs={{0,4},{1,5},{2,6},{3,7},{4,0},{5,1},{6,2},{7,3},{8,12},{9,13},{10,... | collective-permute-start | bytes 73736 | tf_op jit(solution)/shard_map/ppermute | solution.py:25
  26.0 2.2 %collective-permute-done.3 = f32[4,3,512]{2,1,0:T(4,128)S(1)} collective-permute-done((f32[4,3,512]{2,1,0:T(4,128)S(1)}, f32[4,3,512]{2,1,0:T(4,128)S(1)}, u32[]{:S(2)}, u32[]{:S(2)}) %collective-permute-start.3) | collective-permute-done | bytes 24608 | tf_op jit(solution)/shard_map/ppermute | solution.py:25
  28.2 1.8 collective-permute-start.4
  30.0 2.0 collective-permute-done.4
  32.0 0.4 collective-permute-start.5
  32.4 3.4 %multiply_reduce_fusion = f32[512,512]{1,0:T(8,128)S(1)} fusion(bf16[1,512,9,512]{3,1,2,0:T(8,128)(2,1)} %param.14), kind=kLoop, calls=%fused_computation.3 | loop fusion | flops 6815744 | bytes 5767168 | tf_op jit(solution)/shard_map/reduce_sum | solution.py:258
  35.8 0.2 convolution_add_fusion.1
  36.1 1.0 fusion.1
  37.1 2.3 %copy-done.2 = bf16[9,512,512]{2,1,0:T(8,128)(2,1)S(1)} copy-done((bf16[9,512,512]{2,1,0:T(8,128)(2,1)S(1)}, bf16[9,512,512]{2,1,0:T(8,128)(2,1)}, u32[]{:S(2)}) %copy-start.2) | copy-done | bytes 4718616
  39.4 2.8 %forward_conv.6 = (bf16[256,512]{1,0:T(8,128)(2,1)S(1)}, bf16[16,24,16,512]{3,2,1,0:T(8,128)(2,1)}, f32[24,256,512]{2,1,0:T(8,128)}, f32[8,128]{1,0:T(8,128)}) custom-call(bf16[256,512]{1,0:T(8,128)(2,1)S(1)} %bitcast.76, f32[16,512]{1,0:T(8,128)S(1)} %select_maximum_fusion.refs_1_.refs_2_.pack, f32[1,512]{1,0:T(1,128)S(1)} %bitcast.82, ...), custom_call_target="tpu_custom_call" | custom-call | flops 1207959552 | bytes 6029312 | tf_op jit(solution)/shard_map/forward_conv/pallas_call | solution.py:291
  42.3 1.3 collective-permute-start.6
  43.6 1.1 collective-permute-done.6.refs_0_
  44.7 2.9 %forward_conv.7 = (bf16[256,512]{1,0:T(8,128)(2,1)S(1)}, bf16[16,24,16,512]{3,2,1,0:T(8,128)(2,1)}, f32[24,256,512]{2,1,0:T(8,128)}, f32[8,128]{1,0:T(8,128)}) custom-call(bf16[256,512]{1,0:T(8,128)(2,1)S(1)} %collective-permute-done.6.refs_0_, bf16[256,512]{1,0:T(8,128)(2,1)S(1)} %bitcast.77, ...), custom_call_target="tpu_custom_call", output_to_operand_aliasing={{1}: (5, {}), {2}: (6, {})} | custom-call | flops 1207959552 | bytes 6029312 | tf_op jit(solution)/shard_map/forward_conv/pallas_call | solution.py:291
  47.6 2.3 %collective-permute-start.7 = (bf16[256,512]{1,0:T(8,128)(2,1)S(1)}, bf16[256,512]{1,0:T(8,128)(2,1)S(1)}, u32[]{:S(2)}, u32[]{:S(2)}) collective-permute-start(bf16[256,512]{1,0:T(8,128)(2,1)S(1)} %get-tuple-element.61), channel_id=1, source_target_pairs={{0,8},{8,16},{1,9},{9,17},{2,10},{10,18},{3,11},{11,19},{4,12},{12... | collective-permute-start | bytes 786440 | tf_op jit(solution)/shard_map/ppermute | solution.py:332
  49.9 1.1 collective-permute-done.7.refs_0_
  51.0 2.8 %forward_conv.8 = (bf16[256,512]{1,0:T(8,128)(2,1)S(1)}, bf16[16,24,16,512]{3,2,1,0:T(8,128)(2,1)}, f32[24,256,512]{2,1,0:T(8,128)}, f32[8,128]{1,0:T(8,128)}) custom-call(bf16[256,512]{1,0:T(8,128)(2,1)S(1)} %collective-permute-done.7.refs_0_, bf16[256,512]{1,0:T(8,128)(2,1)S(1)} %bitcast.78, ...), custom_call_target="tpu_custom_call", output_to_operand_aliasing={{1}: (5, {}), {2}: (6, {})} | custom-call | flops 1207959552 | bytes 6029312 | tf_op jit(solution)/shard_map/forward_conv/pallas_call | solution.py:291
  53.8 4.1 %collective-permute-start.8 = (bf16[256,512]{1,0:T(8,128)(2,1)S(1)}, bf16[256,512]{1,0:T(8,128)(2,1)S(1)}, u32[]{:S(2)}, u32[]{:S(2)}) collective-permute-start(bf16[256,512]{1,0:T(8,128)(2,1)S(1)} %get-tuple-element.64), channel_id=1, source_target_pairs={{0,8},{8,16},{16,24},{1,9},{9,17},{17,25},{2,10},{10,18},{18,26},{... | collective-permute-start | bytes 786440 | tf_op jit(solution)/shard_map/ppermute | solution.py:332
  58.0 1.1 collective-permute-done.8.refs_0_
  59.1 0.7 collective-permute-start.9
  59.8 0.7 collective-permute-start.10
  60.6 0.9 forward_conv.11
  61.5 1.3 slice-done
  63.0 0.7 collective-permute-start.11
  63.7 0.7 collective-permute-start.12
  64.5 1.3 collective-permute-start.13
  65.8 39.7 %collective-permute-done.13.refs_0_ = bf16[256,512]{1,0:T(8,128)(2,1)S(1)} collective-permute-done((bf16[256,512]{1,0:T(8,128)(2,1)S(1)}, bf16[256,512]{1,0:T(8,128)(2,1)S(1)}, u32[]{:S(2)}, u32[]{:S(2)}) %collective-permute-start.13) | collective-permute-done | bytes 262176 | tf_op jit(solution)/shard_map/ppermute | solution.py:351
  105.5 3.4 %backward_conv.9 = (bf16[256,512]{1,0:T(8,128)(2,1)S(1)}, bf16[16,24,16,512]{3,2,1,0:T(8,128)(2,1)}, f32[1024,8,512]{2,1,0:T(8,128)}) custom-call(bf16[256,512]{1,0:T(8,128)(2,1)S(1)} %collective-permute-done.13.refs_0_, f32[1,512]{1,0:T(1,128)S(1)} %bitcast.91, ...), custom_call_target="tpu_custom_call", output_to_operand_aliasing={{1}: (8, {}), {2}: (9, {})} | custom-call | flops 1207959552 | bytes 6029312 | tf_op jit(solution)/shard_map/backward_conv/pallas_call | solution.py:310
  108.9 1.3 collective-permute-start.14
  110.2 6.4 %collective-permute-done.14.refs_0_ = bf16[256,512]{1,0:T(8,128)(2,1)S(1)} collective-permute-done((bf16[256,512]{1,0:T(8,128)(2,1)S(1)}, bf16[256,512]{1,0:T(8,128)(2,1)S(1)}, u32[]{:S(2)}, u32[]{:S(2)}) %collective-permute-start.14) | collective-permute-done | bytes 262176 | tf_op jit(solution)/shard_map/ppermute | solution.py:351
  116.6 3.3 %backward_conv.10 = (bf16[256,512]{1,0:T(8,128)(2,1)S(1)}, bf16[16,24,16,512]{3,2,1,0:T(8,128)(2,1)}, f32[1024,8,512]{2,1,0:T(8,128)}) custom-call(bf16[256,512]{1,0:T(8,128)(2,1)S(1)} %collective-permute-done.14.refs_0_, f32[1,512]{1,0:T(1,128)S(1)} %bitcast.92, ...), custom_call_target="tpu_custom_call", output_to_operand_aliasing={{1}: (8, {}), {2}: (9, {})} | custom-call | flops 1207959552 | bytes 6029312 | tf_op jit(solution)/shard_map/backward_conv/pallas_call | solution.py:310
  119.9 1.3 collective-permute-start.15
  121.2 5.8 %collective-permute-done.15.refs_0_ = bf16[256,512]{1,0:T(8,128)(2,1)S(1)} collective-permute-done((bf16[256,512]{1,0:T(8,128)(2,1)S(1)}, bf16[256,512]{1,0:T(8,128)(2,1)S(1)}, u32[]{:S(2)}, u32[]{:S(2)}) %collective-permute-start.15) | collective-permute-done | bytes 262176 | tf_op jit(solution)/shard_map/ppermute | solution.py:351
  127.0 4.1 %backward_conv.11 = (bf16[256,512]{1,0:T(8,128)(2,1)}, bf16[16,24,16,512]{3,2,1,0:T(8,128)(2,1)}, f32[1024,8,512]{2,1,0:T(8,128)}) custom-call(bf16[256,512]{1,0:T(8,128)(2,1)S(1)} %collective-permute-done.15.refs_0_, f32[1,512]{1,0:T(1,128)S(1)} %bitcast.93, ...), custom_call_target="tpu_custom_call", output_to_operand_aliasing={{1}: (8, {}), {2}: (9, {})} | custom-call | flops 1207959552 | bytes 6029312 | tf_op jit(solution)/shard_map/backward_conv/pallas_call | solution.py:310
  131.1 9.3 %weight_grad.1 = (bf16[4,3,64,512]{3,2,1,0:T(8,128)(2,1)S(1)}, bf16[4,3,64,512]{3,2,1,0:T(8,128)(2,1)S(1)}, bf16[4,2,64,512]{3,2,1,0:T(8,128)(2,1)S(1)}, bf16[4,...) custom-call(bf16[16,24,16,512]{3,2,1,0:T(8,128)(2,1)} %get-tuple-ele, ...), custom_call_target="tpu_custom_call" | custom-call | flops 3623878656 | bytes 20971520 | tf_op jit(solution)/shard_map/weight_grad/pallas_call | solution.py:364
  140.3 1.8 collective-permute-start.19
  142.1 0.3 collective-permute-start.22
  142.4 2.0 collective-permute-start.25
  144.4 1.4 collective-permute-start.16
  145.8 9.4 %collective-permute-done.19 = bf16[4,2,64,512]{3,2,1,0:T(8,128)(2,1)S(1)} collective-permute-done((bf16[4,2,64,512]{3,2,1,0:T(8,128)(2,1)S(1)}, bf16[4,2,64,512]{3,2,1,0:T(8,128)(2,1)S(1)}, u32[]{:S(2)}, u32[]{:S(2)}) %collective-permute-start.19) | collective-permute-done | bytes 524320 | tf_op jit(solution)/shard_map/ppermute | solution.py:25
  155.4 2.1 collective-permute-start.20
  157.5 9.0 %collective-permute-done.22 = bf16[4,2,64,512]{3,2,1,0:T(8,128)(2,1)S(1)} collective-permute-done((bf16[4,2,64,512]{3,2,1,0:T(8,128)(2,1)S(1)}, bf16[4,2,64,512]{3,2,1,0:T(8,128)(2,1)S(1)}, u32[]{:S(2)}, u32[]{:S(2)}) %collective-permute-start.22) | collective-permute-done | bytes 524320 | tf_op jit(solution)/shard_map/ppermute | solution.py:25
  166.6 2.1 collective-permute-start.23
  168.9 1.5 collective-permute-start.26
  170.5 2.8 %collective-permute-start.21 = (bf16[1,2,64,512]{3,2,1,0:T(8,128)(2,1)S(1)}, bf16[1,2,64,512]{3,2,1,0:T(8,128)(2,1)S(1)}, u32[]{:S(2)}, u32[]{:S(2)}) collective-permute-start(bf16[1,2,64,512]{3,2,1,0:T(8,128)(2,1)S(1)} %slice.232), channel_id=1, source_target_pairs={{0,4},{1,5},{2,6},{3,7},{4,0},{5,1},{6,2},{7,3},{8,12},{9,13},{10,... | collective-permute-start | bytes 393224 | tf_op jit(solution)/shard_map/ppermute | solution.py:25
  173.6 4.4 %collective-permute-start.24 = (bf16[1,2,64,512]{3,2,1,0:T(8,128)(2,1)S(1)}, bf16[1,2,64,512]{3,2,1,0:T(8,128)(2,1)S(1)}, u32[]{:S(2)}, u32[]{:S(2)}) collective-permute-start(bf16[1,2,64,512]{3,2,1,0:T(8,128)(2,1)S(1)} %slice.231), channel_id=1, source_target_pairs={{0,4},{1,5},{2,6},{3,7},{4,0},{5,1},{6,2},{7,3},{8,12},{9,13},{10,... | collective-permute-start | bytes 393224 | tf_op jit(solution)/shard_map/ppermute | solution.py:25
  177.9 6.8 %collective-permute-done.26 = bf16[2,2,64,512]{3,2,1,0:T(8,128)(2,1)S(1)} collective-permute-done((bf16[2,2,64,512]{3,2,1,0:T(8,128)(2,1)S(1)}, bf16[2,2,64,512]{3,2,1,0:T(8,128)(2,1)S(1)}, u32[]{:S(2)}, u32[]{:S(2)}) %collective-permute-start.26) | collective-permute-done | bytes 262176 | tf_op jit(solution)/shard_map/ppermute | solution.py:25
  184.8 3.0 %collective-permute-start.27 = (bf16[1,2,64,512]{3,2,1,0:T(8,128)(2,1)S(1)}, bf16[1,2,64,512]{3,2,1,0:T(8,128)(2,1)S(1)}, u32[]{:S(2)}, u32[]{:S(2)}) collective-permute-start(bf16[1,2,64,512]{3,2,1,0:T(8,128)(2,1)S(1)} %slice.230), channel_id=1, source_target_pairs={{0,4},{1,5},{2,6},{3,7},{4,0},{5,1},{6,2},{7,3},{8,12},{9,13},{10,... | collective-permute-start | bytes 393224 | tf_op jit(solution)/shard_map/ppermute | solution.py:25
  188.1 1.9 collective-permute-start.17
  190.1 7.6 %collective-permute-done.17 = bf16[2,3,64,512]{3,2,1,0:T(8,128)(2,1)S(1)} collective-permute-done((bf16[2,3,64,512]{3,2,1,0:T(8,128)(2,1)S(1)}, bf16[2,3,64,512]{3,2,1,0:T(8,128)(2,1)S(1)}, u32[]{:S(2)}, u32[]{:S(2)}) %collective-permute-start.17) | collective-permute-done | bytes 393248 | tf_op jit(solution)/shard_map/ppermute | solution.py:25
  197.9 0.4 collective-permute-start.18
  198.4 8.3 %collective-permute-done.18 = bf16[1,3,64,512]{3,2,1,0:T(8,128)(2,1)S(1)} collective-permute-done((bf16[1,3,64,512]{3,2,1,0:T(8,128)(2,1)S(1)}, bf16[1,3,64,512]{3,2,1,0:T(8,128)(2,1)S(1)}, u32[]{:S(2)}, u32[]{:S(2)}) %collective-permute-start.18) | collective-permute-done | bytes 196640 | tf_op jit(solution)/shard_map/ppermute | solution.py:25
  206.9 1.0 copy-done.7
  (80 shorter events, 2.4 us)
Async XLA Ops:
  0.0 4.3 %copy-start = (f32[1024,512]{1,0:T(8,128)S(1)}, f32[1024,512]{1,0:T(8,128)}, u32[]{:S(2)}) copy-start(f32[1024,512]{1,0:T(8,128)} %param.11) | copy-start | bytes 6291460
  0.0 12.9 %collective-permute-start = (s32[1,3,77]{2,1,0:T(4,128)}, s32[1,3,77]{2,1,0:T(4,128)S(1)}, u32[]{:S(2)}, u32[]{:S(2)}) collective-permute-start(s32[1,3,77]{2,1,0:T(4,128)} %bitcast.94), channel_id=1, source_target_pairs={{0,1},{1,0},{2,3},{3,2},{4,5},{5,4},{6,7},{7,6},{8,9},{9,8},{10,11... | collective-permute-start | bytes 2780 | tf_op jit(solution)/shard_map/ppermute | solution.py:25
  6.1 6.9 %copy-start.6 = (s32[3,77]{1,0:T(4,128)S(1)}, s32[3,77]{1,0:T(4,128)}, u32[]{:S(2)}) copy-start(s32[3,77]{1,0:T(4,128)} %param.8) | copy-start | bytes 2776
  6.1 16.8 %copy-start.4 = (bf16[1544,512]{1,0:T(8,128)(2,1)S(1)}, bf16[1544,512]{1,0:T(8,128)(2,1)}, u32[]{:S(2)}) copy-start(bf16[1544,512]{1,0:T(8,128)(2,1)} %param.10) | copy-start | bytes 4743172
  12.9 3.7 %collective-permute-start.1 = (s32[2,3,77]{2,1,0:T(4,128)S(1)}, s32[2,3,77]{2,1,0:T(4,128)S(1)}, u32[]{:S(2)}, u32[]{:S(2)}) collective-permute-start(s32[2,3,77]{2,1,0:T(4,128)S(1)} %pad_add_fusion.1), channel_id=1, source_target_pairs={{0,2},{1,3},{2,0},{3,1},{4,6},{5,7},{6,4},{7,5},{8,10},{9,11},{10,... | collective-permute-start | bytes 5552 | tf_op jit(solution)/shard_map/ppermute | solution.py:25
  16.6 4.5 %collective-permute-start.2 = (s32[4,3,77]{2,1,0:T(4,128)S(1)}, s32[4,3,77]{2,1,0:T(4,128)S(1)}, u32[]{:S(2)}, u32[]{:S(2)}) collective-permute-start(s32[4,3,77]{2,1,0:T(4,128)S(1)} %pad_add_fusion), channel_id=1, source_target_pairs={{0,4},{1,5},{2,6},{3,7},{4,0},{5,1},{6,2},{7,3},{8,12},{9,13},{10,... | collective-permute-start | bytes 11096 | tf_op jit(solution)/shard_map/ppermute | solution.py:25
  23.3 4.9 %collective-permute-start.3 = (f32[4,3,512]{2,1,0:T(4,128)S(1)}, f32[4,3,512]{2,1,0:T(4,128)S(1)}, u32[]{:S(2)}, u32[]{:S(2)}) collective-permute-start(f32[4,3,512]{2,1,0:T(4,128)S(1)} %slice.110), channel_id=1, source_target_pairs={{0,4},{1,5},{2,6},{3,7},{4,0},{5,1},{6,2},{7,3},{8,12},{9,13},{10,... | collective-permute-start | bytes 73736 | tf_op jit(solution)/shard_map/ppermute | solution.py:25
  28.2 3.8 %collective-permute-start.4 = (f32[2,3,512]{2,1,0:T(4,128)S(1)}, f32[2,3,512]{2,1,0:T(4,128)S(1)}, u32[]{:S(2)}, u32[]{:S(2)}) collective-permute-start(f32[2,3,512]{2,1,0:T(4,128)S(1)} %slice.145), channel_id=1, source_target_pairs={{0,2},{1,3},{2,0},{3,1},{4,6},{5,7},{6,4},{7,5},{8,10},{9,11},{10,... | collective-permute-start | bytes 36872 | tf_op jit(solution)/shard_map/ppermute | solution.py:25
  32.0 3.8 %copy-start.5 = (bf16[1,512,512]{2,1,0:T(8,128)(2,1)S(1)}, bf16[1,512,512]{2,1,0:T(8,128)(2,1)}, u32[]{:S(2)}) copy-start(bf16[1,512,512]{2,1,0:T(8,128)(2,1)} %param.13) | copy-start | bytes 1572868
  32.0 3.8 %collective-permute-start.5 = (f32[1,3,512]{2,1,0:T(4,128)S(1)}, f32[1,3,512]{2,1,0:T(4,128)S(1)}, u32[]{:S(2)}, u32[]{:S(2)}) collective-permute-start(f32[1,3,512]{2,1,0:T(4,128)S(1)} %slice.147), channel_id=1, source_target_pairs={{0,1},{1,0},{2,3},{3,2},{4,5},{5,4},{6,7},{7,6},{8,9},{9,8},{10,11... | collective-permute-start | bytes 18440 | tf_op jit(solution)/shard_map/ppermute | solution.py:25
  35.8 1.3 copy-start.3
  37.1 2.3 %copy-start.2 = (bf16[9,512,512]{2,1,0:T(8,128)(2,1)S(1)}, bf16[9,512,512]{2,1,0:T(8,128)(2,1)}, u32[]{:S(2)}) copy-start(bf16[9,512,512]{2,1,0:T(8,128)(2,1)} %copy.33) | copy-start | bytes 14155780
  42.3 2.4 %collective-permute-start.6 = (bf16[256,512]{1,0:T(8,128)(2,1)S(1)}, bf16[256,512]{1,0:T(8,128)(2,1)S(1)}, u32[]{:S(2)}, u32[]{:S(2)}) collective-permute-start(bf16[256,512]{1,0:T(8,128)(2,1)S(1)} %get-tuple-element.58), channel_id=1, source_target_pairs={{0,8},{1,9},{2,10},{3,11},{4,12},{5,13},{6,14},{7,15}} | collective-permute-start | bytes 786440 | tf_op jit(solution)/shard_map/ppermute | solution.py:332
  47.6 3.4 %collective-permute-start.7 = (bf16[256,512]{1,0:T(8,128)(2,1)S(1)}, bf16[256,512]{1,0:T(8,128)(2,1)S(1)}, u32[]{:S(2)}, u32[]{:S(2)}) collective-permute-start(bf16[256,512]{1,0:T(8,128)(2,1)S(1)} %get-tuple-element.61), channel_id=1, source_target_pairs={{0,8},{8,16},{1,9},{9,17},{2,10},{10,18},{3,11},{11,19},{4,12},{12... | collective-permute-start | bytes 786440 | tf_op jit(solution)/shard_map/ppermute | solution.py:332
  53.8 5.2 %collective-permute-start.8 = (bf16[256,512]{1,0:T(8,128)(2,1)S(1)}, bf16[256,512]{1,0:T(8,128)(2,1)S(1)}, u32[]{:S(2)}, u32[]{:S(2)}) collective-permute-start(bf16[256,512]{1,0:T(8,128)(2,1)S(1)} %get-tuple-element.64), channel_id=1, source_target_pairs={{0,8},{8,16},{16,24},{1,9},{9,17},{17,25},{2,10},{10,18},{18,26},{... | collective-permute-start | bytes 786440 | tf_op jit(solution)/shard_map/ppermute | solution.py:332
  59.1 0.7 collective-permute-start.9
  59.8 0.7 collective-permute-start.10
  60.5 2.3 %slice-start = ((s8[4718592]{0:T(1024)(128)(4,1)}), s8[4194304]{0:T(1024)(128)(4,1)S(1)}, s32[]{:S(2)}) async-start(s8[4718592]{0:T(1024)(128)(4,1)} %bitcast.62), calls=%async_computation | async-start | bytes 8388608
  60.6 2.4 %slice-start.1 = ((s8[4718592]{0:T(1024)(128)(4,1)}), s8[524288]{0:T(1024)(128)(4,1)S(1)}, s32[]{:S(2)}) async-start(s8[4718592]{0:T(1024)(128)(4,1)} %bitcast.62), calls=%async_computation.1 | async-start | bytes 1048576
  63.0 0.7 collective-permute-start.11
  63.7 0.7 collective-permute-start.12
  64.5 41.0 %collective-permute-start.13 = (bf16[256,512]{1,0:T(8,128)(2,1)S(1)}, bf16[256,512]{1,0:T(8,128)(2,1)S(1)}, u32[]{:S(2)}, u32[]{:S(2)}) collective-permute-start(bf16[256,512]{1,0:T(8,128)(2,1)S(1)} %get-tuple-element.83), channel_id=1, source_target_pairs={{8,0},{16,8},{24,16},{9,1},{17,9},{25,17},{10,2},{18,10},{26,18},{... | collective-permute-start | bytes 786440 | tf_op jit(solution)/shard_map/ppermute | solution.py:351
  108.9 7.7 %collective-permute-start.14 = (bf16[256,512]{1,0:T(8,128)(2,1)S(1)}, bf16[256,512]{1,0:T(8,128)(2,1)S(1)}, u32[]{:S(2)}, u32[]{:S(2)}) collective-permute-start(bf16[256,512]{1,0:T(8,128)(2,1)S(1)} %get-tuple-element.86), channel_id=1, source_target_pairs={{8,0},{16,8},{9,1},{17,9},{10,2},{18,10},{11,3},{19,11},{12,4},{20... | collective-permute-start | bytes 786440 | tf_op jit(solution)/shard_map/ppermute | solution.py:351
  119.9 7.1 %collective-permute-start.15 = (bf16[256,512]{1,0:T(8,128)(2,1)S(1)}, bf16[256,512]{1,0:T(8,128)(2,1)S(1)}, u32[]{:S(2)}, u32[]{:S(2)}) collective-permute-start(bf16[256,512]{1,0:T(8,128)(2,1)S(1)} %get-tuple-element.89), channel_id=1, source_target_pairs={{8,0},{9,1},{10,2},{11,3},{12,4},{13,5},{14,6},{15,7}} | collective-permute-start | bytes 786440 | tf_op jit(solution)/shard_map/ppermute | solution.py:351
  140.3 14.9 %collective-permute-start.19 = (bf16[4,2,64,512]{3,2,1,0:T(8,128)(2,1)S(1)}, bf16[4,2,64,512]{3,2,1,0:T(8,128)(2,1)S(1)}, u32[]{:S(2)}, u32[]{:S(2)}) collective-permute-start(bf16[4,2,64,512]{3,2,1,0:T(8,128)(2,1)S(1)} %get-tuple-element.98), channel_id=1, source_target_pairs={{0,1},{1,0},{2,3},{3,2},{4,5},{5,4},{6,7},{7,6},{8,9},{9,8},{10,11... | collective-permute-start | bytes 1572872 | tf_op jit(solution)/shard_map/ppermute | solution.py:25
  142.1 24.3 %collective-permute-start.22 = (bf16[4,2,64,512]{3,2,1,0:T(8,128)(2,1)S(1)}, bf16[4,2,64,512]{3,2,1,0:T(8,128)(2,1)S(1)}, u32[]{:S(2)}, u32[]{:S(2)}) collective-permute-start(bf16[4,2,64,512]{3,2,1,0:T(8,128)(2,1)S(1)} %get-tuple-element.100), channel_id=1, source_target_pairs={{0,1},{1,0},{2,3},{3,2},{4,5},{5,4},{6,7},{7,6},{8,9},{9,8},{10,11... | collective-permute-start | bytes 1572872 | tf_op jit(solution)/shard_map/ppermute | solution.py:25
  142.4 26.3 %collective-permute-start.25 = (bf16[4,2,64,512]{3,2,1,0:T(8,128)(2,1)S(1)}, bf16[4,2,64,512]{3,2,1,0:T(8,128)(2,1)S(1)}, u32[]{:S(2)}, u32[]{:S(2)}) collective-permute-start(bf16[4,2,64,512]{3,2,1,0:T(8,128)(2,1)S(1)} %get-tuple-element.102), channel_id=1, source_target_pairs={{0,2},{1,3},{2,0},{3,1},{4,6},{5,7},{6,4},{7,5},{8,10},{9,11},{10,... | collective-permute-start | bytes 1572872 | tf_op jit(solution)/shard_map/ppermute | solution.py:25
  144.4 43.4 %collective-permute-start.16 = (bf16[4,3,64,512]{3,2,1,0:T(8,128)(2,1)S(1)}, bf16[4,3,64,512]{3,2,1,0:T(8,128)(2,1)S(1)}, u32[]{:S(2)}, u32[]{:S(2)}) collective-permute-start(bf16[4,3,64,512]{3,2,1,0:T(8,128)(2,1)S(1)} %get-tuple-element.96), channel_id=1, source_target_pairs={{0,1},{1,0},{2,3},{3,2},{4,5},{5,4},{6,7},{7,6},{8,9},{9,8},{10,11... | collective-permute-start | bytes 2359304 | tf_op jit(solution)/shard_map/ppermute | solution.py:25
  155.4 15.0 %collective-permute-start.20 = (bf16[2,2,64,512]{3,2,1,0:T(8,128)(2,1)S(1)}, bf16[2,2,64,512]{3,2,1,0:T(8,128)(2,1)S(1)}, u32[]{:S(2)}, u32[]{:S(2)}) collective-permute-start(bf16[2,2,64,512]{3,2,1,0:T(8,128)(2,1)S(1)} %slice.228), channel_id=1, source_target_pairs={{0,2},{1,3},{2,0},{3,1},{4,6},{5,7},{6,4},{7,5},{8,10},{9,11},{10,... | collective-permute-start | bytes 786440 | tf_op jit(solution)/shard_map/ppermute | solution.py:25
  166.6 6.8 %collective-permute-start.23 = (bf16[2,2,64,512]{3,2,1,0:T(8,128)(2,1)S(1)}, bf16[2,2,64,512]{3,2,1,0:T(8,128)(2,1)S(1)}, u32[]{:S(2)}, u32[]{:S(2)}) collective-permute-start(bf16[2,2,64,512]{3,2,1,0:T(8,128)(2,1)S(1)} %slice.227), channel_id=1, source_target_pairs={{0,2},{1,3},{2,0},{3,1},{4,6},{5,7},{6,4},{7,5},{8,10},{9,11},{10,... | collective-permute-start | bytes 786440 | tf_op jit(solution)/shard_map/ppermute | solution.py:25
  168.9 15.8 %collective-permute-start.26 = (bf16[2,2,64,512]{3,2,1,0:T(8,128)(2,1)S(1)}, bf16[2,2,64,512]{3,2,1,0:T(8,128)(2,1)S(1)}, u32[]{:S(2)}, u32[]{:S(2)}) collective-permute-start(bf16[2,2,64,512]{3,2,1,0:T(8,128)(2,1)S(1)} %slice.226), channel_id=1, source_target_pairs={{0,1},{1,0},{2,3},{3,2},{4,5},{5,4},{6,7},{7,6},{8,9},{9,8},{10,11... | collective-permute-start | bytes 786440 | tf_op jit(solution)/shard_map/ppermute | solution.py:25
  170.5 19.5 %collective-permute-start.21 = (bf16[1,2,64,512]{3,2,1,0:T(8,128)(2,1)S(1)}, bf16[1,2,64,512]{3,2,1,0:T(8,128)(2,1)S(1)}, u32[]{:S(2)}, u32[]{:S(2)}) collective-permute-start(bf16[1,2,64,512]{3,2,1,0:T(8,128)(2,1)S(1)} %slice.232), channel_id=1, source_target_pairs={{0,4},{1,5},{2,6},{3,7},{4,0},{5,1},{6,2},{7,3},{8,12},{9,13},{10,... | collective-permute-start | bytes 393224 | tf_op jit(solution)/shard_map/ppermute | solution.py:25
  173.6 16.5 %collective-permute-start.24 = (bf16[1,2,64,512]{3,2,1,0:T(8,128)(2,1)S(1)}, bf16[1,2,64,512]{3,2,1,0:T(8,128)(2,1)S(1)}, u32[]{:S(2)}, u32[]{:S(2)}) collective-permute-start(bf16[1,2,64,512]{3,2,1,0:T(8,128)(2,1)S(1)} %slice.231), channel_id=1, source_target_pairs={{0,4},{1,5},{2,6},{3,7},{4,0},{5,1},{6,2},{7,3},{8,12},{9,13},{10,... | collective-permute-start | bytes 393224 | tf_op jit(solution)/shard_map/ppermute | solution.py:25
  184.8 13.5 %collective-permute-start.27 = (bf16[1,2,64,512]{3,2,1,0:T(8,128)(2,1)S(1)}, bf16[1,2,64,512]{3,2,1,0:T(8,128)(2,1)S(1)}, u32[]{:S(2)}, u32[]{:S(2)}) collective-permute-start(bf16[1,2,64,512]{3,2,1,0:T(8,128)(2,1)S(1)} %slice.230), channel_id=1, source_target_pairs={{0,4},{1,5},{2,6},{3,7},{4,0},{5,1},{6,2},{7,3},{8,12},{9,13},{10,... | collective-permute-start | bytes 393224 | tf_op jit(solution)/shard_map/ppermute | solution.py:25
  188.1 9.6 %collective-permute-start.17 = (bf16[2,3,64,512]{3,2,1,0:T(8,128)(2,1)S(1)}, bf16[2,3,64,512]{3,2,1,0:T(8,128)(2,1)S(1)}, u32[]{:S(2)}, u32[]{:S(2)}) collective-permute-start(bf16[2,3,64,512]{3,2,1,0:T(8,128)(2,1)S(1)} %slice.225), channel_id=1, source_target_pairs={{0,2},{1,3},{2,0},{3,1},{4,6},{5,7},{6,4},{7,5},{8,10},{9,11},{10,... | collective-permute-start | bytes 1179656 | tf_op jit(solution)/shard_map/ppermute | solution.py:25
  197.9 8.7 %collective-permute-start.18 = (bf16[1,3,64,512]{3,2,1,0:T(8,128)(2,1)S(1)}, bf16[1,3,64,512]{3,2,1,0:T(8,128)(2,1)S(1)}, u32[]{:S(2)}, u32[]{:S(2)}) collective-permute-start(bf16[1,3,64,512]{3,2,1,0:T(8,128)(2,1)S(1)} %slice.229), channel_id=1, source_target_pairs={{0,4},{1,5},{2,6},{3,7},{4,0},{5,1},{6,2},{7,3},{8,12},{9,13},{10,... | collective-permute-start | bytes 589832 | tf_op jit(solution)/shard_map/ppermute | solution.py:25
  198.3 9.6 %copy-start.1 = (f32[1024,512]{1,0:T(8,128)S(1)}, f32[1024,512]{1,0:T(8,128)}, u32[]{:S(2)}) copy-start(f32[1024,512]{1,0:T(8,128)} %param.11) | copy-start | bytes 6291460
  206.9 1.0 copy-start.7

commit v3 on v2

v3 whole, which is shorter than its diff:
```python
import functools
import math

import jax
import jax.numpy as jnp
from jax import lax
from jax.experimental import pallas as pl
from jax.experimental.pallas import tpu as pltpu
from jax.sharding import PartitionSpec as P


TXT_LEN = 77
RES = 16
F32 = jnp.float32
BF16 = jnp.bfloat16
VMEM = pltpu.VMEM
LIMIT = 40 * 1024 * 1024
SLOTS = 60


def params():
    return pltpu.CompilerParams(vmem_limit_bytes=LIMIT)


def swap(x, bit, count):
    return lax.ppermute(x, "dp", [(i, i ^ bit) for i in range(count)])


def column_masks(rows, side):
    column = lax.broadcasted_iota(jnp.int32, (rows, 1), 0) % side
    return column != 0, column != side - 1


def put_shifts(pieces, value, side, at, rows):
    not_first, not_last = column_masks(rows, side)
    left = jnp.where(not_first, pltpu.roll(value, 1, 0), 0.0)
    right = jnp.where(not_last, pltpu.roll(value, rows - 1, 0), 0.0)
    for index, shifted in enumerate((left, value, right)):
        pieces[index, pl.ds(at, rows), :] = shifted.astype(BF16)


def blank_edges(pieces, rows, pad):
    blank = jnp.zeros((pad, pieces.shape[2]), BF16)
    for index in range(3):
        pieces[index, pl.ds(0, pad), :] = blank
        pieces[index, pl.ds(pad + rows, pad), :] = blank


def conv_of(pieces, weight, sign, side, rows):
    channels = pieces.shape[2]
    total = None
    for tap in range(9):
        down, across = sign * (tap // 3 - 1), sign * (tap % 3 - 1)
        term = lax.dot_general(
            pieces[across + 1, pl.ds(side + down * side, rows), :],
            weight[pl.ds(tap * channels, channels), :],
            (((1,), ((1 if sign > 0 else 0),)), ((), ())),
            preferred_element_type=F32,
        )
        total = term if total is None else total + term
    return total


def forward_kernel(tick, side, micro, *refs):
    if tick:
        received, start, pack, head, weight = refs[:5]
        refs = refs[7:]
    else:
        start, pack, head, weight = refs[:4]
        received = start
        refs = refs[4:]
    out, kept_in, kept_conv, score, pieces, mod_box, conv_box, sems = refs
    rows = start.shape[0]
    section = lax.axis_index("section")
    position = tick - section

    @pl.when((position >= 0) & (position < micro))
    def _():
        blank_edges(pieces, rows, side)
        style = pack[pl.ds(position, 1), :]
        source = received[...]
        if tick:
            source = jnp.where(section == 0, start[...].astype(F32), source.astype(F32))
        mod = (style * source.astype(F32)).astype(BF16)
        mod_box[pl.ds(0, side)] = mod.reshape(side, side, mod.shape[1])
        squared = style * style
        high = squared.astype(BF16).astype(F32)
        row = lax.broadcasted_iota(jnp.int32, (side, mod.shape[1]), 0)
        mod_box[side] = jnp.where(row == 0, high, jnp.where(row == 1, squared - high, 0.0)).astype(BF16)
        first = pltpu.make_async_copy(mod_box, kept_in.at[:, position], sems.at[0])
        first.start()
        put_shifts(pieces, mod.astype(F32), side, side, rows)
        conv = conv_of(pieces, weight, 1, side, rows)
        conv_box[...] = conv
        second = pltpu.make_async_copy(conv_box, kept_conv.at[position], sems.at[1])
        second.start()
        pre = pack[pl.ds(8 + position, 1), :] * conv
        result = (pre / (1.0 + jnp.exp(-pre))).astype(BF16)
        out[...] = result
        sums = jnp.sum(result.astype(F32), axis=0, keepdims=True) * head[...]
        score[...] = jnp.broadcast_to(jnp.sum(sums, axis=1, keepdims=True), score.shape)
        first.wait()
        second.wait()


def backward_kernel(tick, side, micro, norm_div, *refs):
    if tick:
        received = refs[0]
        refs = refs[1:]
    head, pack = refs[:2]
    scores, refs = refs[2 : 2 + micro], refs[2 + micro :]
    kept_conv, weight = refs[:2]
    refs = refs[3:] if tick else refs[2:]
    out, kept_grad, pieces, conv_box, grad_box, sems = refs
    rows = conv_box.shape[0]
    section = lax.axis_index("section")
    sections = lax.axis_size("section")
    gen_count = sections - sections // 4
    position = tick - (sections - 1 - section)

    @pl.when((position >= 0) & (position < micro))
    def _():
        load = pltpu.make_async_copy(kept_conv.at[position], conv_box, sems.at[0])
        load.start()
        blank_edges(pieces, rows, side)
        raw = scores[0][...]
        for index in range(1, micro):
            raw = jnp.where(position == index, scores[index][...], raw)
        raw = raw[:1, :1] / norm_div
        d_factor = (1.0 / (1.0 + jnp.exp(-raw))).astype(BF16).astype(F32)
        g_factor = (-1.0 / (1.0 + jnp.exp(raw))).astype(BF16).astype(F32)
        scale = jnp.where(section < gen_count, jnp.ones_like(raw), d_factor)
        boost = jnp.where(section == gen_count, g_factor, jnp.ones_like(raw))
        demod = pack[pl.ds(8 + position, 1), :]
        unit = (head[...] / norm_div).astype(BF16).astype(F32)
        incoming = jnp.broadcast_to(unit, conv_box.shape)
        if tick:
            incoming = jnp.where(section == sections - 1, incoming, received[...].astype(F32))
        load.wait()
        conv = conv_box[...]
        pre = demod * conv
        sigma = 1.0 / (1.0 + jnp.exp(-pre))
        grad_pre = incoming * sigma * (1.0 + pre * (1.0 - sigma))
        grad_conv = demod * grad_pre
        channels = conv.shape[1]
        grad_box[pl.ds(0, side)] = (scale * grad_conv).astype(BF16).reshape(side, side, channels)
        term = jnp.sum(grad_pre * conv, axis=0, keepdims=True) * demod * demod * demod
        term = jnp.where(section < gen_count, term, 0.0)
        high = term.astype(BF16).astype(F32)
        row = lax.broadcasted_iota(jnp.int32, (side, channels), 0)
        grad_box[side] = jnp.where(row == 0, high, jnp.where(row == 1, term - high, 0.0)).astype(BF16)
        first = pltpu.make_async_copy(grad_box, kept_grad.at[:, position], sems.at[1])
        first.start()
        put_shifts(pieces, grad_conv.astype(BF16).astype(F32), side, side, rows)
        back = conv_of(pieces, weight, -1, side, rows)
        out[...] = (pack[pl.ds(position, 1), :] * boost * back).astype(BF16)
        first.wait()


GROUP_BITS = 2
GROUP = 1 << GROUP_BITS


def pack_kernel(micro, side, count, kept_grad, *rest):
    outs, turned = rest[:GROUP], rest[GROUP]
    channels = kept_grad.shape[3]
    rows = side * micro * side
    part = channels // count
    here = lax.axis_index("dp")
    extra = micro * side
    stacked = kept_grad[...].reshape(rows + extra, channels).astype(F32)
    stacked = jnp.concatenate([stacked, jnp.zeros((128 - extra, channels), F32)], axis=0)
    turned[...] = jnp.transpose(stacked).astype(BF16)
    for flip in range(GROUP):
        for slot in range(count // GROUP):
            source = pl.multiple_of((here ^ flip ^ (slot << GROUP_BITS)) * part, part)
            outs[flip][pl.ds(slot * part, part), :] = turned[pl.ds(source, part), :]


def weight_grad_kernel(micro, side, count, chunks, *refs):
    grads, mods, weight = refs[:GROUP], refs[GROUP : 2 * GROUP], refs[2 * GROUP]
    refs = refs[2 * GROUP + 1 :]
    outs, (pieces, mixture) = refs[: 2 * len(chunks)], refs[2 * len(chunks) :]
    channels = weight.shape[1]
    rows = side * micro * side
    band = micro * side
    tall = rows + 2 * band
    part = channels // count
    here = lax.axis_index("dp")
    blank = jnp.zeros((band, channels), BF16)
    for member in range(GROUP):
        base = member * tall
        for index in range(3):
            pieces[index, pl.ds(base, band), :] = blank
            pieces[index, pl.ds(base + band + rows, band), :] = blank
        value = mods[member][pl.ds(0, side)].reshape(rows, channels)
        put_shifts(pieces, value.astype(F32), side, base + band, rows)
        terms = grads[member][:, pl.ds(rows, 128)].astype(F32)
        squares = mods[member][side].reshape(band, channels).astype(F32)
        left = lax.broadcasted_iota(jnp.int32, (128, 128), 0)
        right = lax.broadcasted_iota(jnp.int32, (128, 128), 1)
        join = ((left // side == right) & (left % side < 2) & (right < micro)).astype(F32)
        terms = jnp.dot(terms, join, preferred_element_type=F32, precision=lax.Precision.HIGHEST)
        joined = lax.broadcasted_iota(jnp.int32, (8, band), 0) == lax.broadcasted_iota(
            jnp.int32, (8, band), 1
        ) // side
        squares = jnp.dot(joined.astype(F32), squares, preferred_element_type=F32, precision=lax.Precision.HIGHEST)
        term = jnp.dot(
            terms[:, :8], squares, preferred_element_type=F32, precision=lax.Precision.HIGHEST
        )
        if member:
            mixture[...] += term
        else:
            mixture[...] = term
    slots = count // GROUP
    for chunk, taps in enumerate(chunks):
        keep, send = outs[2 * chunk], outs[2 * chunk + 1]
        for spot, tap in enumerate(taps):
            total = None
            for member in range(GROUP):
                begin = member * tall + (tap // 3) * band
                term = jnp.dot(
                    grads[member][:, pl.ds(0, rows)], pieces[tap % 3, pl.ds(begin, rows), :],
                    preferred_element_type=F32,
                )
                total = term if total is None else total + term
            for slot in range(slots):
                source = pl.multiple_of((here ^ (slot << GROUP_BITS)) * part, part)
                fixed = total[slot * part : (slot + 1) * part] - weight[
                    pl.ds(tap * channels + source, part), :
                ].astype(F32) * mixture[pl.ds(slot * part, part), :]
                if slot < slots // 2:
                    keep[slot, spot] = fixed
                else:
                    send[slot - slots // 2, spot] = fixed.astype(BF16)


def on_device(
    text_ids, seed_ids, text_table, latent_table, start_map, style_weight, conv_weight, score_head
):
    sections = lax.axis_size("section")
    count = lax.axis_size("dp")
    bits = count.bit_length() - 1
    gen_count = sections - sections // 4
    section_at = lax.axis_index("section")
    here = lax.axis_index("dp")
    is_gen = section_at < gen_count
    micro = seed_ids.shape[0]
    channels, pixels = start_map.shape
    side = RES
    vocab_rows = text_table.shape[0]
    norm_div = pixels * math.sqrt(channels)

    ids = text_ids[None]
    weight = conv_weight[0]
    weight_out = jnp.transpose(weight, (1, 0, 2))
    flat_out = weight_out.reshape(9 * channels, channels)
    squares = jnp.sum(jnp.square(weight_out.astype(F32)), axis=0)
    first_map = start_map.T
    latent = jnp.take(latent_table, seed_ids, axis=0)
    for stage in range(bits):
        other = swap(ids, 1 << stage, count)
        if stage == 0:
            other, squares, first_map, latent = lax.optimization_barrier(
                (other, squares, first_map, latent)
            )
        ids = jnp.concatenate([ids, other], axis=0)
    wanted = ids.reshape(count * micro, TXT_LEN) - here * vocab_rows
    rows = lax.broadcasted_iota(jnp.int32, (1, 1, vocab_rows), 2)
    hits = jnp.sum((wanted[:, :, None] == rows).astype(F32), axis=1)
    sums = jnp.dot(hits.astype(BF16), text_table, preferred_element_type=F32)
    sums = sums.reshape(count, micro, channels)
    for stage in reversed(range(bits)):
        half = 1 << stage
        sums = sums[:half] + swap(sums[half:], half, count)
    text_mean = sums[0] / TXT_LEN

    code_now = jnp.where(is_gen, latent + text_mean, text_mean).astype(BF16)
    styles = 1.0 + lax.dot_general(
        code_now, style_weight[0], (((1,), (1,)), ((), ())), preferred_element_type=F32
    )
    demods = lax.rsqrt(
        lax.dot_general(
            styles * styles, squares, (((1,), (1,)), ((), ())), precision=lax.Precision.HIGHEST
        )
        + 1e-08
    )
    demods = jnp.where(is_gen, demods, jnp.ones_like(demods))
    rest = ((0, 8 - micro), (0, 0))
    pack = jnp.concatenate([jnp.pad(styles, rest), jnp.pad(demods, rest)], axis=0)
    head = score_head[None]
    ticks = micro + sections - 1

    whole = pl.BlockSpec(memory_space=VMEM)
    far = pl.BlockSpec(memory_space=pltpu.HBM)
    flops = 2 * 9 * channels * channels * pixels
    conv_cost = pl.CostEstimate(
        flops=flops, bytes_accessed=9 * channels * channels * 2 + 5 * channels * pixels * 2,
        transcendentals=channels * pixels,
    )
    tall = 2 * side + pixels
    conv_scratch = [VMEM((3, tall, channels), BF16)]
    plain = jax.ShapeDtypeStruct((pixels, channels), BF16)
    lined = jax.ShapeDtypeStruct((side + 1, micro, side, channels), BF16)
    tower = jax.ShapeDtypeStruct((SLOTS, pixels, channels), F32)

    def forward(tick, arrays):
        return pl.pallas_call(
            functools.partial(forward_kernel, tick, side, micro),
            in_specs=[whole] * 5 + [far] * 2 if tick else [whole] * 4,
            out_specs=[whole, far, far, whole],
            out_shape=[plain, lined, tower, jax.ShapeDtypeStruct((8, 128), F32)],
            scratch_shapes=conv_scratch
            + [
                VMEM((side + 1, side, channels), BF16),
                VMEM((pixels, channels), F32),
                pltpu.SemaphoreType.DMA((2,)),
            ],
            input_output_aliases={5: 1, 6: 2} if tick else {},
            cost_estimate=conv_cost,
            compiler_params=params(),
            name="forward_conv",
        )(*arrays)

    def backward(tick, arrays):
        fixed = 3 + micro if tick else 2 + micro
        return pl.pallas_call(
            functools.partial(backward_kernel, tick, side, micro, norm_div),
            in_specs=[whole] * fixed + [far, whole] + [far] * (1 if tick else 0),
            out_specs=[whole, far],
            out_shape=[plain, lined],
            scratch_shapes=conv_scratch
            + [
                VMEM((pixels, channels), F32),
                VMEM((side + 1, side, channels), BF16),
                pltpu.SemaphoreType.DMA((2,)),
            ],
            input_output_aliases={fixed + 2: 1} if tick else {},
            cost_estimate=conv_cost,
            compiler_params=params(),
            name="backward_conv",
        )(*arrays)

    scores = []
    kept_in = kept_conv = outgoing = None
    for tick in range(ticks):
        if tick:
            received = lax.ppermute(
                outgoing, "section", [(i, i + 1) for i in range(sections - 1) if 0 <= tick - 1 - i < micro]
            )
            arrays = (received, first_map, pack, head, flat_out, kept_in, kept_conv)
        else:
            arrays = (first_map, pack, head, flat_out)
        outgoing, kept_in, kept_conv, score = forward(tick, arrays)
        scores.append(score)
    scores = scores[sections - 1 :]
    for hop in range(sections - gen_count - 1):
        target = sections - 2 - hop
        passed = lax.ppermute(scores, "section", [(target + 1, target)])
        scores = [jnp.where(section_at == target, new, old) for new, old in zip(passed, scores)]

    mods = [kept_in]
    for flip in range(1, GROUP):
        mods.append(swap(kept_in, flip, count))
    kept_grad = outgoing = None
    for tick in range(ticks):
        arrays = (head, pack, *scores, kept_conv, flat_out)
        if tick:
            received = lax.ppermute(
                outgoing, "section",
                [(i, i - 1) for i in range(1, sections) if 0 <= tick - 1 - (sections - 1 - i) < micro],
            )
            arrays = (received, *arrays, kept_grad)
        outgoing, kept_grad = backward(tick, arrays)

    part = channels // count
    own = channels // GROUP
    chunks = ((0, 1, 2), (3, 4, 5), (6, 7, 8))
    wide = micro * pixels + 128
    packed = pl.pallas_call(
        functools.partial(pack_kernel, micro, side, count),
        in_specs=[whole],
        out_specs=[whole] * GROUP,
        out_shape=[jax.ShapeDtypeStruct((own, wide), BF16)] * GROUP,
        scratch_shapes=[VMEM((channels, wide), BF16)],
        cost_estimate=pl.CostEstimate(flops=0, bytes_accessed=4 * micro * pixels * channels, transcendentals=0),
        compiler_params=params(),
        name="pack_grad",
    )(kept_grad)
    grads = [packed[0]] + [swap(packed[flip], flip, count) for flip in range(1, GROUP)]
    slots = count // GROUP
    shapes = []
    for taps in chunks:
        shapes += [
            jax.ShapeDtypeStruct((slots // 2, len(taps), part, channels), F32),
            jax.ShapeDtypeStruct((slots // 2, len(taps), part, channels), BF16),
        ]
    pairs = pl.pallas_call(
        functools.partial(weight_grad_kernel, micro, side, count, chunks),
        in_specs=[whole] * (2 * GROUP + 1),
        out_specs=[whole] * len(shapes),
        out_shape=shapes,
        scratch_shapes=[VMEM((3, GROUP * micro * tall, channels), BF16), VMEM((own, channels), F32)],
        cost_estimate=pl.CostEstimate(flops=micro * flops, bytes_accessed=20 * 1024 * 1024, transcendentals=0),
        compiler_params=params(),
        name="weight_grad",
    )(*grads, *mods, flat_out)
    done = [None] * 9
    for chunk, taps in enumerate(chunks):
        keep, send = pairs[2 * chunk], pairs[2 * chunk + 1]
        half = slots // 2
        while True:
            total = keep + swap(send, half << GROUP_BITS, count).astype(F32)
            half //= 2
            if not half:
                break
            keep = total[:half]
            send = total[half:].astype(BF16)
        for spot, tap in enumerate(taps):
            done[tap] = total[0, spot]
    return jnp.stack(done, axis=1)[None]


def solution(mesh):
    placed = (
        P("dp", None),
        P("dp"),
        P("dp", None),
        P(),
        P(),
        P("section", None, None),
        P("section", None, None, None),
        P(),
    )
    return jax.shard_map(
        on_device,
        mesh=mesh,
        in_specs=placed,
        out_specs=P("section", "dp", None, None),
        check_vma=False,
    )
```

time: 209 us -> 184 us (0.88)
  the two profiles are of different devices: /device:TPU:0 before, /device:TPU:27 now
where the time goes in v3:
time: 184 us
  waiting for transfers between devices  118 us (64%)
  Pallas kernels  26.4 us (14%)
  starting transfers between devices  22.6 us (12%)
  other arithmetic  6.59 us (4%)
  local copies, waits for them, and re-layouts  5.29 us (3%)
  matrix products  4 us (2%)
    ppermute x15, waiting for transfers between devices, swap(): return lax.ppermute(x, 'dp', [(i, i ^ bit) for i in range(count)])  80 us
    ppermute x5, waiting for transfers between devices, on_device(): lax.ppermute(outgoing, 'section', [(i, i + 1) for i in range(sections - 1...  35.2 us
    pallas_call x6, Pallas kernels, forward(): pl.pallas_call(functools.partial(forward_kernel, tick, side, micro), in_s...  9.88 us
    pallas_call x6, Pallas kernels, backward(): pl.pallas_call(functools.partial(backward_kernel, tick, side, micro, norm...  9.7 us
    ppermute x5, starting transfers between devices, on_device(): lax.ppermute(outgoing, 'section', [(i, i - 1) for i in range(1, sections)...  9.6 us
    ppermute x15, starting transfers between devices, swap(): return lax.ppermute(x, 'dp', [(i, i ^ bit) for i in range(count)])  7.78 us
    pallas_call x1, Pallas kernels, on_device(): pl.pallas_call(functools.partial(weight_grad_kernel, micro, side, count,...  6.48 us
    ppermute x5, starting transfers between devices, on_device(): lax.ppermute(outgoing, 'section', [(i, i + 1) for i in range(sections - 1...  5.23 us
  transfers between devices with their start and end apart: 25, of which 19 were waited for; matrix products, arithmetic and copies ran while one was open for 4% of the time, Pallas kernels for 1%

profile of v3, /device:TPU:27, one launch (start us, length us, event | category | flops | bytes accessed | tf_op | source)
XLA Modules:
  0.0 183.9 jit_solution(9504533270956829208)
XLA Ops:
  0.0 1.2 collective-permute-start
  1.2 0.7 compare_and_fusion
  1.9 0.7 compare_select_fusion
  2.6 3.4 %multiply_reduce_fusion = f32[512,512]{1,0:T(8,128)S(1)} fusion(bf16[1,512,9,512]{3,1,2,0:T(8,128)(2,1)} %param.14), kind=kLoop, calls=%fused_computation.3 | loop fusion | flops 6815744 | bytes 5767168 | tf_op jit(solution)/shard_map/reduce_sum | solution.py:258
  6.0 0.6 gather_fusion
  6.6 1.1 copy.26
  7.7 0.2 collective-permute-start.1
  8.0 2.3 %collective-permute-done.1 = s32[2,3,77]{2,1,0:T(4,128)S(1)} collective-permute-done((s32[2,3,77]{2,1,0:T(4,128)S(1)}, s32[2,3,77]{2,1,0:T(4,128)S(1)}, u32[]{:S(2)}, u32[]{:S(2)}) %collective-permute-start.1) | collective-permute-done | bytes 1880 | tf_op jit(solution)/shard_map/ppermute | solution.py:26
  10.3 3.3 %collective-permute-done.2 = s32[4,3,77]{2,1,0:T(4,128)S(1)} collective-permute-done((s32[4,3,77]{2,1,0:T(4,128)S(1)}, s32[4,3,77]{2,1,0:T(4,128)S(1)}, u32[]{:S(2)}, u32[]{:S(2)}) %collective-permute-start.2) | collective-permute-done | bytes 3728 | tf_op jit(solution)/shard_map/ppermute | solution.py:26
  13.7 0.1 copy.27
  13.8 1.6 convert_reduce_fusion
  15.4 1.7 fusion.23
  17.2 0.1 collective-permute-start.3
  17.3 3.8 %collective-permute-done.3 = f32[4,3,512]{2,1,0:T(4,128)S(1)} collective-permute-done((f32[4,3,512]{2,1,0:T(4,128)S(1)}, f32[4,3,512]{2,1,0:T(4,128)S(1)}, u32[]{:S(2)}, u32[]{:S(2)}) %collective-permute-start.3) | collective-permute-done | bytes 24608 | tf_op jit(solution)/shard_map/ppermute | solution.py:26
  21.3 2.6 %collective-permute-done.4 = f32[2,3,512]{2,1,0:T(4,128)S(1)} collective-permute-done((f32[2,3,512]{2,1,0:T(4,128)S(1)}, f32[2,3,512]{2,1,0:T(4,128)S(1)}, u32[]{:S(2)}, u32[]{:S(2)}) %collective-permute-start.4) | collective-permute-done | bytes 12320 | tf_op jit(solution)/shard_map/ppermute | solution.py:26
  23.9 0.4 collective-permute-start.5
  24.3 2.2 %collective-permute-done.5 = f32[1,3,512]{2,1,0:T(4,128)S(1)} collective-permute-done((f32[1,3,512]{2,1,0:T(4,128)S(1)}, f32[1,3,512]{2,1,0:T(4,128)S(1)}, u32[]{:S(2)}, u32[]{:S(2)}) %collective-permute-start.5) | collective-permute-done | bytes 6176 | tf_op jit(solution)/shard_map/ppermute | solution.py:26
  26.4 1.3 convolution_add_fusion.1
  27.7 1.0 fusion.1
  28.7 2.3 %copy-done.1 = bf16[1,512,9,512]{3,1,2,0:T(8,128)(2,1)S(1)} copy-done((bf16[1,512,9,512]{3,1,2,0:T(8,128)(2,1)S(1)}, bf16[1,512,9,512]{3,1,2,0:T(8,128)(2,1)}, u32[]{:S(2)}) %copy-start.1) | copy-done | bytes 4718616
  31.1 0.6 forward_conv.6
  31.7 0.7 collective-permute-start.6
  32.4 0.6 forward_conv.7
  33.0 0.7 collective-permute-start.7
  33.7 0.6 forward_conv.8
  34.4 1.3 collective-permute-start.8
  35.7 23.0 %collective-permute-done.8.refs_0_ = bf16[256,512]{1,0:T(8,128)(2,1)S(1)} collective-permute-done((bf16[256,512]{1,0:T(8,128)(2,1)S(1)}, bf16[256,512]{1,0:T(8,128)(2,1)S(1)}, u32[]{:S(2)}, u32[]{:S(2)}) %collective-permute-start.8) | collective-permute-done | bytes 262176 | tf_op jit(solution)/shard_map/ppermute | solution.py:348
  58.7 2.4 %forward_conv.9 = (bf16[256,512]{1,0:T(8,128)(2,1)S(1)}, bf16[17,3,16,512]{3,2,1,0:T(8,128)(2,1)S(1)}, f32[60,256,512]{2,1,0:T(8,128)}, f32[8,128]{1,0:T(8,128)S(1)}) custom-call(bf16[256,512]{1,0:T(8,128)(2,1)S(1)} %collective-permute-done.8.refs_0_, bf16[256,512]{1,0:T(8,128)(2,1)S(1)} %bitcast.75, ...), custom_call_target="tpu_custom_call", output_to_operand_aliasing={{1}: (5, {}), {2}: (6, {})} | custom-call | flops 1207959552 | bytes 6029312 | tf_op jit(solution)/shard_map/forward_conv/pallas_call | solution.py:308
  61.1 1.3 collective-permute-start.9
  62.4 6.4 %collective-permute-done.9.refs_0_ = bf16[256,512]{1,0:T(8,128)(2,1)S(1)} collective-permute-done((bf16[256,512]{1,0:T(8,128)(2,1)S(1)}, bf16[256,512]{1,0:T(8,128)(2,1)S(1)}, u32[]{:S(2)}, u32[]{:S(2)}) %collective-permute-start.9) | collective-permute-done | bytes 262176 | tf_op jit(solution)/shard_map/ppermute | solution.py:348
  68.8 2.5 %forward_conv.10 = (bf16[256,512]{1,0:T(8,128)(2,1)S(1)}, bf16[17,3,16,512]{3,2,1,0:T(8,128)(2,1)S(1)}, f32[60,256,512]{2,1,0:T(8,128)}, f32[8,128]{1,0:T(8,128)S(1)}) custom-call(bf16[256,512]{1,0:T(8,128)(2,1)S(1)} %collective-permute-done.9.refs_0_, bf16[256,512]{1,0:T(8,128)(2,1)S(1)} %bitcast.76, ...), custom_call_target="tpu_custom_call", output_to_operand_aliasing={{1}: (5, {}), {2}: (6, {})} | custom-call | flops 1207959552 | bytes 6029312 | tf_op jit(solution)/shard_map/forward_conv/pallas_call | solution.py:308
  71.3 1.3 collective-permute-start.10
  72.6 5.7 %collective-permute-done.10.refs_0_ = bf16[256,512]{1,0:T(8,128)(2,1)S(1)} collective-permute-done((bf16[256,512]{1,0:T(8,128)(2,1)S(1)}, bf16[256,512]{1,0:T(8,128)(2,1)S(1)}, u32[]{:S(2)}, u32[]{:S(2)}) %collective-permute-start.10) | collective-permute-done | bytes 262176 | tf_op jit(solution)/shard_map/ppermute | solution.py:348
  78.3 3.1 %forward_conv.11 = (bf16[256,512]{1,0:T(8,128)(2,1)}, bf16[17,3,16,512]{3,2,1,0:T(8,128)(2,1)S(1)}, f32[60,256,512]{2,1,0:T(8,128)}, f32[8,128]{1,0:T(8,128)S(1)}) custom-call(bf16[256,512]{1,0:T(8,128)(2,1)S(1)} %collective-permute-done.10.refs_0_, bf16[256,512]{1,0:T(8,128)(2,1)S(1)} %bitcast.77, ...), custom_call_target="tpu_custom_call", output_to_operand_aliasing={{1}: (5, {}), {2}: (6, {})} | custom-call | flops 1207959552 | bytes 6029312 | tf_op jit(solution)/shard_map/forward_conv/pallas_call | solution.py:308
  81.5 2.9 %backward_conv.6 = (bf16[256,512]{1,0:T(8,128)(2,1)S(1)}, bf16[17,3,16,512]{3,2,1,0:T(8,128)(2,1)S(1)}) custom-call(f32[1,512]{1,0:T(1,128)S(1)} %bitcast.84, f32[16,512]{1,0:T(8,128)S(1)} %select_maximum_fusion.refs_1_.refs_2_, f32[8,128]{1,0:T(8,128)S(1)} %get-tuple-element.63.refs_2_.refs_3_, f32[8,128]{1,0:T(8,128)S(1)} %get-tuple-element.67.refs_3_.refs_4_, ...), custom_call_target="tpu_custom_call" | custom-call | flops 1207959552 | bytes 6029312 | tf_op jit(solution)/shard_map/backward_conv/pallas_call | solution.py:327
  84.4 1.3 collective-permute-start.11
  85.7 1.1 collective-permute-done.11.refs_0_
  86.8 2.9 %backward_conv.7 = (bf16[256,512]{1,0:T(8,128)(2,1)S(1)}, bf16[17,3,16,512]{3,2,1,0:T(8,128)(2,1)S(1)}) custom-call(bf16[256,512]{1,0:T(8,128)(2,1)S(1)} %collective-permute-done.11.refs_0_, f32[1,512]{1,0:T(1,128)S(1)} %bitcast.85, f32[16,512]{1,0:T(8,128)S(1)} %select_maximum_fusion.refs_1_.refs_2_, ...), custom_call_target="tpu_custom_call", output_to_operand_aliasing={{1}: (8, {})} | custom-call | flops 1207959552 | bytes 6029312 | tf_op jit(solution)/shard_map/backward_conv/pallas_call | solution.py:327
  89.8 2.3 %collective-permute-start.12 = (bf16[256,512]{1,0:T(8,128)(2,1)S(1)}, bf16[256,512]{1,0:T(8,128)(2,1)S(1)}, u32[]{:S(2)}, u32[]{:S(2)}) collective-permute-start(bf16[256,512]{1,0:T(8,128)(2,1)S(1)} %get-tuple-element.75), channel_id=1, source_target_pairs={{16,8},{24,16},{17,9},{25,17},{18,10},{26,18},{19,11},{27,19},{20,... | collective-permute-start | bytes 786440 | tf_op jit(solution)/shard_map/ppermute | solution.py:369
  92.0 1.1 collective-permute-done.12.refs_0_
  93.2 2.9 %backward_conv.8 = (bf16[256,512]{1,0:T(8,128)(2,1)S(1)}, bf16[17,3,16,512]{3,2,1,0:T(8,128)(2,1)S(1)}) custom-call(bf16[256,512]{1,0:T(8,128)(2,1)S(1)} %collective-permute-done.12.refs_0_, f32[1,512]{1,0:T(1,128)S(1)} %bitcast.86, f32[16,512]{1,0:T(8,128)S(1)} %select_maximum_fusion.refs_1_.refs_2_, ...), custom_call_target="tpu_custom_call", output_to_operand_aliasing={{1}: (8, {})} | custom-call | flops 1207959552 | bytes 6029312 | tf_op jit(solution)/shard_map/backward_conv/pallas_call | solution.py:327
  96.1 4.6 %collective-permute-start.13 = (bf16[256,512]{1,0:T(8,128)(2,1)S(1)}, bf16[256,512]{1,0:T(8,128)(2,1)S(1)}, u32[]{:S(2)}, u32[]{:S(2)}) collective-permute-start(bf16[256,512]{1,0:T(8,128)(2,1)S(1)} %get-tuple-element.77), channel_id=1, source_target_pairs={{8,0},{16,8},{24,16},{9,1},{17,9},{25,17},{10,2},{18,10},{26,18},{... | collective-permute-start | bytes 786440 | tf_op jit(solution)/shard_map/ppermute | solution.py:369
  100.7 0.1 collective-permute-start.21
  100.8 1.0 collective-permute-done.13.refs_0_
  101.9 0.7 collective-permute-start.14
  102.6 0.5 collective-permute-start.20
  103.1 1.1 collective-permute-start.19
  104.3 0.7 collective-permute-start.15
  105.0 1.0 backward_conv.11
  105.9 0.4 pack_grad.1
  106.3 0.4 collective-permute-start.16
  106.7 1.0 collective-permute-start.17
  107.7 12.3 %collective-permute-done.21.refs_7_ = bf16[17,3,16,512]{3,2,1,0:T(8,128)(2,1)S(1)} collective-permute-done((bf16[17,3,16,512]{3,2,1,0:T(8,128)(2,1)S(1)}, bf16[17,3,16,512]{3,2,1,0:T(8,128)(2,1)S(1)}, u32[]{:S(2)}, u32[]{:S(2)}) %collective-permute-start.21) | collective-permute-done | bytes 835616 | tf_op jit(solution)/shard_map/ppermute | solution.py:26
  120.0 17.1 %collective-permute-done.20.refs_6_ = bf16[17,3,16,512]{3,2,1,0:T(8,128)(2,1)S(1)} collective-permute-done((bf16[17,3,16,512]{3,2,1,0:T(8,128)(2,1)S(1)}, bf16[17,3,16,512]{3,2,1,0:T(8,128)(2,1)S(1)}, u32[]{:S(2)}, u32[]{:S(2)}) %collective-permute-start.20) | collective-permute-done | bytes 835616 | tf_op jit(solution)/shard_map/ppermute | solution.py:26
  137.1 3.1 %collective-permute-done.19.refs_5_ = bf16[17,3,16,512]{3,2,1,0:T(8,128)(2,1)S(1)} collective-permute-done((bf16[17,3,16,512]{3,2,1,0:T(8,128)(2,1)S(1)}, bf16[17,3,16,512]{3,2,1,0:T(8,128)(2,1)S(1)}, u32[]{:S(2)}, u32[]{:S(2)}) %collective-permute-start.19) | collective-permute-done | bytes 835616 | tf_op jit(solution)/shard_map/ppermute | solution.py:26
  140.1 7.1 %collective-permute-done.16.refs_1_ = bf16[128,896]{1,0:T(8,128)(2,1)S(1)} collective-permute-done((bf16[128,896]{1,0:T(8,128)(2,1)S(1)}, bf16[128,896]{1,0:T(8,128)(2,1)S(1)}, u32[]{:S(2)}, u32[]{:S(2)}) %collective-permute-start.16) | collective-permute-done | bytes 229408 | tf_op jit(solution)/shard_map/ppermute | solution.py:26
  147.3 0.5 collective-permute-done.18.refs_3_
  147.8 6.5 %weight_grad.1 = (f32[1,3,64,512]{3,2,1,0:T(8,128)S(1)}, bf16[1,3,64,512]{3,2,1,0:T(8,128)(2,1)S(1)}, f32[1,3,64,512]{3,2,1,0:T(8,128)S(1)}, bf16[1,3,64,512]{3,...) custom-call(bf16[128,896]{1,0:T(8,128)(2,1)S(1)} %get-tuple-element.84.refs_0_, ...), custom_call_target="tpu_custom_call" | custom-call | flops 3623878656 | bytes 20971520 | tf_op jit(solution)/shard_map/weight_grad/pallas_call | solution.py:398
  154.3 2.4 %collective-permute-start.23 = (bf16[1,3,64,512]{3,2,1,0:T(8,128)(2,1)S(1)}, bf16[1,3,64,512]{3,2,1,0:T(8,128)(2,1)S(1)}, u32[]{:S(2)}, u32[]{:S(2)}) collective-permute-start(bf16[1,3,64,512]{3,2,1,0:T(8,128)(2,1)S(1)} %get-tuple-element.92), channel_id=1, source_target_pairs={{0,4},{1,5},{2,6},{3,7},{4,0},{5,1},{6,2},{7,3},{8,12},{9,13},{10,... | collective-permute-start | bytes 589832 | tf_op jit(solution)/shard_map/ppermute | solution.py:26
  156.7 0.1 collective-permute-start.24
  156.8 17.6 %collective-permute-done.22 = bf16[1,3,64,512]{3,2,1,0:T(8,128)(2,1)S(1)} collective-permute-done((bf16[1,3,64,512]{3,2,1,0:T(8,128)(2,1)S(1)}, bf16[1,3,64,512]{3,2,1,0:T(8,128)(2,1)S(1)}, u32[]{:S(2)}, u32[]{:S(2)}) %collective-permute-start.22) | collective-permute-done | bytes 196640 | tf_op jit(solution)/shard_map/ppermute | solution.py:26
  174.4 4.1 %collective-permute-done.23 = bf16[1,3,64,512]{3,2,1,0:T(8,128)(2,1)S(1)} collective-permute-done((bf16[1,3,64,512]{3,2,1,0:T(8,128)(2,1)S(1)}, bf16[1,3,64,512]{3,2,1,0:T(8,128)(2,1)S(1)}, u32[]{:S(2)}, u32[]{:S(2)}) %collective-permute-start.23) | collective-permute-done | bytes 196640 | tf_op jit(solution)/shard_map/ppermute | solution.py:26
  178.7 4.1 %collective-permute-done.24 = bf16[1,3,64,512]{3,2,1,0:T(8,128)(2,1)S(1)} collective-permute-done((bf16[1,3,64,512]{3,2,1,0:T(8,128)(2,1)S(1)}, bf16[1,3,64,512]{3,2,1,0:T(8,128)(2,1)S(1)}, u32[]{:S(2)}, u32[]{:S(2)}) %collective-permute-start.24) | collective-permute-done | bytes 196640 | tf_op jit(solution)/shard_map/ppermute | solution.py:26
  182.9 1.0 copy-done.4
  (51 shorter events, 0.7 us)
Async XLA Ops:
  0.0 6.0 %copy-start = (f32[1024,512]{1,0:T(8,128)S(1)}, f32[1024,512]{1,0:T(8,128)}, u32[]{:S(2)}) copy-start(f32[1024,512]{1,0:T(8,128)} %param.11) | copy-start | bytes 6291460
  0.0 7.7 %collective-permute-start = (s32[1,3,77]{2,1,0:T(4,128)}, s32[1,3,77]{2,1,0:T(4,128)S(1)}, u32[]{:S(2)}, u32[]{:S(2)}) collective-permute-start(s32[1,3,77]{2,1,0:T(4,128)} %bitcast.90), channel_id=1, source_target_pairs={{0,1},{1,0},{2,3},{3,2},{4,5},{5,4},{6,7},{7,6},{8,9},{9,8},{10,11... | collective-permute-start | bytes 2780 | tf_op jit(solution)/shard_map/ppermute | solution.py:26
  2.6 5.2 %copy-start.3 = (s32[3,77]{1,0:T(4,128)S(1)}, s32[3,77]{1,0:T(4,128)}, u32[]{:S(2)}) copy-start(s32[3,77]{1,0:T(4,128)} %param.8) | copy-start | bytes 2776
  7.7 2.5 %collective-permute-start.1 = (s32[2,3,77]{2,1,0:T(4,128)S(1)}, s32[2,3,77]{2,1,0:T(4,128)S(1)}, u32[]{:S(2)}, u32[]{:S(2)}) collective-permute-start(s32[2,3,77]{2,1,0:T(4,128)S(1)} %pad_add_fusion.1), channel_id=1, source_target_pairs={{0,2},{1,3},{2,0},{3,1},{4,6},{5,7},{6,4},{7,5},{8,10},{9,11},{10,... | collective-permute-start | bytes 5552 | tf_op jit(solution)/shard_map/ppermute | solution.py:26
  10.3 3.4 %collective-permute-start.2 = (s32[4,3,77]{2,1,0:T(4,128)S(1)}, s32[4,3,77]{2,1,0:T(4,128)S(1)}, u32[]{:S(2)}, u32[]{:S(2)}) collective-permute-start(s32[4,3,77]{2,1,0:T(4,128)S(1)} %pad_add_fusion), channel_id=1, source_target_pairs={{0,4},{1,5},{2,6},{3,7},{4,0},{5,1},{6,2},{7,3},{8,12},{9,13},{10,... | collective-permute-start | bytes 11096 | tf_op jit(solution)/shard_map/ppermute | solution.py:26
  17.1 11.6 %copy-start.2 = (f32[512]{0:T(512)S(1)}, f32[512]{0:T(512)}, u32[]{:S(2)}) copy-start(f32[512]{0:T(512)} %param.15) | copy-start | bytes 6148
  17.2 4.0 %collective-permute-start.3 = (f32[4,3,512]{2,1,0:T(4,128)S(1)}, f32[4,3,512]{2,1,0:T(4,128)S(1)}, u32[]{:S(2)}, u32[]{:S(2)}) collective-permute-start(f32[4,3,512]{2,1,0:T(4,128)S(1)} %slice.54), channel_id=1, source_target_pairs={{0,4},{1,5},{2,6},{3,7},{4,0},{5,1},{6,2},{7,3},{8,12},{9,13},{10,... | collective-permute-start | bytes 73736 | tf_op jit(solution)/shard_map/ppermute | solution.py:26
  21.2 2.7 %collective-permute-start.4 = (f32[2,3,512]{2,1,0:T(4,128)S(1)}, f32[2,3,512]{2,1,0:T(4,128)S(1)}, u32[]{:S(2)}, u32[]{:S(2)}) collective-permute-start(f32[2,3,512]{2,1,0:T(4,128)S(1)} %slice.73), channel_id=1, source_target_pairs={{0,2},{1,3},{2,0},{3,1},{4,6},{5,7},{6,4},{7,5},{8,10},{9,11},{10,... | collective-permute-start | bytes 36872 | tf_op jit(solution)/shard_map/ppermute | solution.py:26
  23.9 2.6 %collective-permute-start.5 = (f32[1,3,512]{2,1,0:T(4,128)S(1)}, f32[1,3,512]{2,1,0:T(4,128)S(1)}, u32[]{:S(2)}, u32[]{:S(2)}) collective-permute-start(f32[1,3,512]{2,1,0:T(4,128)S(1)} %slice.75), channel_id=1, source_target_pairs={{0,1},{1,0},{2,3},{3,2},{4,5},{5,4},{6,7},{7,6},{8,9},{9,8},{10,11... | collective-permute-start | bytes 18440 | tf_op jit(solution)/shard_map/ppermute | solution.py:26
  28.7 2.3 %copy-start.1 = (bf16[1,512,9,512]{3,1,2,0:T(8,128)(2,1)S(1)}, bf16[1,512,9,512]{3,1,2,0:T(8,128)(2,1)}, u32[]{:S(2)}) copy-start(bf16[1,512,9,512]{3,1,2,0:T(8,128)(2,1)} %param.14) | copy-start | bytes 14155780
  31.7 0.7 collective-permute-start.6
  33.0 0.7 collective-permute-start.7
  34.4 24.3 %collective-permute-start.8 = (bf16[256,512]{1,0:T(8,128)(2,1)S(1)}, bf16[256,512]{1,0:T(8,128)(2,1)S(1)}, u32[]{:S(2)}, u32[]{:S(2)}) collective-permute-start(bf16[256,512]{1,0:T(8,128)(2,1)S(1)} %get-tuple-element.60), channel_id=1, source_target_pairs={{0,8},{8,16},{16,24},{1,9},{9,17},{17,25},{2,10},{10,18},{18,26},{... | collective-permute-start | bytes 786440 | tf_op jit(solution)/shard_map/ppermute | solution.py:348
  61.1 7.7 %collective-permute-start.9 = (bf16[256,512]{1,0:T(8,128)(2,1)S(1)}, bf16[256,512]{1,0:T(8,128)(2,1)S(1)}, u32[]{:S(2)}, u32[]{:S(2)}) collective-permute-start(bf16[256,512]{1,0:T(8,128)(2,1)S(1)} %get-tuple-element.64), channel_id=1, source_target_pairs={{8,16},{16,24},{9,17},{17,25},{10,18},{18,26},{11,19},{19,27},{12,... | collective-permute-start | bytes 786440 | tf_op jit(solution)/shard_map/ppermute | solution.py:348
  71.3 7.0 %collective-permute-start.10 = (bf16[256,512]{1,0:T(8,128)(2,1)S(1)}, bf16[256,512]{1,0:T(8,128)(2,1)S(1)}, u32[]{:S(2)}, u32[]{:S(2)}) collective-permute-start(bf16[256,512]{1,0:T(8,128)(2,1)S(1)} %get-tuple-element.68), channel_id=1, source_target_pairs={{16,24},{17,25},{18,26},{19,27},{20,28},{21,29},{22,30},{23,31}} | collective-permute-start | bytes 786440 | tf_op jit(solution)/shard_map/ppermute | solution.py:348
  78.3 3.2 %slice-start = ((s8[4718592]{0:T(1024)(128)(4,1)}), s8[4194304]{0:T(1024)(128)(4,1)S(1)}, s32[]{:S(2)}) async-start(s8[4718592]{0:T(1024)(128)(4,1)} %bitcast.63), calls=%async_computation | async-start | bytes 8388608
  78.3 3.2 %slice-start.1 = ((s8[4718592]{0:T(1024)(128)(4,1)}), s8[524288]{0:T(1024)(128)(4,1)S(1)}, s32[]{:S(2)}) async-start(s8[4718592]{0:T(1024)(128)(4,1)} %bitcast.63), calls=%async_computation.1 | async-start | bytes 1048576
  84.4 2.4 %collective-permute-start.11 = (bf16[256,512]{1,0:T(8,128)(2,1)S(1)}, bf16[256,512]{1,0:T(8,128)(2,1)S(1)}, u32[]{:S(2)}, u32[]{:S(2)}) collective-permute-start(bf16[256,512]{1,0:T(8,128)(2,1)S(1)} %get-tuple-element.73), channel_id=1, source_target_pairs={{24,16},{25,17},{26,18},{27,19},{28,20},{29,21},{30,22},{31,23}} | collective-permute-start | bytes 786440 | tf_op jit(solution)/shard_map/ppermute | solution.py:369
  89.8 3.4 %collective-permute-start.12 = (bf16[256,512]{1,0:T(8,128)(2,1)S(1)}, bf16[256,512]{1,0:T(8,128)(2,1)S(1)}, u32[]{:S(2)}, u32[]{:S(2)}) collective-permute-start(bf16[256,512]{1,0:T(8,128)(2,1)S(1)} %get-tuple-element.75), channel_id=1, source_target_pairs={{16,8},{24,16},{17,9},{25,17},{18,10},{26,18},{19,11},{27,19},{20,... | collective-permute-start | bytes 786440 | tf_op jit(solution)/shard_map/ppermute | solution.py:369
  96.1 5.8 %collective-permute-start.13 = (bf16[256,512]{1,0:T(8,128)(2,1)S(1)}, bf16[256,512]{1,0:T(8,128)(2,1)S(1)}, u32[]{:S(2)}, u32[]{:S(2)}) collective-permute-start(bf16[256,512]{1,0:T(8,128)(2,1)S(1)} %get-tuple-element.77), channel_id=1, source_target_pairs={{8,0},{16,8},{24,16},{9,1},{17,9},{25,17},{10,2},{18,10},{26,18},{... | collective-permute-start | bytes 786440 | tf_op jit(solution)/shard_map/ppermute | solution.py:369
  100.7 19.3 %collective-permute-start.21 = (bf16[17,3,16,512]{3,2,1,0:T(8,128)(2,1)S(1)}, bf16[17,3,16,512]{3,2,1,0:T(8,128)(2,1)S(1)}, u32[]{:S(2)}, u32[]{:S(2)}) collective-permute-start(bf16[17,3,16,512]{3,2,1,0:T(8,128)(2,1)S(1)} %get-tuple-element.88.refs_4_), channel_id=1, source_target_pairs={{0,3},{1,2},{2,1},{3,0},{4,7},{5,6},{6,5},{7,4},{8,11},{9,10},{10,... | collective-permute-start | bytes 2506760 | tf_op jit(solution)/shard_map/ppermute | solution.py:26
  101.9 2.3 %collective-permute-start.14 = (bf16[256,512]{1,0:T(8,128)(2,1)S(1)}, bf16[256,512]{1,0:T(8,128)(2,1)S(1)}, u32[]{:S(2)}, u32[]{:S(2)}) collective-permute-start(bf16[256,512]{1,0:T(8,128)(2,1)S(1)} %get-tuple-element.79), channel_id=1, source_target_pairs={{8,0},{16,8},{9,1},{17,9},{10,2},{18,10},{11,3},{19,11},{12,4},{20... | collective-permute-start | bytes 786440 | tf_op jit(solution)/shard_map/ppermute | solution.py:369
  102.6 34.5 %collective-permute-start.20 = (bf16[17,3,16,512]{3,2,1,0:T(8,128)(2,1)S(1)}, bf16[17,3,16,512]{3,2,1,0:T(8,128)(2,1)S(1)}, u32[]{:S(2)}, u32[]{:S(2)}) collective-permute-start(bf16[17,3,16,512]{3,2,1,0:T(8,128)(2,1)S(1)} %get-tuple-element.88.refs_4_), channel_id=1, source_target_pairs={{0,2},{1,3},{2,0},{3,1},{4,6},{5,7},{6,4},{7,5},{8,10},{9,11},{10,... | collective-permute-start | bytes 2506760 | tf_op jit(solution)/shard_map/ppermute | solution.py:26
  103.1 37.0 %collective-permute-start.19 = (bf16[17,3,16,512]{3,2,1,0:T(8,128)(2,1)S(1)}, bf16[17,3,16,512]{3,2,1,0:T(8,128)(2,1)S(1)}, u32[]{:S(2)}, u32[]{:S(2)}) collective-permute-start(bf16[17,3,16,512]{3,2,1,0:T(8,128)(2,1)S(1)} %get-tuple-element.88.refs_4_), channel_id=1, source_target_pairs={{0,1},{1,0},{2,3},{3,2},{4,5},{5,4},{6,7},{7,6},{8,9},{9,8},{10,11... | collective-permute-start | bytes 2506760 | tf_op jit(solution)/shard_map/ppermute | solution.py:26
  104.3 0.7 collective-permute-start.15
  106.3 40.9 %collective-permute-start.16 = (bf16[128,896]{1,0:T(8,128)(2,1)S(1)}, bf16[128,896]{1,0:T(8,128)(2,1)S(1)}, u32[]{:S(2)}, u32[]{:S(2)}) collective-permute-start(bf16[128,896]{1,0:T(8,128)(2,1)S(1)} %get-tuple-element.85), channel_id=1, source_target_pairs={{0,1},{1,0},{2,3},{3,2},{4,5},{5,4},{6,7},{7,6},{8,9},{9,8},{10,11... | collective-permute-start | bytes 688136 | tf_op jit(solution)/shard_map/ppermute | solution.py:26
  106.7 40.5 %collective-permute-start.17 = (bf16[128,896]{1,0:T(8,128)(2,1)S(1)}, bf16[128,896]{1,0:T(8,128)(2,1)S(1)}, u32[]{:S(2)}, u32[]{:S(2)}) collective-permute-start(bf16[128,896]{1,0:T(8,128)(2,1)S(1)} %get-tuple-element.86), channel_id=1, source_target_pairs={{0,2},{1,3},{2,0},{3,1},{4,6},{5,7},{6,4},{7,5},{8,10},{9,11},{10,... | collective-permute-start | bytes 688136 | tf_op jit(solution)/shard_map/ppermute | solution.py:26
  120.0 27.7 %collective-permute-start.18 = (bf16[128,896]{1,0:T(8,128)(2,1)S(1)}, bf16[128,896]{1,0:T(8,128)(2,1)S(1)}, u32[]{:S(2)}, u32[]{:S(2)}) collective-permute-start(bf16[128,896]{1,0:T(8,128)(2,1)S(1)} %get-tuple-element.87), channel_id=1, source_target_pairs={{0,3},{1,2},{2,1},{3,0},{4,7},{5,6},{6,5},{7,4},{8,11},{9,10},{10,... | collective-permute-start | bytes 688136 | tf_op jit(solution)/shard_map/ppermute | solution.py:26
  154.2 20.1 %collective-permute-start.22 = (bf16[1,3,64,512]{3,2,1,0:T(8,128)(2,1)S(1)}, bf16[1,3,64,512]{3,2,1,0:T(8,128)(2,1)S(1)}, u32[]{:S(2)}, u32[]{:S(2)}) collective-permute-start(bf16[1,3,64,512]{3,2,1,0:T(8,128)(2,1)S(1)} %get-tuple-element.90), channel_id=1, source_target_pairs={{0,4},{1,5},{2,6},{3,7},{4,0},{5,1},{6,2},{7,3},{8,12},{9,13},{10,... | collective-permute-start | bytes 589832 | tf_op jit(solution)/shard_map/ppermute | solution.py:26
  154.3 24.2 %collective-permute-start.23 = (bf16[1,3,64,512]{3,2,1,0:T(8,128)(2,1)S(1)}, bf16[1,3,64,512]{3,2,1,0:T(8,128)(2,1)S(1)}, u32[]{:S(2)}, u32[]{:S(2)}) collective-permute-start(bf16[1,3,64,512]{3,2,1,0:T(8,128)(2,1)S(1)} %get-tuple-element.92), channel_id=1, source_target_pairs={{0,4},{1,5},{2,6},{3,7},{4,0},{5,1},{6,2},{7,3},{8,12},{9,13},{10,... | collective-permute-start | bytes 589832 | tf_op jit(solution)/shard_map/ppermute | solution.py:26
  156.7 26.1 %collective-permute-start.24 = (bf16[1,3,64,512]{3,2,1,0:T(8,128)(2,1)S(1)}, bf16[1,3,64,512]{3,2,1,0:T(8,128)(2,1)S(1)}, u32[]{:S(2)}, u32[]{:S(2)}) collective-permute-start(bf16[1,3,64,512]{3,2,1,0:T(8,128)(2,1)S(1)} %get-tuple-element.94), channel_id=1, source_target_pairs={{0,4},{1,5},{2,6},{3,7},{4,0},{5,1},{6,2},{7,3},{8,12},{9,13},{10,... | collective-permute-start | bytes 589832 | tf_op jit(solution)/shard_map/ppermute | solution.py:26
  182.9 1.0 copy-start.4

commit v4 on v3

--- a/solution.py
+++ b/solution.py
@@ -14,8 +14,7 @@
 F32 = jnp.float32
 BF16 = jnp.bfloat16
 VMEM = pltpu.VMEM
-LIMIT = 40 * 1024 * 1024
-SLOTS = 60
+LIMIT = 32 * 1024 * 1024
 
 
 def params():
@@ -61,6 +60,74 @@
     return total
 
 
+def prepare_kernel(latent_in, weight, start, squares, first_map, latent):
+    channels = weight.shape[1]
+    latent[...] = latent_in[...]
+    for block in range(0, channels, 64):
+        total = None
+        for tap in range(9):
+            value = weight[pl.ds(tap * channels + block, 64), :].astype(F32)
+            total = value * value if total is None else total + value * value
+        squares[pl.ds(block, 64), :] = total
+    first_map[...] = jnp.transpose(start[...].astype(F32)).astype(BF16)
+
+
+def join_kernel(*refs):
+    out = refs[-1]
+    size = refs[0].shape[0]
+    for index, ref in enumerate(refs[:-1]):
+        out[pl.ds(index * size, size), :] = ref[...]
+
+
+def text_kernel(ids, other_ids, table, stay, go):
+    vocab_rows = table.shape[0]
+    here = lax.axis_index("dp")
+    half = ids.shape[0]
+    full = vocab_rows // 128 * 128
+    width = full if full == vocab_rows else full + 128
+    row = lax.broadcasted_iota(jnp.int32, (2 * half, width), 1)
+    row = jnp.where(row < vocab_rows, row + here * vocab_rows, -1)
+    wanted = jnp.concatenate([ids[...], other_ids[...]], axis=0)
+    hits = jnp.zeros((2 * half, width), F32)
+    for token in range(TXT_LEN):
+        hits = hits + jnp.where(wanted[:, token : token + 1] == row, 1.0, 0.0)
+    hits = hits.astype(BF16)
+    sums = jnp.dot(hits[:, :full], table[pl.ds(0, full), :], preferred_element_type=F32)
+    if width > full:
+        last = table[pl.ds(full, vocab_rows - full), :].astype(F32)
+        blank = jnp.zeros((width - vocab_rows, table.shape[1]), F32)
+        last = jnp.concatenate([last, blank], axis=0).astype(BF16)
+        sums = sums + jnp.dot(hits[:, full:], last, preferred_element_type=F32)
+    stay[...] = sums[:half]
+    go[...] = sums[half:]
+
+
+def add_kernel(one, two, *outs):
+    total = one[...] + two[...]
+    size = outs[0].shape[0]
+    for index, out in enumerate(outs):
+        out[...] = total[index * size : (index + 1) * size]
+
+
+def style_kernel(*refs):
+    sums, (latent, style_weight, squares, pack) = refs[:GROUP], refs[GROUP:]
+    section = lax.axis_index("section")
+    sections = lax.axis_size("section")
+    is_gen = section < sections - sections // 4
+    micro, channels = latent.shape
+    text_mean = ((sums[0][...] + sums[1][...]) + (sums[2][...] + sums[3][...])) / TXT_LEN
+    code = jnp.where(is_gen, latent[...] + text_mean, text_mean)
+    code = jnp.concatenate([code, jnp.zeros((8 - micro, channels), F32)], axis=0).astype(BF16)
+    across = (((1,), (1,)), ((), ()))
+    styles = 1.0 + lax.dot_general(code, style_weight[...], across, preferred_element_type=F32)
+    norms = lax.dot_general(
+        styles * styles, squares[...], across, preferred_element_type=F32,
+        precision=lax.Precision.HIGHEST,
+    )
+    pack[pl.ds(0, 8), :] = styles
+    pack[pl.ds(8, 8), :] = jnp.where(is_gen, lax.rsqrt(norms + 1e-08), 1.0)
+
+
 def forward_kernel(tick, side, micro, *refs):
     if tick:
         received, start, pack, head, weight = refs[:5]
@@ -86,7 +153,8 @@
         squared = style * style
         high = squared.astype(BF16).astype(F32)
         row = lax.broadcasted_iota(jnp.int32, (side, mod.shape[1]), 0)
-        mod_box[side] = jnp.where(row == 0, high, jnp.where(row == 1, squared - high, 0.0)).astype(BF16)
+        low = jnp.where(row < 4, squared - high, 0.0)
+        mod_box[side] = jnp.where(row < 2, high, low).astype(BF16)
         first = pltpu.make_async_copy(mod_box, kept_in.at[:, position], sems.at[0])
         first.start()
         put_shifts(pieces, mod.astype(F32), side, side, rows)
@@ -148,7 +216,8 @@
         term = jnp.where(section < gen_count, term, 0.0)
         high = term.astype(BF16).astype(F32)
         row = lax.broadcasted_iota(jnp.int32, (side, channels), 0)
-        grad_box[side] = jnp.where(row == 0, high, jnp.where(row == 1, term - high, 0.0)).astype(BF16)
+        both = jnp.where(row % 2 == 0, high, term - high)
+        grad_box[side] = jnp.where(row < 4, both, 0.0).astype(BF16)
         first = pltpu.make_async_copy(grad_box, kept_grad.at[:, position], sems.at[1])
         first.start()
         put_shifts(pieces, grad_conv.astype(BF16).astype(F32), side, side, rows)
@@ -177,62 +246,57 @@
             outs[flip][pl.ds(slot * part, part), :] = turned[pl.ds(source, part), :]
 
 
-def weight_grad_kernel(micro, side, count, chunks, *refs):
-    grads, mods, weight = refs[:GROUP], refs[GROUP : 2 * GROUP], refs[2 * GROUP]
-    refs = refs[2 * GROUP + 1 :]
-    outs, (pieces, mixture) = refs[: 2 * len(chunks)], refs[2 * len(chunks) :]
+def shift_kernel(micro, side, *refs):
+    mods, pieces = refs[:GROUP], refs[GROUP]
+    channels = pieces.shape[2]
+    rows = side * micro * side
+    band = micro * side
+    blank = jnp.zeros((band, channels), BF16)
+    for member in range(GROUP):
+        base = member * (rows + 2 * band)
+        for index in range(3):
+            pieces[index, pl.ds(base, band), :] = blank
+            pieces[index, pl.ds(base + band + rows, band), :] = blank
+        value = mods[member][pl.ds(0, side)].reshape(rows, channels)
+        put_shifts(pieces, value.astype(F32), side, base + band, rows)
+
+
+def weight_grad_kernel(micro, side, count, taps, *refs):
+    grads, mods = refs[:GROUP], refs[GROUP : 2 * GROUP]
+    pieces, weight, keep, send = refs[2 * GROUP :]
     channels = weight.shape[1]
     rows = side * micro * side
     band = micro * side
     tall = rows + 2 * band
     part = channels // count
     here = lax.axis_index("dp")
-    blank = jnp.zeros((band, channels), BF16)
+    slots = count // GROUP
+    mixture = None
     for member in range(GROUP):
-        base = member * tall
-        for index in range(3):
-            pieces[index, pl.ds(base, band), :] = blank
-            pieces[index, pl.ds(base + band + rows, band), :] = blank
-        value = mods[member][pl.ds(0, side)].reshape(rows, channels)
-        put_shifts(pieces, value.astype(F32), side, base + band, rows)
-        terms = grads[member][:, pl.ds(rows, 128)].astype(F32)
-        squares = mods[member][side].reshape(band, channels).astype(F32)
-        left = lax.broadcasted_iota(jnp.int32, (128, 128), 0)
-        right = lax.broadcasted_iota(jnp.int32, (128, 128), 1)
-        join = ((left // side == right) & (left % side < 2) & (right < micro)).astype(F32)
-        terms = jnp.dot(terms, join, preferred_element_type=F32, precision=lax.Precision.HIGHEST)
-        joined = lax.broadcasted_iota(jnp.int32, (8, band), 0) == lax.broadcasted_iota(
-            jnp.int32, (8, band), 1
-        ) // side
-        squares = jnp.dot(joined.astype(F32), squares, preferred_element_type=F32, precision=lax.Precision.HIGHEST)
+        squared = mods[member][side].reshape(band, channels).astype(F32)
+        squared = jnp.concatenate([squared, jnp.zeros((128 - band, channels), F32)], axis=0)
         term = jnp.dot(
-            terms[:, :8], squares, preferred_element_type=F32, precision=lax.Precision.HIGHEST
+            grads[member][:, pl.ds(rows, 128)], squared.astype(BF16), preferred_element_type=F32
         )
-        if member:
-            mixture[...] += term
-        else:
-            mixture[...] = term
-    slots = count // GROUP
-    for chunk, taps in enumerate(chunks):
-        keep, send = outs[2 * chunk], outs[2 * chunk + 1]
-        for spot, tap in enumerate(taps):
-            total = None
-            for member in range(GROUP):
-                begin = member * tall + (tap // 3) * band
-                term = jnp.dot(
-                    grads[member][:, pl.ds(0, rows)], pieces[tap % 3, pl.ds(begin, rows), :],
-                    preferred_element_type=F32,
-                )
-                total = term if total is None else total + term
-            for slot in range(slots):
-                source = pl.multiple_of((here ^ (slot << GROUP_BITS)) * part, part)
-                fixed = total[slot * part : (slot + 1) * part] - weight[
-                    pl.ds(tap * channels + source, part), :
-                ].astype(F32) * mixture[pl.ds(slot * part, part), :]
-                if slot < slots // 2:
-                    keep[slot, spot] = fixed
-                else:
-                    send[slot - slots // 2, spot] = fixed.astype(BF16)
+        mixture = term if mixture is None else mixture + term
+    for spot, tap in enumerate(taps):
+        total = None
+        for member in range(GROUP):
+            begin = member * tall + (tap // 3) * band
+            term = jnp.dot(
+                grads[member][:, pl.ds(0, rows)], pieces[tap % 3, pl.ds(begin, rows), :],
+                preferred_element_type=F32,
+            )
+            total = term if total is None else total + term
+        for slot in range(slots):
+            source = pl.multiple_of((here ^ (slot << GROUP_BITS)) * part, part)
+            fixed = total[slot * part : (slot + 1) * part] - weight[
+                pl.ds(tap * channels + source, part), :
+            ].astype(F32) * mixture[slot * part : (slot + 1) * part]
+            if slot < slots // 2:
+                keep[slot, spot] = fixed
+            else:
+                send[slot - slots // 2, spot] = fixed.astype(BF16)
 
 
 def on_device(
@@ -243,56 +307,52 @@
     bits = count.bit_length() - 1
     gen_count = sections - sections // 4
     section_at = lax.axis_index("section")
-    here = lax.axis_index("dp")
-    is_gen = section_at < gen_count
     micro = seed_ids.shape[0]
     channels, pixels = start_map.shape
     side = RES
-    vocab_rows = text_table.shape[0]
     norm_div = pixels * math.sqrt(channels)
 
-    ids = text_ids[None]
-    weight = conv_weight[0]
-    weight_out = jnp.transpose(weight, (1, 0, 2))
-    flat_out = weight_out.reshape(9 * channels, channels)
-    squares = jnp.sum(jnp.square(weight_out.astype(F32)), axis=0)
-    first_map = start_map.T
-    latent = jnp.take(latent_table, seed_ids, axis=0)
-    for stage in range(bits):
-        other = swap(ids, 1 << stage, count)
-        if stage == 0:
-            other, squares, first_map, latent = lax.optimization_barrier(
-                (other, squares, first_map, latent)
-            )
-        ids = jnp.concatenate([ids, other], axis=0)
-    wanted = ids.reshape(count * micro, TXT_LEN) - here * vocab_rows
-    rows = lax.broadcasted_iota(jnp.int32, (1, 1, vocab_rows), 2)
-    hits = jnp.sum((wanted[:, :, None] == rows).astype(F32), axis=1)
-    sums = jnp.dot(hits.astype(BF16), text_table, preferred_element_type=F32)
-    sums = sums.reshape(count, micro, channels)
-    for stage in reversed(range(bits)):
-        half = 1 << stage
-        sums = sums[:half] + swap(sums[half:], half, count)
-    text_mean = sums[0] / TXT_LEN
-
-    code_now = jnp.where(is_gen, latent + text_mean, text_mean).astype(BF16)
-    styles = 1.0 + lax.dot_general(
-        code_now, style_weight[0], (((1,), (1,)), ((), ())), preferred_element_type=F32
+    whole = pl.BlockSpec(memory_space=VMEM)
+    far = pl.BlockSpec(memory_space=pltpu.HBM)
+    flat_out = jnp.transpose(conv_weight[0], (1, 0, 2)).reshape(9 * channels, channels)
+
+    def small(kernel, shapes, *arrays, specs=None, scratch=()):
+        return pl.pallas_call(
+            kernel,
+            in_specs=specs or [whole] * len(arrays),
+            out_specs=[whole] * len(shapes),
+            out_shape=[jax.ShapeDtypeStruct(*shape) for shape in shapes],
+            scratch_shapes=scratch,
+            compiler_params=params(),
+        )(*arrays)
+
+    parts = [text_ids]
+    for flip in range(1, GROUP):
+        parts.append(swap(text_ids, flip, count))
+    squares, first_map, latent = small(
+        prepare_kernel,
+        [((channels, channels), F32), ((pixels, channels), BF16), ((micro, channels), F32)],
+        jnp.take(latent_table, seed_ids, axis=0), flat_out, start_map,
     )
-    demods = lax.rsqrt(
-        lax.dot_general(
-            styles * styles, squares, (((1,), (1,)), ((), ())), precision=lax.Precision.HIGHEST
-        )
-        + 1e-08
-    )
-    demods = jnp.where(is_gen, demods, jnp.ones_like(demods))
-    rest = ((0, 8 - micro), (0, 0))
-    pack = jnp.concatenate([jnp.pad(styles, rest), jnp.pad(demods, rest)], axis=0)
+    (ids,) = small(join_kernel, [((GROUP * micro, TXT_LEN), jnp.int32)], *parts)
+    for stage in range(GROUP_BITS, bits):
+        other_ids = swap(ids, 1 << stage, count)
+        if stage < bits - 1:
+            (ids,) = small(join_kernel, [((2 * ids.shape[0], TXT_LEN), jnp.int32)], ids, other_ids)
+    half = count * micro // 2
+    stay, go = small(text_kernel, [((half, channels), F32)] * 2, ids, other_ids, text_table)
+    for stage in reversed(range(GROUP_BITS, bits)):
+        got = swap(go, 1 << stage, count)
+        size, outs = (micro, GROUP) if stage == GROUP_BITS else (half // 2, 2)
+        sums = small(add_kernel, [((size, channels), F32)] * outs, stay, got)
+        if stage > GROUP_BITS:
+            stay, go = sums
+            half //= 2
+    sums = [sums[0]] + [swap(sums[flip], flip, count) for flip in range(1, GROUP)]
+    (pack,) = small(style_kernel, [((16, channels), F32)], *sums, latent, style_weight[0], squares)
     head = score_head[None]
     ticks = micro + sections - 1
 
-    whole = pl.BlockSpec(memory_space=VMEM)
-    far = pl.BlockSpec(memory_space=pltpu.HBM)
     flops = 2 * 9 * channels * channels * pixels
     conv_cost = pl.CostEstimate(
         flops=flops, bytes_accessed=9 * channels * channels * 2 + 5 * channels * pixels * 2,
@@ -302,7 +362,7 @@
     conv_scratch = [VMEM((3, tall, channels), BF16)]
     plain = jax.ShapeDtypeStruct((pixels, channels), BF16)
     lined = jax.ShapeDtypeStruct((side + 1, micro, side, channels), BF16)
-    tower = jax.ShapeDtypeStruct((SLOTS, pixels, channels), F32)
+    tower = jax.ShapeDtypeStruct((micro, pixels, channels), F32)
 
     def forward(tick, arrays):
         return pl.pallas_call(
@@ -387,24 +447,35 @@
         compiler_params=params(),
         name="pack_grad",
     )(kept_grad)
-    grads = [packed[0]] + [swap(packed[flip], flip, count) for flip in range(1, GROUP)]
+    grads = [packed[0]]
+    for flip in range(1, GROUP):
+        grads.append(swap(packed[flip], flip, count))
     slots = count // GROUP
-    shapes = []
+    pieces = pl.pallas_call(
+        functools.partial(shift_kernel, micro, side),
+        in_specs=[whole] * GROUP,
+        out_specs=whole,
+        out_shape=jax.ShapeDtypeStruct((3, GROUP * micro * tall, channels), BF16),
+        cost_estimate=pl.CostEstimate(flops=0, bytes_accessed=16 * 1024 * 1024, transcendentals=0),
+        compiler_params=params(),
+        name="shift",
+    )(*mods)
+    pairs = []
     for taps in chunks:
-        shapes += [
-            jax.ShapeDtypeStruct((slots // 2, len(taps), part, channels), F32),
-            jax.ShapeDtypeStruct((slots // 2, len(taps), part, channels), BF16),
-        ]
-    pairs = pl.pallas_call(
-        functools.partial(weight_grad_kernel, micro, side, count, chunks),
-        in_specs=[whole] * (2 * GROUP + 1),
-        out_specs=[whole] * len(shapes),
-        out_shape=shapes,
-        scratch_shapes=[VMEM((3, GROUP * micro * tall, channels), BF16), VMEM((own, channels), F32)],
-        cost_estimate=pl.CostEstimate(flops=micro * flops, bytes_accessed=20 * 1024 * 1024, transcendentals=0),
-        compiler_params=params(),
-        name="weight_grad",
-    )(*grads, *mods, flat_out)
+        pairs += pl.pallas_call(
+            functools.partial(weight_grad_kernel, micro, side, count, taps),
+            in_specs=[whole] * (2 * GROUP + 2),
+            out_specs=[whole] * 2,
+            out_shape=[
+                jax.ShapeDtypeStruct((slots // 2, len(taps), part, channels), F32),
+                jax.ShapeDtypeStruct((slots // 2, len(taps), part, channels), BF16),
+            ],
+            cost_estimate=pl.CostEstimate(
+                flops=micro * flops // len(chunks), bytes_accessed=5 * 1024 * 1024, transcendentals=0
+            ),
+            compiler_params=params(),
+            name="weight_grad",
+        )(*grads, *mods, pieces, flat_out)
     done = [None] * 9
     for chunk, taps in enumerate(chunks):
         keep, send = pairs[2 * chunk], pairs[2 * chunk + 1]

time: 184 us -> 165 us (0.90)
  the two profiles are of different devices: /device:TPU:27 before, /device:TPU:2 now
where the time goes in v4:
time: 165 us
  waiting for transfers between devices  89.7 us (54%)
  starting transfers between devices  41.5 us (25%)
  Pallas kernels  25 us (15%)
  local copies, waits for them, and re-layouts  6.49 us (4%)
    ppermute x17, waiting for transfers between devices, swap(): return lax.ppermute(x, 'dp', [(i, i ^ bit) for i in range(count)])  52.4 us
    ppermute x5, waiting for transfers between devices, on_device(): lax.ppermute(outgoing, 'section', [(i, i + 1) for i in range(sections - 1...  23.2 us
    ppermute x17, starting transfers between devices, swap(): return lax.ppermute(x, 'dp', [(i, i ^ bit) for i in range(count)])  22.8 us
    ppermute x5, waiting for transfers between devices, on_device(): lax.ppermute(outgoing, 'section', [(i, i - 1) for i in range(1, sections)...  14.1 us
    ppermute x5, starting transfers between devices, on_device(): lax.ppermute(outgoing, 'section', [(i, i - 1) for i in range(1, sections)...  11.5 us
    pallas_call x6, Pallas kernels, forward(): pl.pallas_call(functools.partial(forward_kernel, tick, side, micro), in_s...  8.12 us
    ppermute x5, starting transfers between devices, on_device(): lax.ppermute(outgoing, 'section', [(i, i + 1) for i in range(sections - 1...  7.12 us
    pallas_call x6, Pallas kernels, backward(): pl.pallas_call(functools.partial(backward_kernel, tick, side, micro, norm...  6.88 us
  transfers between devices with their start and end apart: 27, of which 18 were waited for; matrix products, arithmetic and copies ran while one was open for 1% of the time, Pallas kernels for 5%

profile of v4, /device:TPU:2, one launch (start us, length us, event | category | flops | bytes accessed | tf_op | source)
XLA Modules:
  0.0 164.7 jit_solution(4795466396333289746)
XLA Ops:
  0.0 1.6 collective-permute-start.1
  1.6 1.5 collective-permute-start
  3.5 0.7 compare_and_fusion
  4.2 1.2 collective-permute-done.refs_1_
  5.4 2.4 %collective-permute-done.2.refs_3_ = s32[3,77]{1,0:T(4,128)S(1)} collective-permute-done((s32[3,77]{1,0:T(4,128)}, s32[3,77]{1,0:T(4,128)S(1)}, u32[]{:S(2)}, u32[]{:S(2)}) %collective-permute-start.2) | collective-permute-done | bytes 956 | tf_op jit(solution)/shard_map/ppermute | solution.py:25
  7.8 0.7 copy-done.7
  8.5 2.6 %collective-permute-start.3 = (s32[12,77]{1,0:T(8,128)S(1)}, s32[12,77]{1,0:T(8,128)S(1)}, u32[]{:S(2)}, u32[]{:S(2)}) collective-permute-start(s32[12,77]{1,0:T(8,128)S(1)} %shard_map.82.ids), channel_id=1, source_target_pairs={{0,4},{1,5},{2,6},{3,7},{4,0},{5,1},{6,2},{7,3},{8,12},{9,13},{10,... | collective-permute-start | bytes 11096 | tf_op jit(solution)/shard_map/ppermute | solution.py:25
  11.1 0.7 compare_select_fusion
  11.7 1.3 collective-permute-done.3.other_ids
  13.0 1.4 copy-done.3
  14.4 1.4 shard_map.83
  15.9 2.6 %collective-permute-start.4 = (f32[12,512]{1,0:T(8,128)S(1)}, f32[12,512]{1,0:T(8,128)S(1)}, u32[]{:S(2)}, u32[]{:S(2)}) collective-permute-start(f32[12,512]{1,0:T(8,128)S(1)} %get-tuple-element.56), channel_id=1, source_target_pairs={{0,4},{1,5},{2,6},{3,7},{4,0},{5,1},{6,2},{7,3},{8,12},{9,13},{10,... | collective-permute-start | bytes 73736 | tf_op jit(solution)/shard_map/ppermute | solution.py:25
  19.0 1.9 %collective-permute-done.4.two = f32[12,512]{1,0:T(8,128)S(1)} collective-permute-done((f32[12,512]{1,0:T(8,128)S(1)}, f32[12,512]{1,0:T(8,128)S(1)}, u32[]{:S(2)}, u32[]{:S(2)}) %collective-permute-start.4) | collective-permute-done | bytes 24608 | tf_op jit(solution)/shard_map/ppermute | solution.py:25
  21.0 0.6 collective-permute-start.5
  21.7 2.8 %collective-permute-start.7 = (f32[3,512]{1,0:T(4,128)S(1)}, f32[3,512]{1,0:T(4,128)S(1)}, u32[]{:S(2)}, u32[]{:S(2)}) collective-permute-start(f32[3,512]{1,0:T(4,128)S(1)} %get-tuple-element.60), channel_id=1, source_target_pairs={{0,3},{1,2},{2,1},{3,0},{4,7},{5,6},{6,5},{7,4},{8,11},{9,10},{10,... | collective-permute-start | bytes 18440 | tf_op jit(solution)/shard_map/ppermute | solution.py:25
  24.6 2.3 %copy-done.1 = bf16[1,512,9,512]{3,1,2,0:T(8,128)(2,1)S(1)} copy-done((bf16[1,512,9,512]{3,1,2,0:T(8,128)(2,1)S(1)}, bf16[1,512,9,512]{3,1,2,0:T(8,128)(2,1)}, u32[]{:S(2)}) %copy-start.1) | copy-done | bytes 4718616
  26.9 0.8 shard_map.85
  27.8 1.1 shard_map.86.refs_1_.refs_2_
  29.3 0.6 forward_conv.6
  29.9 0.7 collective-permute-start.8
  30.6 0.6 forward_conv.7
  31.2 1.3 collective-permute-start.9
  32.5 10.6 %collective-permute-done.9.refs_0_ = bf16[256,512]{1,0:T(8,128)(2,1)S(1)} collective-permute-done((bf16[256,512]{1,0:T(8,128)(2,1)S(1)}, bf16[256,512]{1,0:T(8,128)(2,1)S(1)}, u32[]{:S(2)}, u32[]{:S(2)}) %collective-permute-start.9) | collective-permute-done | bytes 262176 | tf_op jit(solution)/shard_map/ppermute | solution.py:408
  43.1 2.4 %forward_conv.8 = (bf16[256,512]{1,0:T(8,128)(2,1)S(1)}, bf16[17,3,16,512]{3,2,1,0:T(8,128)(2,1)S(1)}, f32[3,256,512]{2,1,0:T(8,128)S(1)}, f32[8,128]{1,0:T(8,128)}) custom-call(bf16[256,512]{1,0:T(8,128)(2,1)S(1)} %collective-permute-done.9.refs_0_, ...), custom_call_target="tpu_custom_call", output_to_operand_aliasing={{1}: (5, {}), {2}: (6, {})} | custom-call | flops 1207959552 | bytes 6029312 | tf_op jit(solution)/shard_map/forward_conv/pallas_call | solution.py:368
  45.5 1.9 %collective-permute-start.10 = (bf16[256,512]{1,0:T(8,128)(2,1)S(1)}, bf16[256,512]{1,0:T(8,128)(2,1)S(1)}, u32[]{:S(2)}, u32[]{:S(2)}) collective-permute-start(bf16[256,512]{1,0:T(8,128)(2,1)S(1)} %get-tuple-element.70), channel_id=1, source_target_pairs={{0,8},{8,16},{16,24},{1,9},{9,17},{17,25},{2,10},{10,18},{18,26},{... | collective-permute-start | bytes 786440 | tf_op jit(solution)/shard_map/ppermute | solution.py:408
  47.5 5.8 %collective-permute-done.10.refs_0_ = bf16[256,512]{1,0:T(8,128)(2,1)S(1)} collective-permute-done((bf16[256,512]{1,0:T(8,128)(2,1)S(1)}, bf16[256,512]{1,0:T(8,128)(2,1)S(1)}, u32[]{:S(2)}, u32[]{:S(2)}) %collective-permute-start.10) | collective-permute-done | bytes 262176 | tf_op jit(solution)/shard_map/ppermute | solution.py:408
  53.2 1.9 %forward_conv.9 = (bf16[256,512]{1,0:T(8,128)(2,1)S(1)}, bf16[17,3,16,512]{3,2,1,0:T(8,128)(2,1)S(1)}, f32[3,256,512]{2,1,0:T(8,128)S(1)}, f32[8,128]{1,0:T(8,128)S(1)}) custom-call(bf16[256,512]{1,0:T(8,128)(2,1)S(1)} %collective-permute-done.10.refs_0_, ...), custom_call_target="tpu_custom_call", output_to_operand_aliasing={{1}: (5, {}), {2}: (6, {})} | custom-call | flops 1207959552 | bytes 6029312 | tf_op jit(solution)/shard_map/forward_conv/pallas_call | solution.py:368
  55.1 1.9 %collective-permute-start.11 = (bf16[256,512]{1,0:T(8,128)(2,1)S(1)}, bf16[256,512]{1,0:T(8,128)(2,1)S(1)}, u32[]{:S(2)}, u32[]{:S(2)}) collective-permute-start(bf16[256,512]{1,0:T(8,128)(2,1)S(1)} %get-tuple-element.74), channel_id=1, source_target_pairs={{8,16},{16,24},{9,17},{17,25},{10,18},{18,26},{11,19},{19,27},{12,... | collective-permute-start | bytes 786440 | tf_op jit(solution)/shard_map/ppermute | solution.py:408
  57.0 5.8 %collective-permute-done.11.refs_0_ = bf16[256,512]{1,0:T(8,128)(2,1)S(1)} collective-permute-done((bf16[256,512]{1,0:T(8,128)(2,1)S(1)}, bf16[256,512]{1,0:T(8,128)(2,1)S(1)}, u32[]{:S(2)}, u32[]{:S(2)}) %collective-permute-start.11) | collective-permute-done | bytes 262176 | tf_op jit(solution)/shard_map/ppermute | solution.py:408
  62.8 1.9 %forward_conv.10 = (bf16[256,512]{1,0:T(8,128)(2,1)S(1)}, bf16[17,3,16,512]{3,2,1,0:T(8,128)(2,1)S(1)}, f32[3,256,512]{2,1,0:T(8,128)S(1)}, f32[8,128]{1,0:T(8,128)S(1)}) custom-call(bf16[256,512]{1,0:T(8,128)(2,1)S(1)} %collective-permute-done.11.refs_0_, ...), custom_call_target="tpu_custom_call", output_to_operand_aliasing={{1}: (5, {}), {2}: (6, {})} | custom-call | flops 1207959552 | bytes 6029312 | tf_op jit(solution)/shard_map/forward_conv/pallas_call | solution.py:368
  64.6 1.3 collective-permute-start.12
  66.0 1.1 collective-permute-done.12.refs_0_
  67.1 0.7 forward_conv.11
  67.9 1.3 collective-permute-start.13
  69.2 5.1 %collective-permute-done.13.refs_0_ = bf16[256,512]{1,0:T(8,128)(2,1)S(1)} collective-permute-done((bf16[256,512]{1,0:T(8,128)(2,1)S(1)}, bf16[256,512]{1,0:T(8,128)(2,1)S(1)}, u32[]{:S(2)}, u32[]{:S(2)}) %collective-permute-start.13) | collective-permute-done | bytes 262176 | tf_op jit(solution)/shard_map/ppermute | solution.py:429
  74.3 2.0 %backward_conv.7 = (bf16[256,512]{1,0:T(8,128)(2,1)S(1)}, bf16[17,3,16,512]{3,2,1,0:T(8,128)(2,1)S(1)}) custom-call(bf16[256,512]{1,0:T(8,128)(2,1)S(1)} %collective-permute-done.13.refs_0_, f32[1,512]{1,0:T(1,128)S(1)} %bitcast.68, f32[16,512]{1,0:T(8,128)S(1)} %shard_map.86.refs_1_.refs_2_, ...), custom_call_target="tpu_custom_call", output_to_operand_aliasing={{1}: (8, {})} | custom-call | flops 1207959552 | bytes 6029312 | tf_op jit(solution)/shard_map/backward_conv/pallas_call | solution.py:387
  76.2 1.9 %collective-permute-start.14 = (bf16[256,512]{1,0:T(8,128)(2,1)S(1)}, bf16[256,512]{1,0:T(8,128)(2,1)S(1)}, u32[]{:S(2)}, u32[]{:S(2)}) collective-permute-start(bf16[256,512]{1,0:T(8,128)(2,1)S(1)} %get-tuple-element.85), channel_id=1, source_target_pairs={{16,8},{24,16},{17,9},{25,17},{18,10},{26,18},{19,11},{27,19},{20,... | collective-permute-start | bytes 786440 | tf_op jit(solution)/shard_map/ppermute | solution.py:429
  78.2 3.9 %collective-permute-done.14.refs_0_ = bf16[256,512]{1,0:T(8,128)(2,1)S(1)} collective-permute-done((bf16[256,512]{1,0:T(8,128)(2,1)S(1)}, bf16[256,512]{1,0:T(8,128)(2,1)S(1)}, u32[]{:S(2)}, u32[]{:S(2)}) %collective-permute-start.14) | collective-permute-done | bytes 262176 | tf_op jit(solution)/shard_map/ppermute | solution.py:429
  82.0 2.0 %backward_conv.8 = (bf16[256,512]{1,0:T(8,128)(2,1)S(1)}, bf16[17,3,16,512]{3,2,1,0:T(8,128)(2,1)S(1)}) custom-call(bf16[256,512]{1,0:T(8,128)(2,1)S(1)} %collective-permute-done.14.refs_0_, f32[1,512]{1,0:T(1,128)S(1)} %bitcast.69, f32[16,512]{1,0:T(8,128)S(1)} %shard_map.86.refs_1_.refs_2_, ...), custom_call_target="tpu_custom_call", output_to_operand_aliasing={{1}: (8, {})} | custom-call | flops 1207959552 | bytes 6029312 | tf_op jit(solution)/shard_map/backward_conv/pallas_call | solution.py:387
  84.0 3.8 %collective-permute-start.15 = (bf16[256,512]{1,0:T(8,128)(2,1)S(1)}, bf16[256,512]{1,0:T(8,128)(2,1)S(1)}, u32[]{:S(2)}, u32[]{:S(2)}) collective-permute-start(bf16[256,512]{1,0:T(8,128)(2,1)S(1)} %get-tuple-element.87), channel_id=1, source_target_pairs={{8,0},{16,8},{24,16},{9,1},{17,9},{25,17},{10,2},{18,10},{26,18},{... | collective-permute-start | bytes 786440 | tf_op jit(solution)/shard_map/ppermute | solution.py:429
  87.8 1.0 collective-permute-start.23
  88.8 2.9 %collective-permute-done.15.refs_0_ = bf16[256,512]{1,0:T(8,128)(2,1)S(1)} collective-permute-done((bf16[256,512]{1,0:T(8,128)(2,1)S(1)}, bf16[256,512]{1,0:T(8,128)(2,1)S(1)}, u32[]{:S(2)}, u32[]{:S(2)}) %collective-permute-start.15) | collective-permute-done | bytes 262176 | tf_op jit(solution)/shard_map/ppermute | solution.py:429
  91.7 2.0 %backward_conv.9 = (bf16[256,512]{1,0:T(8,128)(2,1)S(1)}, bf16[17,3,16,512]{3,2,1,0:T(8,128)(2,1)S(1)}) custom-call(bf16[256,512]{1,0:T(8,128)(2,1)S(1)} %collective-permute-done.15.refs_0_, f32[1,512]{1,0:T(1,128)S(1)} %bitcast.70, f32[16,512]{1,0:T(8,128)S(1)} %shard_map.86.refs_1_.refs_2_, ...), custom_call_target="tpu_custom_call", output_to_operand_aliasing={{1}: (8, {})} | custom-call | flops 1207959552 | bytes 6029312 | tf_op jit(solution)/shard_map/backward_conv/pallas_call | solution.py:387
  93.6 3.8 %collective-permute-start.16 = (bf16[256,512]{1,0:T(8,128)(2,1)S(1)}, bf16[256,512]{1,0:T(8,128)(2,1)S(1)}, u32[]{:S(2)}, u32[]{:S(2)}) collective-permute-start(bf16[256,512]{1,0:T(8,128)(2,1)S(1)} %get-tuple-element.89), channel_id=1, source_target_pairs={{8,0},{16,8},{9,1},{17,9},{10,2},{18,10},{11,3},{19,11},{12,4},{20... | collective-permute-start | bytes 786440 | tf_op jit(solution)/shard_map/ppermute | solution.py:429
  97.8 1.3 collective-permute-start.21
  99.1 2.3 %collective-permute-done.16.refs_0_ = bf16[256,512]{1,0:T(8,128)(2,1)S(1)} collective-permute-done((bf16[256,512]{1,0:T(8,128)(2,1)S(1)}, bf16[256,512]{1,0:T(8,128)(2,1)S(1)}, u32[]{:S(2)}, u32[]{:S(2)}) %collective-permute-start.16) | collective-permute-done | bytes 262176 | tf_op jit(solution)/shard_map/ppermute | solution.py:429
  101.4 0.7 collective-permute-start.17
  102.1 1.0 backward_conv.11
  103.7 1.3 collective-permute-start.19
  105.0 5.3 %collective-permute-done.23.refs_3_.refs_7_ = bf16[17,3,16,512]{3,2,1,0:T(8,128)(2,1)S(1)} collective-permute-done((bf16[17,3,16,512]{3,2,1,0:T(8,128)(2,1)S(1)}, bf16[17,3,16,512]{3,2,1,0:T(8,128)(2,1)S(1)}, u32[]{:S(2)}, u32[]{:S(2)}) %collective-permute-start.23) | collective-permute-done | bytes 835616 | tf_op jit(solution)/shard_map/ppermute | solution.py:25
  110.3 1.0 collective-permute-start.20
  111.2 15.7 %collective-permute-done.22.refs_2_.refs_6_ = bf16[17,3,16,512]{3,2,1,0:T(8,128)(2,1)S(1)} collective-permute-done((bf16[17,3,16,512]{3,2,1,0:T(8,128)(2,1)S(1)}, bf16[17,3,16,512]{3,2,1,0:T(8,128)(2,1)S(1)}, u32[]{:S(2)}, u32[]{:S(2)}) %collective-permute-start.22) | collective-permute-done | bytes 835616 | tf_op jit(solution)/shard_map/ppermute | solution.py:25
  127.0 1.8 %shift.1.refs_8_ = bf16[3,3456,512]{2,1,0:T(8,128)(2,1)S(1)} custom-call(bf16[17,3,16,512]{3,2,1,0:T(8,128)(2,1)S(1)} %get-tuple-element.98.refs_0_.refs_4_, bf16[17,3,16,512]{3,2,1,0:T(8,128)(2,1)S(1)} %collective-permute-done.21.refs_1_.refs_5_, bf16[17,3,16,512]{3,2,1,0:T(8,128)(2,1)S(1)} %collective-permute-done.22.refs_2_.refs_6_, ...), custom_call_target="tpu_custom_call" | custom-call | bytes 16777216 | tf_op jit(solution)/shard_map/shift/pallas_call | solution.py:454
  128.8 4.2 %collective-permute-done.18.refs_1_ = bf16[128,896]{1,0:T(8,128)(2,1)S(1)} collective-permute-done((bf16[128,896]{1,0:T(8,128)(2,1)S(1)}, bf16[128,896]{1,0:T(8,128)(2,1)S(1)}, u32[]{:S(2)}, u32[]{:S(2)}) %collective-permute-start.18) | collective-permute-done | bytes 229408 | tf_op jit(solution)/shard_map/ppermute | solution.py:25
  133.0 2.6 %collective-permute-done.20.refs_3_ = bf16[128,896]{1,0:T(8,128)(2,1)S(1)} collective-permute-done((bf16[128,896]{1,0:T(8,128)(2,1)S(1)}, bf16[128,896]{1,0:T(8,128)(2,1)S(1)}, u32[]{:S(2)}, u32[]{:S(2)}) %collective-permute-start.20) | collective-permute-done | bytes 229408 | tf_op jit(solution)/shard_map/ppermute | solution.py:25
  135.7 1.5 weight_grad.3
  137.2 2.4 %collective-permute-start.24 = (bf16[1,3,64,512]{3,2,1,0:T(8,128)(2,1)S(1)}, bf16[1,3,64,512]{3,2,1,0:T(8,128)(2,1)S(1)}, u32[]{:S(2)}, u32[]{:S(2)}) collective-permute-start(bf16[1,3,64,512]{3,2,1,0:T(8,128)(2,1)S(1)} %get-tuple-element.100), channel_id=1, source_target_pairs={{0,4},{1,5},{2,6},{3,7},{4,0},{5,1},{6,2},{7,3},{8,12},{9,13},{10,... | collective-permute-start | bytes 589832 | tf_op jit(solution)/shard_map/ppermute | solution.py:25
  139.6 1.5 weight_grad.5
  141.1 0.6 collective-permute-start.26
  141.7 1.5 weight_grad.4
  143.2 2.4 %collective-permute-start.25 = (bf16[1,3,64,512]{3,2,1,0:T(8,128)(2,1)S(1)}, bf16[1,3,64,512]{3,2,1,0:T(8,128)(2,1)S(1)}, u32[]{:S(2)}, u32[]{:S(2)}) collective-permute-start(bf16[1,3,64,512]{3,2,1,0:T(8,128)(2,1)S(1)} %get-tuple-element.102), channel_id=1, source_target_pairs={{0,4},{1,5},{2,6},{3,7},{4,0},{5,1},{6,2},{7,3},{8,12},{9,13},{10,... | collective-permute-start | bytes 589832 | tf_op jit(solution)/shard_map/ppermute | solution.py:25
  145.6 10.6 %collective-permute-done.24 = bf16[1,3,64,512]{3,2,1,0:T(8,128)(2,1)S(1)} collective-permute-done((bf16[1,3,64,512]{3,2,1,0:T(8,128)(2,1)S(1)}, bf16[1,3,64,512]{3,2,1,0:T(8,128)(2,1)S(1)}, u32[]{:S(2)}, u32[]{:S(2)}) %collective-permute-start.24) | collective-permute-done | bytes 196640 | tf_op jit(solution)/shard_map/ppermute | solution.py:25
  156.3 7.1 %collective-permute-done.25 = bf16[1,3,64,512]{3,2,1,0:T(8,128)(2,1)S(1)} collective-permute-done((bf16[1,3,64,512]{3,2,1,0:T(8,128)(2,1)S(1)}, bf16[1,3,64,512]{3,2,1,0:T(8,128)(2,1)S(1)}, u32[]{:S(2)}, u32[]{:S(2)}) %collective-permute-start.25) | collective-permute-done | bytes 196640 | tf_op jit(solution)/shard_map/ppermute | solution.py:25
  163.6 1.0 copy-done.8
  (47 shorter events, 2.9 us)
Async XLA Ops:
  0.0 18.5 %copy-start = (f32[1024,512]{1,0:T(8,128)S(1)}, f32[1024,512]{1,0:T(8,128)}, u32[]{:S(2)}) copy-start(f32[1024,512]{1,0:T(8,128)} %param.11) | copy-start | bytes 6291460
  0.0 4.2 %collective-permute-start.1 = (s32[3,77]{1,0:T(4,128)}, s32[3,77]{1,0:T(4,128)S(1)}, u32[]{:S(2)}, u32[]{:S(2)}) collective-permute-start(s32[3,77]{1,0:T(4,128)} %refs_0_.1), channel_id=1, source_target_pairs={{0,2},{1,3},{2,0},{3,1},{4,6},{5,7},{6,4},{7,5},{8,10},{9,11},{10,... | collective-permute-start | bytes 2780 | tf_op jit(solution)/shard_map/ppermute | solution.py:25
  1.6 3.8 %collective-permute-start = (s32[3,77]{1,0:T(4,128)}, s32[3,77]{1,0:T(4,128)S(1)}, u32[]{:S(2)}, u32[]{:S(2)}) collective-permute-start(s32[3,77]{1,0:T(4,128)} %refs_0_.1), channel_id=1, source_target_pairs={{0,1},{1,0},{2,3},{3,2},{4,5},{5,4},{6,7},{7,6},{8,9},{9,8},{10,11... | collective-permute-start | bytes 2780 | tf_op jit(solution)/shard_map/ppermute | solution.py:25
  3.1 4.7 %collective-permute-start.2 = (s32[3,77]{1,0:T(4,128)}, s32[3,77]{1,0:T(4,128)S(1)}, u32[]{:S(2)}, u32[]{:S(2)}) collective-permute-start(s32[3,77]{1,0:T(4,128)} %refs_0_.1), channel_id=1, source_target_pairs={{0,3},{1,2},{2,1},{3,0},{4,7},{5,6},{6,5},{7,4},{8,11},{9,10},{10,... | collective-permute-start | bytes 2780 | tf_op jit(solution)/shard_map/ppermute | solution.py:25
  7.8 0.7 copy-start.7
  8.5 4.5 %collective-permute-start.3 = (s32[12,77]{1,0:T(8,128)S(1)}, s32[12,77]{1,0:T(8,128)S(1)}, u32[]{:S(2)}, u32[]{:S(2)}) collective-permute-start(s32[12,77]{1,0:T(8,128)S(1)} %shard_map.82.ids), channel_id=1, source_target_pairs={{0,4},{1,5},{2,6},{3,7},{4,0},{5,1},{6,2},{7,3},{8,12},{9,13},{10,... | collective-permute-start | bytes 11096 | tf_op jit(solution)/shard_map/ppermute | solution.py:25
  13.0 1.4 copy-start.3
  14.4 10.2 %copy-start.6 = (bf16[512,256]{1,0:T(8,128)(2,1)S(1)}, bf16[512,256]{1,0:T(8,128)(2,1)}, u32[]{:S(2)}) copy-start(bf16[512,256]{1,0:T(8,128)(2,1)} %start.1) | copy-start | bytes 786436
  14.4 13.3 %copy-start.4 = (bf16[1,512,512]{2,1,0:T(8,128)(2,1)S(1)}, bf16[1,512,512]{2,1,0:T(8,128)(2,1)}, u32[]{:S(2)}) copy-start(bf16[1,512,512]{2,1,0:T(8,128)(2,1)} %param.13) | copy-start | bytes 1572868
  15.9 5.1 %collective-permute-start.4 = (f32[12,512]{1,0:T(8,128)S(1)}, f32[12,512]{1,0:T(8,128)S(1)}, u32[]{:S(2)}, u32[]{:S(2)}) collective-permute-start(f32[12,512]{1,0:T(8,128)S(1)} %get-tuple-element.56), channel_id=1, source_target_pairs={{0,4},{1,5},{2,6},{3,7},{4,0},{5,1},{6,2},{7,3},{8,12},{9,13},{10,... | collective-permute-start | bytes 73736 | tf_op jit(solution)/shard_map/ppermute | solution.py:25
  21.0 6.8 %collective-permute-start.5 = (f32[3,512]{1,0:T(4,128)S(1)}, f32[3,512]{1,0:T(4,128)S(1)}, u32[]{:S(2)}, u32[]{:S(2)}) collective-permute-start(f32[3,512]{1,0:T(4,128)S(1)} %get-tuple-element.58), channel_id=1, source_target_pairs={{0,1},{1,0},{2,3},{3,2},{4,5},{5,4},{6,7},{7,6},{8,9},{9,8},{10,11... | collective-permute-start | bytes 18440 | tf_op jit(solution)/shard_map/ppermute | solution.py:25
  21.5 6.2 %collective-permute-start.6 = (f32[3,512]{1,0:T(4,128)S(1)}, f32[3,512]{1,0:T(4,128)S(1)}, u32[]{:S(2)}, u32[]{:S(2)}) collective-permute-start(f32[3,512]{1,0:T(4,128)S(1)} %get-tuple-element.59), channel_id=1, source_target_pairs={{0,2},{1,3},{2,0},{3,1},{4,6},{5,7},{6,4},{7,5},{8,10},{9,11},{10,... | collective-permute-start | bytes 18440 | tf_op jit(solution)/shard_map/ppermute | solution.py:25
  21.7 6.0 %collective-permute-start.7 = (f32[3,512]{1,0:T(4,128)S(1)}, f32[3,512]{1,0:T(4,128)S(1)}, u32[]{:S(2)}, u32[]{:S(2)}) collective-permute-start(f32[3,512]{1,0:T(4,128)S(1)} %get-tuple-element.60), channel_id=1, source_target_pairs={{0,3},{1,2},{2,1},{3,0},{4,7},{5,6},{6,5},{7,4},{8,11},{9,10},{10,... | collective-permute-start | bytes 18440 | tf_op jit(solution)/shard_map/ppermute | solution.py:25
  24.6 2.3 %copy-start.1 = (bf16[1,512,9,512]{3,1,2,0:T(8,128)(2,1)S(1)}, bf16[1,512,9,512]{3,1,2,0:T(8,128)(2,1)}, u32[]{:S(2)}) copy-start(bf16[1,512,9,512]{3,1,2,0:T(8,128)(2,1)} %param.14) | copy-start | bytes 14155780
  26.9 2.3 %copy-start.2 = (bf16[1,512,9,512]{3,1,2,0:T(8,128)(2,1)S(1)}, bf16[1,512,9,512]{3,1,2,0:T(8,128)(2,1)}, u32[]{:S(2)}) copy-start(bf16[1,512,9,512]{3,1,2,0:T(8,128)(2,1)} %param.14) | copy-start | bytes 14155780
  27.7 1.5 copy-start.5
  29.9 0.7 collective-permute-start.8
  31.2 11.9 %collective-permute-start.9 = (bf16[256,512]{1,0:T(8,128)(2,1)S(1)}, bf16[256,512]{1,0:T(8,128)(2,1)S(1)}, u32[]{:S(2)}, u32[]{:S(2)}) collective-permute-start(bf16[256,512]{1,0:T(8,128)(2,1)S(1)} %get-tuple-element.67), channel_id=1, source_target_pairs={{0,8},{8,16},{1,9},{9,17},{2,10},{10,18},{3,11},{11,19},{4,12},{12... | collective-permute-start | bytes 786440 | tf_op jit(solution)/shard_map/ppermute | solution.py:408
  45.5 7.7 %collective-permute-start.10 = (bf16[256,512]{1,0:T(8,128)(2,1)S(1)}, bf16[256,512]{1,0:T(8,128)(2,1)S(1)}, u32[]{:S(2)}, u32[]{:S(2)}) collective-permute-start(bf16[256,512]{1,0:T(8,128)(2,1)S(1)} %get-tuple-element.70), channel_id=1, source_target_pairs={{0,8},{8,16},{16,24},{1,9},{9,17},{17,25},{2,10},{10,18},{18,26},{... | collective-permute-start | bytes 786440 | tf_op jit(solution)/shard_map/ppermute | solution.py:408
  55.1 7.7 %collective-permute-start.11 = (bf16[256,512]{1,0:T(8,128)(2,1)S(1)}, bf16[256,512]{1,0:T(8,128)(2,1)S(1)}, u32[]{:S(2)}, u32[]{:S(2)}) collective-permute-start(bf16[256,512]{1,0:T(8,128)(2,1)S(1)} %get-tuple-element.74), channel_id=1, source_target_pairs={{8,16},{16,24},{9,17},{17,25},{10,18},{18,26},{11,19},{19,27},{12,... | collective-permute-start | bytes 786440 | tf_op jit(solution)/shard_map/ppermute | solution.py:408
  64.6 2.4 %collective-permute-start.12 = (bf16[256,512]{1,0:T(8,128)(2,1)S(1)}, bf16[256,512]{1,0:T(8,128)(2,1)S(1)}, u32[]{:S(2)}, u32[]{:S(2)}) collective-permute-start(bf16[256,512]{1,0:T(8,128)(2,1)S(1)} %get-tuple-element.78), channel_id=1, source_target_pairs={{16,24},{17,25},{18,26},{19,27},{20,28},{21,29},{22,30},{23,31}} | collective-permute-start | bytes 786440 | tf_op jit(solution)/shard_map/ppermute | solution.py:408
  67.9 6.4 %collective-permute-start.13 = (bf16[256,512]{1,0:T(8,128)(2,1)S(1)}, bf16[256,512]{1,0:T(8,128)(2,1)S(1)}, u32[]{:S(2)}, u32[]{:S(2)}) collective-permute-start(bf16[256,512]{1,0:T(8,128)(2,1)S(1)} %get-tuple-element.83), channel_id=1, source_target_pairs={{24,16},{25,17},{26,18},{27,19},{28,20},{29,21},{30,22},{31,23}} | collective-permute-start | bytes 786440 | tf_op jit(solution)/shard_map/ppermute | solution.py:429
  76.2 5.8 %collective-permute-start.14 = (bf16[256,512]{1,0:T(8,128)(2,1)S(1)}, bf16[256,512]{1,0:T(8,128)(2,1)S(1)}, u32[]{:S(2)}, u32[]{:S(2)}) collective-permute-start(bf16[256,512]{1,0:T(8,128)(2,1)S(1)} %get-tuple-element.85), channel_id=1, source_target_pairs={{16,8},{24,16},{17,9},{25,17},{18,10},{26,18},{19,11},{27,19},{20,... | collective-permute-start | bytes 786440 | tf_op jit(solution)/shard_map/ppermute | solution.py:429
  84.0 7.7 %collective-permute-start.15 = (bf16[256,512]{1,0:T(8,128)(2,1)S(1)}, bf16[256,512]{1,0:T(8,128)(2,1)S(1)}, u32[]{:S(2)}, u32[]{:S(2)}) collective-permute-start(bf16[256,512]{1,0:T(8,128)(2,1)S(1)} %get-tuple-element.87), channel_id=1, source_target_pairs={{8,0},{16,8},{24,16},{9,1},{17,9},{25,17},{10,2},{18,10},{26,18},{... | collective-permute-start | bytes 786440 | tf_op jit(solution)/shard_map/ppermute | solution.py:429
  87.8 22.5 %collective-permute-start.23 = (bf16[17,3,16,512]{3,2,1,0:T(8,128)(2,1)S(1)}, bf16[17,3,16,512]{3,2,1,0:T(8,128)(2,1)S(1)}, u32[]{:S(2)}, u32[]{:S(2)}) collective-permute-start(bf16[17,3,16,512]{3,2,1,0:T(8,128)(2,1)S(1)} %get-tuple-element.98.refs_0_.refs_4_), channel_id=1, source_target_pairs={{0,3},{1,2},{2,1},{3,0},{4,7},{5,6},{6,5},{7,4},{8,11},{9,10},{10,... | collective-permute-start | bytes 2506760 | tf_op jit(solution)/shard_map/ppermute | solution.py:25
  93.6 7.7 %collective-permute-start.16 = (bf16[256,512]{1,0:T(8,128)(2,1)S(1)}, bf16[256,512]{1,0:T(8,128)(2,1)S(1)}, u32[]{:S(2)}, u32[]{:S(2)}) collective-permute-start(bf16[256,512]{1,0:T(8,128)(2,1)S(1)} %get-tuple-element.89), channel_id=1, source_target_pairs={{8,0},{16,8},{9,1},{17,9},{10,2},{18,10},{11,3},{19,11},{12,4},{20... | collective-permute-start | bytes 786440 | tf_op jit(solution)/shard_map/ppermute | solution.py:429
  97.5 29.5 %collective-permute-start.22 = (bf16[17,3,16,512]{3,2,1,0:T(8,128)(2,1)S(1)}, bf16[17,3,16,512]{3,2,1,0:T(8,128)(2,1)S(1)}, u32[]{:S(2)}, u32[]{:S(2)}) collective-permute-start(bf16[17,3,16,512]{3,2,1,0:T(8,128)(2,1)S(1)} %get-tuple-element.98.refs_0_.refs_4_), channel_id=1, source_target_pairs={{0,2},{1,3},{2,0},{3,1},{4,6},{5,7},{6,4},{7,5},{8,10},{9,11},{10,... | collective-permute-start | bytes 2506760 | tf_op jit(solution)/shard_map/ppermute | solution.py:25
  97.8 29.2 %collective-permute-start.21 = (bf16[17,3,16,512]{3,2,1,0:T(8,128)(2,1)S(1)}, bf16[17,3,16,512]{3,2,1,0:T(8,128)(2,1)S(1)}, u32[]{:S(2)}, u32[]{:S(2)}) collective-permute-start(bf16[17,3,16,512]{3,2,1,0:T(8,128)(2,1)S(1)} %get-tuple-element.98.refs_0_.refs_4_), channel_id=1, source_target_pairs={{0,1},{1,0},{2,3},{3,2},{4,5},{5,4},{6,7},{7,6},{8,9},{9,8},{10,11... | collective-permute-start | bytes 2506760 | tf_op jit(solution)/shard_map/ppermute | solution.py:25
  101.4 0.7 collective-permute-start.17
  103.4 29.6 %collective-permute-start.18 = (bf16[128,896]{1,0:T(8,128)(2,1)S(1)}, bf16[128,896]{1,0:T(8,128)(2,1)S(1)}, u32[]{:S(2)}, u32[]{:S(2)}) collective-permute-start(bf16[128,896]{1,0:T(8,128)(2,1)S(1)} %get-tuple-element.95), channel_id=1, source_target_pairs={{0,1},{1,0},{2,3},{3,2},{4,5},{5,4},{6,7},{7,6},{8,9},{9,8},{10,11... | collective-permute-start | bytes 688136 | tf_op jit(solution)/shard_map/ppermute | solution.py:25
  103.7 29.3 %collective-permute-start.19 = (bf16[128,896]{1,0:T(8,128)(2,1)S(1)}, bf16[128,896]{1,0:T(8,128)(2,1)S(1)}, u32[]{:S(2)}, u32[]{:S(2)}) collective-permute-start(bf16[128,896]{1,0:T(8,128)(2,1)S(1)} %get-tuple-element.96), channel_id=1, source_target_pairs={{0,2},{1,3},{2,0},{3,1},{4,6},{5,7},{6,4},{7,5},{8,10},{9,11},{10,... | collective-permute-start | bytes 688136 | tf_op jit(solution)/shard_map/ppermute | solution.py:25
  110.3 25.4 %collective-permute-start.20 = (bf16[128,896]{1,0:T(8,128)(2,1)S(1)}, bf16[128,896]{1,0:T(8,128)(2,1)S(1)}, u32[]{:S(2)}, u32[]{:S(2)}) collective-permute-start(bf16[128,896]{1,0:T(8,128)(2,1)S(1)} %get-tuple-element.97), channel_id=1, source_target_pairs={{0,3},{1,2},{2,1},{3,0},{4,7},{5,6},{6,5},{7,4},{8,11},{9,10},{10,... | collective-permute-start | bytes 688136 | tf_op jit(solution)/shard_map/ppermute | solution.py:25
  137.2 19.0 %collective-permute-start.24 = (bf16[1,3,64,512]{3,2,1,0:T(8,128)(2,1)S(1)}, bf16[1,3,64,512]{3,2,1,0:T(8,128)(2,1)S(1)}, u32[]{:S(2)}, u32[]{:S(2)}) collective-permute-start(bf16[1,3,64,512]{3,2,1,0:T(8,128)(2,1)S(1)} %get-tuple-element.100), channel_id=1, source_target_pairs={{0,4},{1,5},{2,6},{3,7},{4,0},{5,1},{6,2},{7,3},{8,12},{9,13},{10,... | collective-permute-start | bytes 589832 | tf_op jit(solution)/shard_map/ppermute | solution.py:25
  141.1 22.4 %collective-permute-start.26 = (bf16[1,3,64,512]{3,2,1,0:T(8,128)(2,1)S(1)}, bf16[1,3,64,512]{3,2,1,0:T(8,128)(2,1)S(1)}, u32[]{:S(2)}, u32[]{:S(2)}) collective-permute-start(bf16[1,3,64,512]{3,2,1,0:T(8,128)(2,1)S(1)} %get-tuple-element.104), channel_id=1, source_target_pairs={{0,4},{1,5},{2,6},{3,7},{4,0},{5,1},{6,2},{7,3},{8,12},{9,13},{10,... | collective-permute-start | bytes 589832 | tf_op jit(solution)/shard_map/ppermute | solution.py:25
  143.2 20.2 %collective-permute-start.25 = (bf16[1,3,64,512]{3,2,1,0:T(8,128)(2,1)S(1)}, bf16[1,3,64,512]{3,2,1,0:T(8,128)(2,1)S(1)}, u32[]{:S(2)}, u32[]{:S(2)}) collective-permute-start(bf16[1,3,64,512]{3,2,1,0:T(8,128)(2,1)S(1)} %get-tuple-element.102), channel_id=1, source_target_pairs={{0,4},{1,5},{2,6},{3,7},{4,0},{5,1},{6,2},{7,3},{8,12},{9,13},{10,... | collective-permute-start | bytes 589832 | tf_op jit(solution)/shard_map/ppermute | solution.py:25
  163.6 1.0 copy-start.8

commit v5 on v4

--- a/solution.py
+++ b/solution.py
@@ -23,6 +23,25 @@
 
 def swap(x, bit, count):
     return lax.ppermute(x, "dp", [(i, i ^ bit) for i in range(count)])
+
+
+def device_flip(value, odd):
+    if odd:
+        return value
+    low, high = value & 1, (value >> 2) & 1
+    return (value & ~5) | (low << 2) | high
+
+
+def own_flip(value, section):
+    return jnp.where(section % 2 == 1, device_flip(value, 1), device_flip(value, 0))
+
+
+def group_swap(x, value, sections, count):
+    pairs = []
+    for section in range(sections):
+        flip = device_flip(value, section % 2)
+        pairs += [(section * count + i, section * count + (i ^ flip)) for i in range(count)]
+    return lax.ppermute(x, ("section", "dp"), pairs)
 
 
 def column_masks(rows, side):
@@ -130,11 +149,10 @@
 
 def forward_kernel(tick, side, micro, *refs):
     if tick:
-        received, start, pack, head, weight = refs[:5]
-        refs = refs[7:]
+        from_core, from_chip, start, pack, head, weight = refs[:6]
+        refs = refs[8:]
     else:
         start, pack, head, weight = refs[:4]
-        received = start
         refs = refs[4:]
     out, kept_in, kept_conv, score, pieces, mod_box, conv_box, sems = refs
     rows = start.shape[0]
@@ -145,10 +163,11 @@
     def _():
         blank_edges(pieces, rows, side)
         style = pack[pl.ds(position, 1), :]
-        source = received[...]
+        source = start[...].astype(F32)
         if tick:
-            source = jnp.where(section == 0, start[...].astype(F32), source.astype(F32))
-        mod = (style * source.astype(F32)).astype(BF16)
+            other = jnp.where(section % 2 == 1, from_core[...].astype(F32), from_chip[...].astype(F32))
+            source = jnp.where(section == 0, source, other)
+        mod = (style * source).astype(BF16)
         mod_box[pl.ds(0, side)] = mod.reshape(side, side, mod.shape[1])
         squared = style * style
         high = squared.astype(BF16).astype(F32)
@@ -173,8 +192,8 @@
 
 def backward_kernel(tick, side, micro, norm_div, *refs):
     if tick:
-        received = refs[0]
-        refs = refs[1:]
+        from_core, from_chip = refs[:2]
+        refs = refs[2:]
     head, pack = refs[:2]
     scores, refs = refs[2 : 2 + micro], refs[2 + micro :]
     kept_conv, weight = refs[:2]
@@ -203,7 +222,8 @@
         unit = (head[...] / norm_div).astype(BF16).astype(F32)
         incoming = jnp.broadcast_to(unit, conv_box.shape)
         if tick:
-            incoming = jnp.where(section == sections - 1, incoming, received[...].astype(F32))
+            other = jnp.where(section % 2 == 0, from_core[...].astype(F32), from_chip[...].astype(F32))
+            incoming = jnp.where(section == sections - 1, incoming, other)
         load.wait()
         conv = conv_box[...]
         pre = demod * conv
@@ -235,14 +255,15 @@
     channels = kept_grad.shape[3]
     rows = side * micro * side
     part = channels // count
-    here = lax.axis_index("dp")
+    here, section = lax.axis_index("dp"), lax.axis_index("section")
     extra = micro * side
     stacked = kept_grad[...].reshape(rows + extra, channels).astype(F32)
     stacked = jnp.concatenate([stacked, jnp.zeros((128 - extra, channels), F32)], axis=0)
     turned[...] = jnp.transpose(stacked).astype(BF16)
     for flip in range(GROUP):
         for slot in range(count // GROUP):
-            source = pl.multiple_of((here ^ flip ^ (slot << GROUP_BITS)) * part, part)
+            block = here ^ own_flip(flip ^ (slot << GROUP_BITS), section)
+            source = pl.multiple_of(block * part, part)
             outs[flip][pl.ds(slot * part, part), :] = turned[pl.ds(source, part), :]
 
 
@@ -269,7 +290,7 @@
     band = micro * side
     tall = rows + 2 * band
     part = channels // count
-    here = lax.axis_index("dp")
+    here, section = lax.axis_index("dp"), lax.axis_index("section")
     slots = count // GROUP
     mixture = None
     for member in range(GROUP):
@@ -289,7 +310,8 @@
             )
             total = term if total is None else total + term
         for slot in range(slots):
-            source = pl.multiple_of((here ^ (slot << GROUP_BITS)) * part, part)
+            block = here ^ own_flip(slot << GROUP_BITS, section)
+            source = pl.multiple_of(block * part, part)
             fixed = total[slot * part : (slot + 1) * part] - weight[
                 pl.ds(tap * channels + source, part), :
             ].astype(F32) * mixture[slot * part : (slot + 1) * part]
@@ -348,7 +370,9 @@
         if stage > GROUP_BITS:
             stay, go = sums
             half //= 2
-    sums = [sums[0]] + [swap(sums[flip], flip, count) for flip in range(1, GROUP)]
+    sums = list(sums)
+    for flip in range(1, GROUP):
+        sums[flip] = swap(sums[flip], flip, count)
     (pack,) = small(style_kernel, [((16, channels), F32)], *sums, latent, style_weight[0], squares)
     head = score_head[None]
     ticks = micro + sections - 1
@@ -367,7 +391,7 @@
     def forward(tick, arrays):
         return pl.pallas_call(
             functools.partial(forward_kernel, tick, side, micro),
-            in_specs=[whole] * 5 + [far] * 2 if tick else [whole] * 4,
+            in_specs=[whole] * 6 + [far] * 2 if tick else [whole] * 4,
             out_specs=[whole, far, far, whole],
             out_shape=[plain, lined, tower, jax.ShapeDtypeStruct((8, 128), F32)],
             scratch_shapes=conv_scratch
@@ -376,14 +400,14 @@
                 VMEM((pixels, channels), F32),
                 pltpu.SemaphoreType.DMA((2,)),
             ],
-            input_output_aliases={5: 1, 6: 2} if tick else {},
+            input_output_aliases={6: 1, 7: 2} if tick else {},
             cost_estimate=conv_cost,
             compiler_params=params(),
             name="forward_conv",
         )(*arrays)
 
     def backward(tick, arrays):
-        fixed = 3 + micro if tick else 2 + micro
+        fixed = 4 + micro if tick else 2 + micro
         return pl.pallas_call(
             functools.partial(backward_kernel, tick, side, micro, norm_div),
             in_specs=[whole] * fixed + [far, whole] + [far] * (1 if tick else 0),
@@ -401,14 +425,18 @@
             name="backward_conv",
         )(*arrays)
 
+    def moved(array, hops):
+        apart = [[hop for hop in hops if min(hop) % 2 == odd] for odd in (0, 1)]
+        chip = lax.ppermute(array, "section", apart[1]) if apart[1] else None
+        core = lax.ppermute(array, "section", apart[0]) if apart[0] else chip
+        return core, (core if chip is None else chip)
+
     scores = []
     kept_in = kept_conv = outgoing = None
     for tick in range(ticks):
         if tick:
-            received = lax.ppermute(
-                outgoing, "section", [(i, i + 1) for i in range(sections - 1) if 0 <= tick - 1 - i < micro]
-            )
-            arrays = (received, first_map, pack, head, flat_out, kept_in, kept_conv)
+            hops = [(i, i + 1) for i in range(sections - 1) if 0 <= tick - 1 - i < micro]
+            arrays = (*moved(outgoing, hops), first_map, pack, head, flat_out, kept_in, kept_conv)
         else:
             arrays = (first_map, pack, head, flat_out)
         outgoing, kept_in, kept_conv, score = forward(tick, arrays)
@@ -421,21 +449,19 @@
 
     mods = [kept_in]
     for flip in range(1, GROUP):
-        mods.append(swap(kept_in, flip, count))
+        mods.append(group_swap(kept_in, flip, sections, count))
     kept_grad = outgoing = None
     for tick in range(ticks):
         arrays = (head, pack, *scores, kept_conv, flat_out)
         if tick:
-            received = lax.ppermute(
-                outgoing, "section",
-                [(i, i - 1) for i in range(1, sections) if 0 <= tick - 1 - (sections - 1 - i) < micro],
-            )
-            arrays = (received, *arrays, kept_grad)
+            hops = [(i, i - 1) for i in range(1, sections) if 0 <= tick - 1 - (sections - 1 - i) < micro]
+            received = moved(outgoing, hops)
+            arrays = (*received, *arrays, kept_grad)
         outgoing, kept_grad = backward(tick, arrays)
 
     part = channels // count
     own = channels // GROUP
-    chunks = ((0, 1, 2), (3, 4, 5), (6, 7, 8))
+    chunks = ((0, 1, 2, 3), (4, 5, 6), (7, 8))
     wide = micro * pixels + 128
     packed = pl.pallas_call(
         functools.partial(pack_kernel, micro, side, count),
@@ -449,7 +475,7 @@
     )(kept_grad)
     grads = [packed[0]]
     for flip in range(1, GROUP):
-        grads.append(swap(packed[flip], flip, count))
+        grads.append(group_swap(packed[flip], flip, sections, count))
     slots = count // GROUP
     pieces = pl.pallas_call(
         functools.partial(shift_kernel, micro, side),
@@ -481,7 +507,7 @@
         keep, send = pairs[2 * chunk], pairs[2 * chunk + 1]
         half = slots // 2
         while True:
-            total = keep + swap(send, half << GROUP_BITS, count).astype(F32)
+            total = keep + group_swap(send, half << GROUP_BITS, sections, count).astype(F32)
             half //= 2
             if not half:
                 break

time: 165 us -> 167 us (1.012)
  the two profiles are of different devices: /device:TPU:2 before, /device:TPU:3 now
where the time goes in v5:
time: 167 us
  waiting for transfers between devices  96 us (57%)
  starting transfers between devices  37.1 us (22%)
  Pallas kernels  25.1 us (15%)
  local copies, waits for them, and re-layouts  6.49 us (4%)
    ppermute x9, waiting for transfers between devices, group_swap(): return lax.ppermute(x, ('section', 'dp'), pairs)  59.4 us
    ppermute x10, waiting for transfers between devices, moved(): core = lax.ppermute(array, 'section', apart[0]) if apart[0] else chip  32.4 us
    ppermute x10, starting transfers between devices, moved(): core = lax.ppermute(array, 'section', apart[0]) if apart[0] else chip  16.7 us
    ppermute x8, starting transfers between devices, swap(): return lax.ppermute(x, 'dp', [(i, i ^ bit) for i in range(count)])  9.98 us
    pallas_call x6, Pallas kernels, forward(): pl.pallas_call(functools.partial(forward_kernel, tick, side, micro), in_s...  8.24 us
    pallas_call x6, Pallas kernels, backward(): pl.pallas_call(functools.partial(backward_kernel, tick, side, micro, norm...  6.88 us
    ppermute x9, starting transfers between devices, group_swap(): return lax.ppermute(x, ('section', 'dp'), pairs)  6.36 us
    unnamed x26, local copies, waits for them, and re-layouts  5.91 us
  transfers between devices with their start and end apart: 33, of which 16 were waited for; matrix products, arithmetic and copies ran while one was open for 1% of the time, Pallas kernels for 4%

profile of v5, /device:TPU:3, one launch (start us, length us, event | category | flops | bytes accessed | tf_op | source)
XLA Modules:
  0.0 166.8 jit_solution(1961387850000487760)
XLA Ops:
  0.0 1.3 collective-permute-start.1
  1.3 1.2 collective-permute-start
  2.7 0.7 compare_and_fusion
  3.3 0.8 collective-permute-done.refs_1_
  4.1 2.0 %collective-permute-done.2.refs_3_ = s32[3,77]{1,0:T(4,128)S(1)} collective-permute-done((s32[3,77]{1,0:T(4,128)}, s32[3,77]{1,0:T(4,128)S(1)}, u32[]{:S(2)}, u32[]{:S(2)}) %collective-permute-start.2) | collective-permute-done | bytes 956 | tf_op jit(solution)/shard_map/ppermute | solution.py:25
  6.1 0.7 copy-done.7
  6.8 2.3 %collective-permute-start.3 = (s32[12,77]{1,0:T(8,128)S(1)}, s32[12,77]{1,0:T(8,128)S(1)}, u32[]{:S(2)}, u32[]{:S(2)}) collective-permute-start(s32[12,77]{1,0:T(8,128)S(1)} %shard_map.82.ids), channel_id=1, source_target_pairs={{0,4},{1,5},{2,6},{3,7},{4,0},{5,1},{6,2},{7,3},{8,12},{9,13},{10,... | collective-permute-start | bytes 11096 | tf_op jit(solution)/shard_map/ppermute | solution.py:25
  9.1 0.7 compare_select_fusion
  9.7 0.4 collective-permute-done.3.other_ids
  10.2 1.4 copy-done.3
  11.6 1.4 shard_map.83
  13.0 2.3 %collective-permute-start.4 = (f32[12,512]{1,0:T(8,128)S(1)}, f32[12,512]{1,0:T(8,128)S(1)}, u32[]{:S(2)}, u32[]{:S(2)}) collective-permute-start(f32[12,512]{1,0:T(8,128)S(1)} %get-tuple-element.56), channel_id=1, source_target_pairs={{0,4},{1,5},{2,6},{3,7},{4,0},{5,1},{6,2},{7,3},{8,12},{9,13},{10,... | collective-permute-start | bytes 73736 | tf_op jit(solution)/shard_map/ppermute | solution.py:25
  15.3 0.6 gather_fusion
  15.9 1.0 collective-permute-done.4.two
  17.2 2.4 %collective-permute-start.7 = (f32[3,512]{1,0:T(4,128)S(1)}, f32[3,512]{1,0:T(4,128)S(1)}, u32[]{:S(2)}, u32[]{:S(2)}) collective-permute-start(f32[3,512]{1,0:T(4,128)S(1)} %get-tuple-element.60), channel_id=1, source_target_pairs={{0,3},{1,2},{2,1},{3,0},{4,7},{5,6},{6,5},{7,4},{8,11},{9,10},{10,... | collective-permute-start | bytes 18440 | tf_op jit(solution)/shard_map/ppermute | solution.py:25
  19.7 2.3 %copy-done.1 = bf16[1,512,9,512]{3,1,2,0:T(8,128)(2,1)S(1)} copy-done((bf16[1,512,9,512]{3,1,2,0:T(8,128)(2,1)S(1)}, bf16[1,512,9,512]{3,1,2,0:T(8,128)(2,1)}, u32[]{:S(2)}) %copy-start.1) | copy-done | bytes 4718616
  22.1 0.8 shard_map.85
  22.9 1.1 shard_map.86.refs_1_.refs_3_
  24.4 0.6 forward_conv.6
  25.0 0.7 collective-permute-start.8
  25.7 0.6 forward_conv.7
  26.3 0.7 collective-permute-start.10
  27.0 0.7 collective-permute-start.9
  27.7 0.6 forward_conv.8
  28.4 0.7 collective-permute-start.12
  29.1 1.3 collective-permute-start.11
  30.4 18.9 %collective-permute-done.11.refs_0_ = bf16[256,512]{1,0:T(8,128)(2,1)S(1)} collective-permute-done((bf16[256,512]{1,0:T(8,128)(2,1)S(1)}, bf16[256,512]{1,0:T(8,128)(2,1)S(1)}, u32[]{:S(2)}, u32[]{:S(2)}) %collective-permute-start.11) | collective-permute-done | bytes 262176 | tf_op jit(solution)/shard_map/ppermute | solution.py:431
  49.3 1.9 %forward_conv.9 = (bf16[256,512]{1,0:T(8,128)(2,1)S(1)}, bf16[17,3,16,512]{3,2,1,0:T(8,128)(2,1)S(1)}, f32[3,256,512]{2,1,0:T(8,128)S(1)}, f32[8,128]{1,0:T(8,128)S(1)}) custom-call(bf16[256,512]{1,0:T(8,128)(2,1)S(1)} %collective-permute-done.11.refs_0_, ...), custom_call_target="tpu_custom_call", output_to_operand_aliasing={{1}: (6, {}), {2}: (7, {})} | custom-call | flops 1207959552 | bytes 6029312 | tf_op jit(solution)/shard_map/forward_conv/pallas_call | solution.py:392
  51.2 0.7 collective-permute-start.14
  51.9 1.3 collective-permute-start.13
  53.2 5.7 %collective-permute-done.13.refs_0_ = bf16[256,512]{1,0:T(8,128)(2,1)S(1)} collective-permute-done((bf16[256,512]{1,0:T(8,128)(2,1)S(1)}, bf16[256,512]{1,0:T(8,128)(2,1)S(1)}, u32[]{:S(2)}, u32[]{:S(2)}) %collective-permute-start.13) | collective-permute-done | bytes 262176 | tf_op jit(solution)/shard_map/ppermute | solution.py:431
  58.9 1.9 %forward_conv.10 = (bf16[256,512]{1,0:T(8,128)(2,1)S(1)}, bf16[17,3,16,512]{3,2,1,0:T(8,128)(2,1)S(1)}, f32[3,256,512]{2,1,0:T(8,128)S(1)}, f32[8,128]{1,0:T(8,128)S(1)}) custom-call(bf16[256,512]{1,0:T(8,128)(2,1)S(1)} %collective-permute-done.13.refs_0_, ...), custom_call_target="tpu_custom_call", output_to_operand_aliasing={{1}: (6, {}), {2}: (7, {})} | custom-call | flops 1207959552 | bytes 6029312 | tf_op jit(solution)/shard_map/forward_conv/pallas_call | solution.py:392
  60.8 1.3 collective-permute-start.15
  62.1 5.1 %collective-permute-done.15.refs_0_.refs_1_ = bf16[256,512]{1,0:T(8,128)(2,1)S(1)} collective-permute-done((bf16[256,512]{1,0:T(8,128)(2,1)S(1)}, bf16[256,512]{1,0:T(8,128)(2,1)S(1)}, u32[]{:S(2)}, u32[]{:S(2)}) %collective-permute-start.15) | collective-permute-done | bytes 262176 | tf_op jit(solution)/shard_map/ppermute | solution.py:431
  67.2 2.6 %forward_conv.11 = (bf16[256,512]{1,0:T(8,128)(2,1)}, bf16[17,3,16,512]{3,2,1,0:T(8,128)(2,1)S(1)}, f32[3,256,512]{2,1,0:T(8,128)S(1)}, f32[8,128]{1,0:T(8,128)S(1)}) custom-call(bf16[256,512]{1,0:T(8,128)(2,1)S(1)} %collective-permute-done.15.refs_0_.refs_1_, ...), custom_call_target="tpu_custom_call", output_to_operand_aliasing={{1}: (6, {}), {2}: (7, {})} | custom-call | flops 1207959552 | bytes 6029312 | tf_op jit(solution)/shard_map/forward_conv/pallas_call | solution.py:392
  69.8 1.9 %backward_conv.6 = (bf16[256,512]{1,0:T(8,128)(2,1)S(1)}, bf16[17,3,16,512]{3,2,1,0:T(8,128)(2,1)S(1)}) custom-call(f32[1,512]{1,0:T(1,128)S(1)} %bitcast.67, f32[16,512]{1,0:T(8,128)S(1)} %shard_map.86.refs_1_.refs_3_, f32[8,128]{1,0:T(8,128)S(1)} %get-tuple-element.73.refs_2_.refs_4_, f32[8,128]{1,0:T(8,128)S(1)} %get-tuple-element.77.refs_3_.refs_5_, ...), custom_call_target="tpu_custom_call" | custom-call | flops 1207959552 | bytes 6029312 | tf_op jit(solution)/shard_map/backward_conv/pallas_call | solution.py:411
  71.7 1.3 collective-permute-start.16
  73.0 1.1 collective-permute-done.16.refs_0_.refs_1_
  74.1 2.0 %backward_conv.7 = (bf16[256,512]{1,0:T(8,128)(2,1)S(1)}, bf16[17,3,16,512]{3,2,1,0:T(8,128)(2,1)S(1)}) custom-call(bf16[256,512]{1,0:T(8,128)(2,1)S(1)} %collective-permute-done.16.refs_0_.refs_1_, bf16[256,512]{1,0:T(8,128)(2,1)S(1)} %collective-permute-done.16.refs_0_.refs_1_, f32[1,512]{1,0:T(1,128)S(1)} %bitcast.68, ...), custom_call_target="tpu_custom_call", output_to_operand_aliasing={{1}: (9, {})} | custom-call | flops 1207959552 | bytes 6029312 | tf_op jit(solution)/shard_map/backward_conv/pallas_call | solution.py:411
  76.1 0.7 collective-permute-start.18
  76.8 2.9 %collective-permute-start.17 = (bf16[256,512]{1,0:T(8,128)(2,1)S(1)}, bf16[256,512]{1,0:T(8,128)(2,1)S(1)}, u32[]{:S(2)}, u32[]{:S(2)}) collective-permute-start(bf16[256,512]{1,0:T(8,128)(2,1)S(1)} %get-tuple-element.85), channel_id=1, source_target_pairs={{24,16},{25,17},{26,18},{27,19},{28,20},{29,21},{30,22},{31,23}} | collective-permute-start | bytes 786440 | tf_op jit(solution)/shard_map/ppermute | solution.py:431
  79.8 1.1 collective-permute-done.17.refs_0_
  80.9 2.0 %backward_conv.8 = (bf16[256,512]{1,0:T(8,128)(2,1)S(1)}, bf16[17,3,16,512]{3,2,1,0:T(8,128)(2,1)S(1)}) custom-call(bf16[256,512]{1,0:T(8,128)(2,1)S(1)} %collective-permute-done.17.refs_0_, bf16[256,512]{1,0:T(8,128)(2,1)S(1)} %collective-permute-done.18.refs_1_, f32[1,512]{1,0:T(1,128)S(1)} %bitcast.69, ...), custom_call_target="tpu_custom_call", output_to_operand_aliasing={{1}: (9, {})} | custom-call | flops 1207959552 | bytes 6029312 | tf_op jit(solution)/shard_map/backward_conv/pallas_call | solution.py:411
  82.9 0.7 collective-permute-start.20
  83.5 5.9 %collective-permute-start.19 = (bf16[256,512]{1,0:T(8,128)(2,1)S(1)}, bf16[256,512]{1,0:T(8,128)(2,1)S(1)}, u32[]{:S(2)}, u32[]{:S(2)}) collective-permute-start(bf16[256,512]{1,0:T(8,128)(2,1)S(1)} %get-tuple-element.87), channel_id=1, source_target_pairs={{8,0},{24,16},{9,1},{25,17},{10,2},{26,18},{11,3},{27,19},{12,4},{... | collective-permute-start | bytes 786440 | tf_op jit(solution)/shard_map/ppermute | solution.py:431
  89.4 0.7 collective-permute-start.29
  90.6 0.7 collective-permute-start.22
  91.3 0.7 collective-permute-start.21
  92.1 1.5 collective-permute-start.27
  93.6 0.7 collective-permute-start.23
  94.3 1.0 backward_conv.11
  95.8 1.3 collective-permute-start.25
  97.1 30.6 %collective-permute-done.29.refs_3_.refs_7_ = bf16[17,3,16,512]{3,2,1,0:T(8,128)(2,1)S(1)} collective-permute-done((bf16[17,3,16,512]{3,2,1,0:T(8,128)(2,1)S(1)}, bf16[17,3,16,512]{3,2,1,0:T(8,128)(2,1)S(1)}, u32[]{:S(2)}, u32[]{:S(2)}) %collective-permute-start.29) | collective-permute-done | bytes 835616 | tf_op jit(solution)/shard_map/ppermute | solution.py:44
  127.7 13.6 %collective-permute-done.28.refs_2_.refs_6_ = bf16[17,3,16,512]{3,2,1,0:T(8,128)(2,1)S(1)} collective-permute-done((bf16[17,3,16,512]{3,2,1,0:T(8,128)(2,1)S(1)}, bf16[17,3,16,512]{3,2,1,0:T(8,128)(2,1)S(1)}, u32[]{:S(2)}, u32[]{:S(2)}) %collective-permute-start.28) | collective-permute-done | bytes 835616 | tf_op jit(solution)/shard_map/ppermute | solution.py:44
  141.2 1.8 %shift.1.refs_8_ = bf16[3,3456,512]{2,1,0:T(8,128)(2,1)S(1)} custom-call(bf16[17,3,16,512]{3,2,1,0:T(8,128)(2,1)S(1)} %get-tuple-element.98.refs_0_.refs_4_, bf16[17,3,16,512]{3,2,1,0:T(8,128)(2,1)S(1)} %collective-permute-done.27.refs_1_.refs_5_, bf16[17,3,16,512]{3,2,1,0:T(8,128)(2,1)S(1)} %collective-permute-done.28.refs_2_.refs_6_, ...), custom_call_target="tpu_custom_call" | custom-call | bytes 16777216 | tf_op jit(solution)/shard_map/shift/pallas_call | solution.py:480
  143.1 0.6 collective-permute-done.25.refs_2_
  143.7 3.7 %collective-permute-done.26.refs_3_ = bf16[128,896]{1,0:T(8,128)(2,1)S(1)} collective-permute-done((bf16[128,896]{1,0:T(8,128)(2,1)S(1)}, bf16[128,896]{1,0:T(8,128)(2,1)S(1)}, u32[]{:S(2)}, u32[]{:S(2)}) %collective-permute-start.26) | collective-permute-done | bytes 229408 | tf_op jit(solution)/shard_map/ppermute | solution.py:44
  147.4 1.1 weight_grad.5
  148.6 1.5 weight_grad.4
  150.1 2.4 %collective-permute-start.31 = (bf16[1,3,64,512]{3,2,1,0:T(8,128)(2,1)S(1)}, bf16[1,3,64,512]{3,2,1,0:T(8,128)(2,1)S(1)}, u32[]{:S(2)}, u32[]{:S(2)}) collective-permute-start(bf16[1,3,64,512]{3,2,1,0:T(8,128)(2,1)S(1)} %get-tuple-element.102), channel_id=1, source_target_pairs={{0,1},{1,0},{2,3},{3,2},{4,5},{5,4},{6,7},{7,6},{8,12},{9,13},{10,... | collective-permute-start | bytes 589832 | tf_op jit(solution)/shard_map/ppermute | solution.py:44
  152.5 1.9 %weight_grad.3 = (f32[1,4,64,512]{3,2,1,0:T(8,128)S(1)}, bf16[1,4,64,512]{3,2,1,0:T(8,128)(2,1)S(1)}) custom-call(bf16[128,896]{1,0:T(8,128)(2,1)S(1)} %get-tuple-element.94.refs_0_, bf16[128,896]{1,0:T(8,128)(2,1)S(1)} %collective-permute-done.24.refs_1_, bf16[128,896]{1,0:T(8,128)(2,1)S(1)} %collective-permute-done.25.refs_2_, ...), custom_call_target="tpu_custom_call" | custom-call | flops 1207959552 | bytes 5242880 | tf_op jit(solution)/shard_map/weight_grad/pallas_call | solution.py:491
  154.5 2.4 %collective-permute-done.31 = bf16[1,3,64,512]{3,2,1,0:T(8,128)(2,1)S(1)} collective-permute-done((bf16[1,3,64,512]{3,2,1,0:T(8,128)(2,1)S(1)}, bf16[1,3,64,512]{3,2,1,0:T(8,128)(2,1)S(1)}, u32[]{:S(2)}, u32[]{:S(2)}) %collective-permute-start.31) | collective-permute-done | bytes 196640 | tf_op jit(solution)/shard_map/ppermute | solution.py:44
  157.0 8.5 %collective-permute-done.30 = bf16[1,4,64,512]{3,2,1,0:T(8,128)(2,1)S(1)} collective-permute-done((bf16[1,4,64,512]{3,2,1,0:T(8,128)(2,1)S(1)}, bf16[1,4,64,512]{3,2,1,0:T(8,128)(2,1)S(1)}, u32[]{:S(2)}, u32[]{:S(2)}) %collective-permute-start.30) | collective-permute-done | bytes 262176 | tf_op jit(solution)/shard_map/ppermute | solution.py:44
  165.7 1.0 copy-done.8
  (59 shorter events, 2.4 us)
Async XLA Ops:
  0.0 15.3 %copy-start = (f32[1024,512]{1,0:T(8,128)S(1)}, f32[1024,512]{1,0:T(8,128)}, u32[]{:S(2)}) copy-start(f32[1024,512]{1,0:T(8,128)} %param.11) | copy-start | bytes 6291460
  0.0 3.3 %collective-permute-start.1 = (s32[3,77]{1,0:T(4,128)}, s32[3,77]{1,0:T(4,128)S(1)}, u32[]{:S(2)}, u32[]{:S(2)}) collective-permute-start(s32[3,77]{1,0:T(4,128)} %refs_0_.1), channel_id=1, source_target_pairs={{0,2},{1,3},{2,0},{3,1},{4,6},{5,7},{6,4},{7,5},{8,10},{9,11},{10,... | collective-permute-start | bytes 2780 | tf_op jit(solution)/shard_map/ppermute | solution.py:25
  1.3 2.8 %collective-permute-start = (s32[3,77]{1,0:T(4,128)}, s32[3,77]{1,0:T(4,128)S(1)}, u32[]{:S(2)}, u32[]{:S(2)}) collective-permute-start(s32[3,77]{1,0:T(4,128)} %refs_0_.1), channel_id=1, source_target_pairs={{0,1},{1,0},{2,3},{3,2},{4,5},{5,4},{6,7},{7,6},{8,9},{9,8},{10,11... | collective-permute-start | bytes 2780 | tf_op jit(solution)/shard_map/ppermute | solution.py:25
  2.5 3.5 %collective-permute-start.2 = (s32[3,77]{1,0:T(4,128)}, s32[3,77]{1,0:T(4,128)S(1)}, u32[]{:S(2)}, u32[]{:S(2)}) collective-permute-start(s32[3,77]{1,0:T(4,128)} %refs_0_.1), channel_id=1, source_target_pairs={{0,3},{1,2},{2,1},{3,0},{4,7},{5,6},{6,5},{7,4},{8,11},{9,10},{10,... | collective-permute-start | bytes 2780 | tf_op jit(solution)/shard_map/ppermute | solution.py:25
  6.1 0.7 copy-start.7
  6.8 3.4 %collective-permute-start.3 = (s32[12,77]{1,0:T(8,128)S(1)}, s32[12,77]{1,0:T(8,128)S(1)}, u32[]{:S(2)}, u32[]{:S(2)}) collective-permute-start(s32[12,77]{1,0:T(8,128)S(1)} %shard_map.82.ids), channel_id=1, source_target_pairs={{0,4},{1,5},{2,6},{3,7},{4,0},{5,1},{6,2},{7,3},{8,12},{9,13},{10,... | collective-permute-start | bytes 11096 | tf_op jit(solution)/shard_map/ppermute | solution.py:25
  10.2 1.4 copy-start.3
  11.6 8.1 %copy-start.6 = (bf16[512,256]{1,0:T(8,128)(2,1)S(1)}, bf16[512,256]{1,0:T(8,128)(2,1)}, u32[]{:S(2)}) copy-start(bf16[512,256]{1,0:T(8,128)(2,1)} %start.1) | copy-start | bytes 786436
  11.6 11.3 %copy-start.4 = (bf16[1,512,512]{2,1,0:T(8,128)(2,1)S(1)}, bf16[1,512,512]{2,1,0:T(8,128)(2,1)}, u32[]{:S(2)}) copy-start(bf16[1,512,512]{2,1,0:T(8,128)(2,1)} %param.13) | copy-start | bytes 1572868
  13.0 3.9 %collective-permute-start.4 = (f32[12,512]{1,0:T(8,128)S(1)}, f32[12,512]{1,0:T(8,128)S(1)}, u32[]{:S(2)}, u32[]{:S(2)}) collective-permute-start(f32[12,512]{1,0:T(8,128)S(1)} %get-tuple-element.56), channel_id=1, source_target_pairs={{0,4},{1,5},{2,6},{3,7},{4,0},{5,1},{6,2},{7,3},{8,12},{9,13},{10,... | collective-permute-start | bytes 73736 | tf_op jit(solution)/shard_map/ppermute | solution.py:25
  16.9 6.0 %collective-permute-start.5 = (f32[3,512]{1,0:T(4,128)S(1)}, f32[3,512]{1,0:T(4,128)S(1)}, u32[]{:S(2)}, u32[]{:S(2)}) collective-permute-start(f32[3,512]{1,0:T(4,128)S(1)} %get-tuple-element.58), channel_id=1, source_target_pairs={{0,1},{1,0},{2,3},{3,2},{4,5},{5,4},{6,7},{7,6},{8,9},{9,8},{10,11... | collective-permute-start | bytes 18440 | tf_op jit(solution)/shard_map/ppermute | solution.py:25
  17.2 5.7 %collective-permute-start.6 = (f32[3,512]{1,0:T(4,128)S(1)}, f32[3,512]{1,0:T(4,128)S(1)}, u32[]{:S(2)}, u32[]{:S(2)}) collective-permute-start(f32[3,512]{1,0:T(4,128)S(1)} %get-tuple-element.59), channel_id=1, source_target_pairs={{0,2},{1,3},{2,0},{3,1},{4,6},{5,7},{6,4},{7,5},{8,10},{9,11},{10,... | collective-permute-start | bytes 18440 | tf_op jit(solution)/shard_map/ppermute | solution.py:25
  17.2 5.7 %collective-permute-start.7 = (f32[3,512]{1,0:T(4,128)S(1)}, f32[3,512]{1,0:T(4,128)S(1)}, u32[]{:S(2)}, u32[]{:S(2)}) collective-permute-start(f32[3,512]{1,0:T(4,128)S(1)} %get-tuple-element.60), channel_id=1, source_target_pairs={{0,3},{1,2},{2,1},{3,0},{4,7},{5,6},{6,5},{7,4},{8,11},{9,10},{10,... | collective-permute-start | bytes 18440 | tf_op jit(solution)/shard_map/ppermute | solution.py:25
  19.7 2.3 %copy-start.1 = (bf16[1,512,9,512]{3,1,2,0:T(8,128)(2,1)S(1)}, bf16[1,512,9,512]{3,1,2,0:T(8,128)(2,1)}, u32[]{:S(2)}) copy-start(bf16[1,512,9,512]{3,1,2,0:T(8,128)(2,1)} %param.14) | copy-start | bytes 14155780
  22.1 2.3 %copy-start.2 = (bf16[1,512,9,512]{3,1,2,0:T(8,128)(2,1)S(1)}, bf16[1,512,9,512]{3,1,2,0:T(8,128)(2,1)}, u32[]{:S(2)}) copy-start(bf16[1,512,9,512]{3,1,2,0:T(8,128)(2,1)} %param.14) | copy-start | bytes 14155780
  22.9 1.5 copy-start.5
  25.0 0.7 collective-permute-start.8
  26.3 1.4 collective-permute-start.10
  27.0 0.7 collective-permute-start.9
  28.4 2.0 %collective-permute-start.12 = (bf16[256,512]{1,0:T(8,128)(2,1)S(1)}, bf16[256,512]{1,0:T(8,128)(2,1)S(1)}, u32[]{:S(2)}, u32[]{:S(2)}) collective-permute-start(bf16[256,512]{1,0:T(8,128)(2,1)S(1)} %get-tuple-element.70), channel_id=1, source_target_pairs={{8,16},{9,17},{10,18},{11,19},{12,20},{13,21},{14,22},{15,23}} | collective-permute-start | bytes 786440 | tf_op jit(solution)/shard_map/ppermute | solution.py:430
  29.1 20.2 %collective-permute-start.11 = (bf16[256,512]{1,0:T(8,128)(2,1)S(1)}, bf16[256,512]{1,0:T(8,128)(2,1)S(1)}, u32[]{:S(2)}, u32[]{:S(2)}) collective-permute-start(bf16[256,512]{1,0:T(8,128)(2,1)S(1)} %get-tuple-element.70), channel_id=1, source_target_pairs={{0,8},{16,24},{1,9},{17,25},{2,10},{18,26},{3,11},{19,27},{4,12},{... | collective-permute-start | bytes 786440 | tf_op jit(solution)/shard_map/ppermute | solution.py:431
  51.2 2.0 %collective-permute-start.14 = (bf16[256,512]{1,0:T(8,128)(2,1)S(1)}, bf16[256,512]{1,0:T(8,128)(2,1)S(1)}, u32[]{:S(2)}, u32[]{:S(2)}) collective-permute-start(bf16[256,512]{1,0:T(8,128)(2,1)S(1)} %get-tuple-element.74), channel_id=1, source_target_pairs={{8,16},{9,17},{10,18},{11,19},{12,20},{13,21},{14,22},{15,23}} | collective-permute-start | bytes 786440 | tf_op jit(solution)/shard_map/ppermute | solution.py:430
  51.9 7.0 %collective-permute-start.13 = (bf16[256,512]{1,0:T(8,128)(2,1)S(1)}, bf16[256,512]{1,0:T(8,128)(2,1)S(1)}, u32[]{:S(2)}, u32[]{:S(2)}) collective-permute-start(bf16[256,512]{1,0:T(8,128)(2,1)S(1)} %get-tuple-element.74), channel_id=1, source_target_pairs={{16,24},{17,25},{18,26},{19,27},{20,28},{21,29},{22,30},{23,31}} | collective-permute-start | bytes 786440 | tf_op jit(solution)/shard_map/ppermute | solution.py:431
  60.8 6.4 %collective-permute-start.15 = (bf16[256,512]{1,0:T(8,128)(2,1)S(1)}, bf16[256,512]{1,0:T(8,128)(2,1)S(1)}, u32[]{:S(2)}, u32[]{:S(2)}) collective-permute-start(bf16[256,512]{1,0:T(8,128)(2,1)S(1)} %get-tuple-element.78), channel_id=1, source_target_pairs={{16,24},{17,25},{18,26},{19,27},{20,28},{21,29},{22,30},{23,31}} | collective-permute-start | bytes 786440 | tf_op jit(solution)/shard_map/ppermute | solution.py:431
  71.7 2.4 %collective-permute-start.16 = (bf16[256,512]{1,0:T(8,128)(2,1)S(1)}, bf16[256,512]{1,0:T(8,128)(2,1)S(1)}, u32[]{:S(2)}, u32[]{:S(2)}) collective-permute-start(bf16[256,512]{1,0:T(8,128)(2,1)S(1)} %get-tuple-element.83), channel_id=1, source_target_pairs={{24,16},{25,17},{26,18},{27,19},{28,20},{29,21},{30,22},{31,23}} | collective-permute-start | bytes 786440 | tf_op jit(solution)/shard_map/ppermute | solution.py:431
  76.1 3.6 %collective-permute-start.18 = (bf16[256,512]{1,0:T(8,128)(2,1)S(1)}, bf16[256,512]{1,0:T(8,128)(2,1)S(1)}, u32[]{:S(2)}, u32[]{:S(2)}) collective-permute-start(bf16[256,512]{1,0:T(8,128)(2,1)S(1)} %get-tuple-element.85), channel_id=1, source_target_pairs={{16,8},{17,9},{18,10},{19,11},{20,12},{21,13},{22,14},{23,15}} | collective-permute-start | bytes 786440 | tf_op jit(solution)/shard_map/ppermute | solution.py:430
  76.8 4.1 %collective-permute-start.17 = (bf16[256,512]{1,0:T(8,128)(2,1)S(1)}, bf16[256,512]{1,0:T(8,128)(2,1)S(1)}, u32[]{:S(2)}, u32[]{:S(2)}) collective-permute-start(bf16[256,512]{1,0:T(8,128)(2,1)S(1)} %get-tuple-element.85), channel_id=1, source_target_pairs={{24,16},{25,17},{26,18},{27,19},{28,20},{29,21},{30,22},{31,23}} | collective-permute-start | bytes 786440 | tf_op jit(solution)/shard_map/ppermute | solution.py:431
  82.9 7.3 %collective-permute-start.20 = (bf16[256,512]{1,0:T(8,128)(2,1)S(1)}, bf16[256,512]{1,0:T(8,128)(2,1)S(1)}, u32[]{:S(2)}, u32[]{:S(2)}) collective-permute-start(bf16[256,512]{1,0:T(8,128)(2,1)S(1)} %get-tuple-element.87), channel_id=1, source_target_pairs={{16,8},{17,9},{18,10},{19,11},{20,12},{21,13},{22,14},{23,15}} | collective-permute-start | bytes 786440 | tf_op jit(solution)/shard_map/ppermute | solution.py:430
  83.5 7.0 %collective-permute-start.19 = (bf16[256,512]{1,0:T(8,128)(2,1)S(1)}, bf16[256,512]{1,0:T(8,128)(2,1)S(1)}, u32[]{:S(2)}, u32[]{:S(2)}) collective-permute-start(bf16[256,512]{1,0:T(8,128)(2,1)S(1)} %get-tuple-element.87), channel_id=1, source_target_pairs={{8,0},{24,16},{9,1},{25,17},{10,2},{26,18},{11,3},{27,19},{12,4},{... | collective-permute-start | bytes 786440 | tf_op jit(solution)/shard_map/ppermute | solution.py:431
  89.4 38.3 %collective-permute-start.29 = (bf16[17,3,16,512]{3,2,1,0:T(8,128)(2,1)S(1)}, bf16[17,3,16,512]{3,2,1,0:T(8,128)(2,1)S(1)}, u32[]{:S(2)}, u32[]{:S(2)}) collective-permute-start(bf16[17,3,16,512]{3,2,1,0:T(8,128)(2,1)S(1)} %get-tuple-element.98.refs_0_.refs_4_), channel_id=1, source_target_pairs={{0,6},{1,7},{2,4},{3,5},{4,2},{5,3},{6,0},{7,1},{8,11},{9,10},{10,... | collective-permute-start | bytes 2506760 | tf_op jit(solution)/shard_map/ppermute | solution.py:44
  90.6 3.0 %collective-permute-start.22 = (bf16[256,512]{1,0:T(8,128)(2,1)S(1)}, bf16[256,512]{1,0:T(8,128)(2,1)S(1)}, u32[]{:S(2)}, u32[]{:S(2)}) collective-permute-start(bf16[256,512]{1,0:T(8,128)(2,1)S(1)} %get-tuple-element.89), channel_id=1, source_target_pairs={{16,8},{17,9},{18,10},{19,11},{20,12},{21,13},{22,14},{23,15}} | collective-permute-start | bytes 786440 | tf_op jit(solution)/shard_map/ppermute | solution.py:430
  91.3 2.4 %collective-permute-start.21 = (bf16[256,512]{1,0:T(8,128)(2,1)S(1)}, bf16[256,512]{1,0:T(8,128)(2,1)S(1)}, u32[]{:S(2)}, u32[]{:S(2)}) collective-permute-start(bf16[256,512]{1,0:T(8,128)(2,1)S(1)} %get-tuple-element.89), channel_id=1, source_target_pairs={{8,0},{9,1},{10,2},{11,3},{12,4},{13,5},{14,6},{15,7}} | collective-permute-start | bytes 786440 | tf_op jit(solution)/shard_map/ppermute | solution.py:431
  92.0 49.3 %collective-permute-start.28 = (bf16[17,3,16,512]{3,2,1,0:T(8,128)(2,1)S(1)}, bf16[17,3,16,512]{3,2,1,0:T(8,128)(2,1)S(1)}, u32[]{:S(2)}, u32[]{:S(2)}) collective-permute-start(bf16[17,3,16,512]{3,2,1,0:T(8,128)(2,1)S(1)} %get-tuple-element.98.refs_0_.refs_4_), channel_id=1, source_target_pairs={{0,2},{1,3},{2,0},{3,1},{4,6},{5,7},{6,4},{7,5},{8,10},{9,11},{10,... | collective-permute-start | bytes 2506760 | tf_op jit(solution)/shard_map/ppermute | solution.py:44
  92.1 49.2 %collective-permute-start.27 = (bf16[17,3,16,512]{3,2,1,0:T(8,128)(2,1)S(1)}, bf16[17,3,16,512]{3,2,1,0:T(8,128)(2,1)S(1)}, u32[]{:S(2)}, u32[]{:S(2)}) collective-permute-start(bf16[17,3,16,512]{3,2,1,0:T(8,128)(2,1)S(1)} %get-tuple-element.98.refs_0_.refs_4_), channel_id=1, source_target_pairs={{0,4},{1,5},{2,6},{3,7},{4,0},{5,1},{6,2},{7,3},{8,9},{9,8},{10,11... | collective-permute-start | bytes 2506760 | tf_op jit(solution)/shard_map/ppermute | solution.py:44
  93.6 0.7 collective-permute-start.23
  95.7 47.4 %collective-permute-start.24 = (bf16[128,896]{1,0:T(8,128)(2,1)S(1)}, bf16[128,896]{1,0:T(8,128)(2,1)S(1)}, u32[]{:S(2)}, u32[]{:S(2)}) collective-permute-start(bf16[128,896]{1,0:T(8,128)(2,1)S(1)} %get-tuple-element.95), channel_id=1, source_target_pairs={{0,4},{1,5},{2,6},{3,7},{4,0},{5,1},{6,2},{7,3},{8,9},{9,8},{10,11... | collective-permute-start | bytes 688136 | tf_op jit(solution)/shard_map/ppermute | solution.py:44
  95.8 47.9 %collective-permute-start.25 = (bf16[128,896]{1,0:T(8,128)(2,1)S(1)}, bf16[128,896]{1,0:T(8,128)(2,1)S(1)}, u32[]{:S(2)}, u32[]{:S(2)}) collective-permute-start(bf16[128,896]{1,0:T(8,128)(2,1)S(1)} %get-tuple-element.96), channel_id=1, source_target_pairs={{0,2},{1,3},{2,0},{3,1},{4,6},{5,7},{6,4},{7,5},{8,10},{9,11},{10,... | collective-permute-start | bytes 688136 | tf_op jit(solution)/shard_map/ppermute | solution.py:44
  127.7 19.7 %collective-permute-start.26 = (bf16[128,896]{1,0:T(8,128)(2,1)S(1)}, bf16[128,896]{1,0:T(8,128)(2,1)S(1)}, u32[]{:S(2)}, u32[]{:S(2)}) collective-permute-start(bf16[128,896]{1,0:T(8,128)(2,1)S(1)} %get-tuple-element.97), channel_id=1, source_target_pairs={{0,6},{1,7},{2,4},{3,5},{4,2},{5,3},{6,0},{7,1},{8,11},{9,10},{10,... | collective-permute-start | bytes 688136 | tf_op jit(solution)/shard_map/ppermute | solution.py:44
  148.5 6.0 %collective-permute-start.32 = (bf16[1,2,64,512]{3,2,1,0:T(8,128)(2,1)S(1)}, bf16[1,2,64,512]{3,2,1,0:T(8,128)(2,1)S(1)}, u32[]{:S(2)}, u32[]{:S(2)}) collective-permute-start(bf16[1,2,64,512]{3,2,1,0:T(8,128)(2,1)S(1)} %get-tuple-element.104), channel_id=1, source_target_pairs={{0,1},{1,0},{2,3},{3,2},{4,5},{5,4},{6,7},{7,6},{8,12},{9,13},{10,... | collective-permute-start | bytes 393224 | tf_op jit(solution)/shard_map/ppermute | solution.py:44
  150.1 6.9 %collective-permute-start.31 = (bf16[1,3,64,512]{3,2,1,0:T(8,128)(2,1)S(1)}, bf16[1,3,64,512]{3,2,1,0:T(8,128)(2,1)S(1)}, u32[]{:S(2)}, u32[]{:S(2)}) collective-permute-start(bf16[1,3,64,512]{3,2,1,0:T(8,128)(2,1)S(1)} %get-tuple-element.102), channel_id=1, source_target_pairs={{0,1},{1,0},{2,3},{3,2},{4,5},{5,4},{6,7},{7,6},{8,12},{9,13},{10,... | collective-permute-start | bytes 589832 | tf_op jit(solution)/shard_map/ppermute | solution.py:44
  154.4 11.1 %collective-permute-start.30 = (bf16[1,4,64,512]{3,2,1,0:T(8,128)(2,1)S(1)}, bf16[1,4,64,512]{3,2,1,0:T(8,128)(2,1)S(1)}, u32[]{:S(2)}, u32[]{:S(2)}) collective-permute-start(bf16[1,4,64,512]{3,2,1,0:T(8,128)(2,1)S(1)} %get-tuple-element.100), channel_id=1, source_target_pairs={{0,1},{1,0},{2,3},{3,2},{4,5},{5,4},{6,7},{7,6},{8,12},{9,13},{10,... | collective-permute-start | bytes 786440 | tf_op jit(solution)/shard_map/ppermute | solution.py:44
  165.7 1.0 copy-start.8

commit v6 on v5

--- a/solution.py
+++ b/solution.py
@@ -14,7 +14,7 @@
 F32 = jnp.float32
 BF16 = jnp.bfloat16
 VMEM = pltpu.VMEM
-LIMIT = 32 * 1024 * 1024
+LIMIT = 24 * 1024 * 1024
 
 
 def params():
@@ -36,9 +36,9 @@
     return jnp.where(section % 2 == 1, device_flip(value, 1), device_flip(value, 0))
 
 
-def group_swap(x, value, sections, count):
+def group_swap(x, value, sections, count, chosen=None):
     pairs = []
-    for section in range(sections):
+    for section in range(sections) if chosen is None else chosen:
         flip = device_flip(value, section % 2)
         pairs += [(section * count + i, section * count + (i ^ flip)) for i in range(count)]
     return lax.ppermute(x, ("section", "dp"), pairs)
@@ -268,23 +268,28 @@
 
 
 def shift_kernel(micro, side, *refs):
-    mods, pieces = refs[:GROUP], refs[GROUP]
+    mods, (pieces, lines) = refs[: GROUP + 1], refs[GROUP + 1 :]
     channels = pieces.shape[2]
     rows = side * micro * side
     band = micro * side
+    is_last = lax.axis_index("section") == lax.axis_size("section") - 1
     blank = jnp.zeros((band, channels), BF16)
     for member in range(GROUP):
         base = member * (rows + 2 * band)
         for index in range(3):
             pieces[index, pl.ds(base, band), :] = blank
             pieces[index, pl.ds(base + band + rows, band), :] = blank
-        value = mods[member][pl.ds(0, side)].reshape(rows, channels)
-        put_shifts(pieces, value.astype(F32), side, base + band, rows)
+        value = mods[member][...].reshape(rows + band, channels).astype(F32)
+        if member == GROUP - 1:
+            other = mods[GROUP][...].reshape(rows + band, channels).astype(F32)
+            value = jnp.where(is_last, other, value)
+        lines[pl.ds(member * 128, band), :] = value[rows:].astype(BF16)
+        lines[pl.ds(member * 128 + band, 128 - band), :] = jnp.zeros((128 - band, channels), BF16)
+        put_shifts(pieces, value[:rows], side, base + band, rows)
 
 
 def weight_grad_kernel(micro, side, count, taps, *refs):
-    grads, mods = refs[:GROUP], refs[GROUP : 2 * GROUP]
-    pieces, weight, keep, send = refs[2 * GROUP :]
+    grads, (pieces, lines, weight, keep, send) = refs[:GROUP], refs[GROUP:]
     channels = weight.shape[1]
     rows = side * micro * side
     band = micro * side
@@ -294,10 +299,9 @@
     slots = count // GROUP
     mixture = None
     for member in range(GROUP):
-        squared = mods[member][side].reshape(band, channels).astype(F32)
-        squared = jnp.concatenate([squared, jnp.zeros((128 - band, channels), F32)], axis=0)
         term = jnp.dot(
-            grads[member][:, pl.ds(rows, 128)], squared.astype(BF16), preferred_element_type=F32
+            grads[member][:, pl.ds(rows, 128)], lines[pl.ds(member * 128, 128), :],
+            preferred_element_type=F32,
         )
         mixture = term if mixture is None else mixture + term
     for spot, tap in enumerate(taps):
@@ -319,6 +323,14 @@
                 keep[slot, spot] = fixed
             else:
                 send[slot - slots // 2, spot] = fixed.astype(BF16)
+
+
+def final_kernel(first, keep, got, *refs):
+    out, box, sems = refs[-3:]
+    box[...] = keep[0] + got[0].astype(F32)
+    copy = pltpu.make_async_copy(box, out.at[pl.ds(first, box.shape[0])], sems.at[0])
+    copy.start()
+    copy.wait()
 
 
 def on_device(
@@ -448,8 +460,10 @@
         scores = [jnp.where(section_at == target, new, old) for new, old in zip(passed, scores)]
 
     mods = [kept_in]
-    for flip in range(1, GROUP):
+    for flip in (1, 2):
         mods.append(group_swap(kept_in, flip, sections, count))
+    mods.append(group_swap(kept_in, 3, sections, count, range(sections - 1)))
+    mods.append(group_swap(mods[2], 1, sections, count, (sections - 1,)))
     kept_grad = outgoing = None
     for tick in range(ticks):
         arrays = (head, pack, *scores, kept_conv, flat_out)
@@ -477,20 +491,23 @@
     for flip in range(1, GROUP):
         grads.append(group_swap(packed[flip], flip, sections, count))
     slots = count // GROUP
-    pieces = pl.pallas_call(
+    pieces, lines = pl.pallas_call(
         functools.partial(shift_kernel, micro, side),
-        in_specs=[whole] * GROUP,
-        out_specs=whole,
-        out_shape=jax.ShapeDtypeStruct((3, GROUP * micro * tall, channels), BF16),
+        in_specs=[whole] * (GROUP + 1),
+        out_specs=[whole] * 2,
+        out_shape=[
+            jax.ShapeDtypeStruct((3, GROUP * micro * tall, channels), BF16),
+            jax.ShapeDtypeStruct((GROUP * 128, channels), BF16),
+        ],
         cost_estimate=pl.CostEstimate(flops=0, bytes_accessed=16 * 1024 * 1024, transcendentals=0),
         compiler_params=params(),
         name="shift",
     )(*mods)
     pairs = []
     for taps in chunks:
-        pairs += pl.pallas_call(
+        called = pl.pallas_call(
             functools.partial(weight_grad_kernel, micro, side, count, taps),
-            in_specs=[whole] * (2 * GROUP + 2),
+            in_specs=[whole] * (GROUP + 3),
             out_specs=[whole] * 2,
             out_shape=[
                 jax.ShapeDtypeStruct((slots // 2, len(taps), part, channels), F32),
@@ -501,21 +518,31 @@
             ),
             compiler_params=params(),
             name="weight_grad",
-        )(*grads, *mods, pieces, flat_out)
-    done = [None] * 9
+        )
+        pairs += called(*grads, pieces, lines, flat_out)
+    result = ()
     for chunk, taps in enumerate(chunks):
         keep, send = pairs[2 * chunk], pairs[2 * chunk + 1]
         half = slots // 2
         while True:
-            total = keep + group_swap(send, half << GROUP_BITS, sections, count).astype(F32)
+            got = group_swap(send, half << GROUP_BITS, sections, count)
             half //= 2
             if not half:
                 break
+            total = keep + got.astype(F32)
             keep = total[:half]
             send = total[half:].astype(BF16)
-        for spot, tap in enumerate(taps):
-            done[tap] = total[0, spot]
-    return jnp.stack(done, axis=1)[None]
+        result = pl.pallas_call(
+            functools.partial(final_kernel, taps[0]),
+            in_specs=[whole, whole] + [far] * len(result),
+            out_specs=[far],
+            out_shape=[jax.ShapeDtypeStruct((9, part, channels), F32)],
+            scratch_shapes=[VMEM((len(taps), part, channels), F32), pltpu.SemaphoreType.DMA((1,))],
+            input_output_aliases={2: 0} if result else {},
+            compiler_params=params(),
+            name="final",
+        )(keep, got, *result)
+    return jnp.transpose(result[0], (1, 0, 2))[None]
 
 
 def solution(mesh):

time: 167 us -> 165 us (0.988)
  the two profiles are of different devices: /device:TPU:3 before, /device:TPU:18 now
where the time goes in v6:
time: 165 us; the launch traced here: 164 us
  waiting for transfers between devices  87.6 us (53%)
  starting transfers between devices  41.7 us (25%)
  Pallas kernels  27.8 us (17%)
  local copies, waits for them, and re-layouts  5.38 us (3%)
    ppermute x10, waiting for transfers between devices, group_swap(): return lax.ppermute(x, ('section', 'dp'), pairs)  48 us
    ppermute x6, waiting for transfers between devices, moved(): chip = lax.ppermute(array, 'section', apart[1]) if apart[1] else None  22.1 us
    ppermute x6, starting transfers between devices, moved(): chip = lax.ppermute(array, 'section', apart[1]) if apart[1] else None  12.8 us
    ppermute x8, waiting for transfers between devices, swap(): return lax.ppermute(x, 'dp', [(i, i ^ bit) for i in range(count)])  11.1 us
    ppermute x10, starting transfers between devices, group_swap(): return lax.ppermute(x, ('section', 'dp'), pairs)  10.6 us
    ppermute x10, starting transfers between devices, moved(): core = lax.ppermute(array, 'section', apart[0]) if apart[0] else chip  10.5 us
    pallas_call x6, Pallas kernels, forward(): pl.pallas_call(functools.partial(forward_kernel, tick, side, micro), in_s...  8.26 us
    ppermute x8, starting transfers between devices, swap(): return lax.ppermute(x, 'dp', [(i, i ^ bit) for i in range(count)])  7.72 us
  transfers between devices with their start and end apart: 34, of which 19 were waited for; matrix products, arithmetic and copies ran while one was open for 1% of the time, Pallas kernels for 7%

profile of v6, /device:TPU:18, one launch (start us, length us, event | category | flops | bytes accessed | tf_op | source)
XLA Modules:
  0.0 164.4 jit_solution(1477691857177620442)
XLA Ops:
  0.0 1.6 collective-permute-start.1
  1.6 1.5 collective-permute-start
  3.5 0.7 compare_and_fusion
  4.2 1.2 collective-permute-done.refs_1_
  5.4 2.4 %collective-permute-done.2.refs_3_ = s32[3,77]{1,0:T(4,128)S(1)} collective-permute-done((s32[3,77]{1,0:T(4,128)}, s32[3,77]{1,0:T(4,128)S(1)}, u32[]{:S(2)}, u32[]{:S(2)}) %collective-permute-start.2) | collective-permute-done | bytes 956 | tf_op jit(solution)/shard_map/ppermute | solution.py:25
  7.8 0.7 copy-done.7
  9.5 3.6 %collective-permute-done.3.other_ids = s32[12,77]{1,0:T(8,128)S(1)} collective-permute-done((s32[12,77]{1,0:T(8,128)S(1)}, s32[12,77]{1,0:T(8,128)S(1)}, u32[]{:S(2)}, u32[]{:S(2)}) %collective-permute-start.3) | collective-permute-done | bytes 3728 | tf_op jit(solution)/shard_map/ppermute | solution.py:25
  13.0 1.4 copy-done.3
  14.4 1.4 shard_map.83
  16.8 3.9 %collective-permute-done.4.two = f32[12,512]{1,0:T(8,128)S(1)} collective-permute-done((f32[12,512]{1,0:T(8,128)S(1)}, f32[12,512]{1,0:T(8,128)S(1)}, u32[]{:S(2)}, u32[]{:S(2)}) %collective-permute-start.4) | collective-permute-done | bytes 24608 | tf_op jit(solution)/shard_map/ppermute | solution.py:25
  21.7 2.5 %collective-permute-start.7 = (f32[3,512]{1,0:T(4,128)S(1)}, f32[3,512]{1,0:T(4,128)S(1)}, u32[]{:S(2)}, u32[]{:S(2)}) collective-permute-start(f32[3,512]{1,0:T(4,128)S(1)} %get-tuple-element.62), channel_id=1, source_target_pairs={{0,3},{1,2},{2,1},{3,0},{4,7},{5,6},{6,5},{7,4},{8,11},{9,10},{10,... | collective-permute-start | bytes 18440 | tf_op jit(solution)/shard_map/ppermute | solution.py:25
  24.3 2.3 %copy-done.1 = bf16[1,512,9,512]{3,1,2,0:T(8,128)(2,1)S(1)} copy-done((bf16[1,512,9,512]{3,1,2,0:T(8,128)(2,1)S(1)}, bf16[1,512,9,512]{3,1,2,0:T(8,128)(2,1)}, u32[]{:S(2)}) %copy-start.1) | copy-done | bytes 4718616
  26.7 0.8 shard_map.85
  27.5 1.1 shard_map.86.refs_1_.refs_3_
  29.6 0.7 collective-permute-start.8
  31.0 1.3 collective-permute-start.10
  32.3 0.7 collective-permute-start.9
  33.0 9.3 %collective-permute-done.10.refs_1_ = bf16[256,512]{1,0:T(8,128)(2,1)S(1)} collective-permute-done((bf16[256,512]{1,0:T(8,128)(2,1)S(1)}, bf16[256,512]{1,0:T(8,128)(2,1)S(1)}, u32[]{:S(2)}, u32[]{:S(2)}) %collective-permute-start.10) | collective-permute-done | bytes 262176 | tf_op jit(solution)/shard_map/ppermute | solution.py:442
  42.2 2.5 %forward_conv.8 = (bf16[256,512]{1,0:T(8,128)(2,1)S(1)}, bf16[17,3,16,512]{3,2,1,0:T(8,128)(2,1)S(1)}, f32[3,256,512]{2,1,0:T(8,128)S(1)}, f32[8,128]{1,0:T(8,128)}) custom-call(bf16[256,512]{1,0:T(8,128)(2,1)S(1)} %collective-permute-done.9.refs_0_, ...), custom_call_target="tpu_custom_call", output_to_operand_aliasing={{1}: (6, {}), {2}: (7, {})} | custom-call | flops 1207959552 | bytes 6029312 | tf_op jit(solution)/shard_map/forward_conv/pallas_call | solution.py:404
  44.8 1.3 collective-permute-start.12
  46.1 1.3 collective-permute-start.11
  47.4 5.1 %collective-permute-done.12.refs_1_ = bf16[256,512]{1,0:T(8,128)(2,1)S(1)} collective-permute-done((bf16[256,512]{1,0:T(8,128)(2,1)S(1)}, bf16[256,512]{1,0:T(8,128)(2,1)S(1)}, u32[]{:S(2)}, u32[]{:S(2)}) %collective-permute-start.12) | collective-permute-done | bytes 262176 | tf_op jit(solution)/shard_map/ppermute | solution.py:442
  52.4 1.9 %forward_conv.9 = (bf16[256,512]{1,0:T(8,128)(2,1)S(1)}, bf16[17,3,16,512]{3,2,1,0:T(8,128)(2,1)S(1)}, f32[3,256,512]{2,1,0:T(8,128)S(1)}, f32[8,128]{1,0:T(8,128)S(1)}) custom-call(bf16[256,512]{1,0:T(8,128)(2,1)S(1)} %collective-permute-done.11.refs_0_, ...), custom_call_target="tpu_custom_call", output_to_operand_aliasing={{1}: (6, {}), {2}: (7, {})} | custom-call | flops 1207959552 | bytes 6029312 | tf_op jit(solution)/shard_map/forward_conv/pallas_call | solution.py:404
  54.4 1.3 collective-permute-start.14
  55.7 1.3 collective-permute-start.13
  57.0 5.1 %collective-permute-done.14.refs_1_ = bf16[256,512]{1,0:T(8,128)(2,1)S(1)} collective-permute-done((bf16[256,512]{1,0:T(8,128)(2,1)S(1)}, bf16[256,512]{1,0:T(8,128)(2,1)S(1)}, u32[]{:S(2)}, u32[]{:S(2)}) %collective-permute-start.14) | collective-permute-done | bytes 262176 | tf_op jit(solution)/shard_map/ppermute | solution.py:442
  62.0 1.9 %forward_conv.10 = (bf16[256,512]{1,0:T(8,128)(2,1)S(1)}, bf16[17,3,16,512]{3,2,1,0:T(8,128)(2,1)S(1)}, f32[3,256,512]{2,1,0:T(8,128)S(1)}, f32[8,128]{1,0:T(8,128)S(1)}) custom-call(bf16[256,512]{1,0:T(8,128)(2,1)S(1)} %collective-permute-done.13.refs_0_, ...), custom_call_target="tpu_custom_call", output_to_operand_aliasing={{1}: (6, {}), {2}: (7, {})} | custom-call | flops 1207959552 | bytes 6029312 | tf_op jit(solution)/shard_map/forward_conv/pallas_call | solution.py:404
  64.0 1.3 collective-permute-start.15
  65.3 1.1 collective-permute-done.15.refs_0_.refs_1_
  66.4 0.7 forward_conv.11
  67.2 1.3 collective-permute-start.16
  68.5 5.1 %collective-permute-done.16.refs_0_.refs_1_ = bf16[256,512]{1,0:T(8,128)(2,1)S(1)} collective-permute-done((bf16[256,512]{1,0:T(8,128)(2,1)S(1)}, bf16[256,512]{1,0:T(8,128)(2,1)S(1)}, u32[]{:S(2)}, u32[]{:S(2)}) %collective-permute-start.16) | collective-permute-done | bytes 262176 | tf_op jit(solution)/shard_map/ppermute | solution.py:443
  73.6 2.0 %backward_conv.7 = (bf16[256,512]{1,0:T(8,128)(2,1)S(1)}, bf16[17,3,16,512]{3,2,1,0:T(8,128)(2,1)S(1)}) custom-call(bf16[256,512]{1,0:T(8,128)(2,1)S(1)} %collective-permute-done.16.refs_0_.refs_1_, bf16[256,512]{1,0:T(8,128)(2,1)S(1)} %collective-permute-done.16.refs_0_.refs_1_, f32[1,512]{1,0:T(1,128)S(1)} %bitcast.34, ...), custom_call_target="tpu_custom_call", output_to_operand_aliasing={{1}: (9, {})} | custom-call | flops 1207959552 | bytes 6029312 | tf_op jit(solution)/shard_map/backward_conv/pallas_call | solution.py:423
  75.6 1.3 collective-permute-start.18
  76.9 1.3 collective-permute-start.17
  78.7 2.1 %collective-permute-done.18.refs_1_ = bf16[256,512]{1,0:T(8,128)(2,1)S(1)} collective-permute-done((bf16[256,512]{1,0:T(8,128)(2,1)S(1)}, bf16[256,512]{1,0:T(8,128)(2,1)S(1)}, u32[]{:S(2)}, u32[]{:S(2)}) %collective-permute-start.18) | collective-permute-done | bytes 262176 | tf_op jit(solution)/shard_map/ppermute | solution.py:442
  80.8 2.0 %backward_conv.8 = (bf16[256,512]{1,0:T(8,128)(2,1)S(1)}, bf16[17,3,16,512]{3,2,1,0:T(8,128)(2,1)S(1)}) custom-call(bf16[256,512]{1,0:T(8,128)(2,1)S(1)} %collective-permute-done.17.refs_0_, bf16[256,512]{1,0:T(8,128)(2,1)S(1)} %collective-permute-done.18.refs_1_, f32[1,512]{1,0:T(1,128)S(1)} %bitcast.35, ...), custom_call_target="tpu_custom_call", output_to_operand_aliasing={{1}: (9, {})} | custom-call | flops 1207959552 | bytes 6029312 | tf_op jit(solution)/shard_map/backward_conv/pallas_call | solution.py:423
  82.8 3.8 %collective-permute-start.20 = (bf16[256,512]{1,0:T(8,128)(2,1)S(1)}, bf16[256,512]{1,0:T(8,128)(2,1)S(1)}, u32[]{:S(2)}, u32[]{:S(2)}) collective-permute-start(bf16[256,512]{1,0:T(8,128)(2,1)S(1)} %get-tuple-element.89), channel_id=1, source_target_pairs={{16,8},{17,9},{18,10},{19,11},{20,12},{21,13},{22,14},{23,15}} | collective-permute-start | bytes 786440 | tf_op jit(solution)/shard_map/ppermute | solution.py:442
  86.6 1.3 collective-permute-start.19
  87.9 1.9 %collective-permute-start.29 = (bf16[17,3,16,512]{3,2,1,0:T(8,128)(2,1)S(1)}, bf16[17,3,16,512]{3,2,1,0:T(8,128)(2,1)S(1)}, u32[]{:S(2)}, u32[]{:S(2)}) collective-permute-start(bf16[17,3,16,512]{3,2,1,0:T(8,128)(2,1)S(1)} %get-tuple-element.100.refs_0_), channel_id=1, source_target_pairs={{0,6},{1,7},{2,4},{3,5},{4,2},{5,3},{6,0},{7,1},{8,11},{9,10},{10,... | collective-permute-start | bytes 2506760 | tf_op jit(solution)/shard_map/ppermute | solution.py:44
  90.5 2.0 %backward_conv.9 = (bf16[256,512]{1,0:T(8,128)(2,1)S(1)}, bf16[17,3,16,512]{3,2,1,0:T(8,128)(2,1)S(1)}) custom-call(bf16[256,512]{1,0:T(8,128)(2,1)S(1)} %collective-permute-done.19.refs_0_, bf16[256,512]{1,0:T(8,128)(2,1)S(1)} %collective-permute-done.20.refs_1_, f32[1,512]{1,0:T(1,128)S(1)} %bitcast.36, ...), custom_call_target="tpu_custom_call", output_to_operand_aliasing={{1}: (9, {})} | custom-call | flops 1207959552 | bytes 6029312 | tf_op jit(solution)/shard_map/backward_conv/pallas_call | solution.py:423
  92.4 3.8 %collective-permute-start.22 = (bf16[256,512]{1,0:T(8,128)(2,1)S(1)}, bf16[256,512]{1,0:T(8,128)(2,1)S(1)}, u32[]{:S(2)}, u32[]{:S(2)}) collective-permute-start(bf16[256,512]{1,0:T(8,128)(2,1)S(1)} %get-tuple-element.91), channel_id=1, source_target_pairs={{16,8},{17,9},{18,10},{19,11},{20,12},{21,13},{22,14},{23,15}} | collective-permute-start | bytes 786440 | tf_op jit(solution)/shard_map/ppermute | solution.py:442
  96.3 0.7 collective-permute-start.21
  97.0 0.9 collective-permute-start.27
  97.9 1.7 %collective-permute-done.28.refs_2_ = bf16[17,3,16,512]{3,2,1,0:T(8,128)(2,1)S(1)} collective-permute-done((bf16[17,3,16,512]{3,2,1,0:T(8,128)(2,1)S(1)}, bf16[17,3,16,512]{3,2,1,0:T(8,128)(2,1)S(1)}, u32[]{:S(2)}, u32[]{:S(2)}) %collective-permute-start.28) | collective-permute-done | bytes 835616 | tf_op jit(solution)/shard_map/ppermute | solution.py:44
  99.6 0.7 collective-permute-start.30
  100.3 0.7 collective-permute-start.23
  101.0 1.0 backward_conv.11
  102.4 0.8 collective-permute-start.24
  103.6 12.8 %collective-permute-done.29.refs_3_ = bf16[17,3,16,512]{3,2,1,0:T(8,128)(2,1)S(1)} collective-permute-done((bf16[17,3,16,512]{3,2,1,0:T(8,128)(2,1)S(1)}, bf16[17,3,16,512]{3,2,1,0:T(8,128)(2,1)S(1)}, u32[]{:S(2)}, u32[]{:S(2)}) %collective-permute-start.29) | collective-permute-done | bytes 835616 | tf_op jit(solution)/shard_map/ppermute | solution.py:44
  116.4 2.6 %collective-permute-start.26 = (bf16[128,896]{1,0:T(8,128)(2,1)S(1)}, bf16[128,896]{1,0:T(8,128)(2,1)S(1)}, u32[]{:S(2)}, u32[]{:S(2)}) collective-permute-start(bf16[128,896]{1,0:T(8,128)(2,1)S(1)} %get-tuple-element.99), channel_id=1, source_target_pairs={{0,6},{1,7},{2,4},{3,5},{4,2},{5,3},{6,0},{7,1},{8,11},{9,10},{10,... | collective-permute-start | bytes 688136 | tf_op jit(solution)/shard_map/ppermute | solution.py:44
  119.0 21.4 %collective-permute-done.27.refs_1_ = bf16[17,3,16,512]{3,2,1,0:T(8,128)(2,1)S(1)} collective-permute-done((bf16[17,3,16,512]{3,2,1,0:T(8,128)(2,1)S(1)}, bf16[17,3,16,512]{3,2,1,0:T(8,128)(2,1)S(1)}, u32[]{:S(2)}, u32[]{:S(2)}) %collective-permute-start.27) | collective-permute-done | bytes 835616 | tf_op jit(solution)/shard_map/ppermute | solution.py:44
  140.4 2.0 %shift.1 = (bf16[3,3456,512]{2,1,0:T(8,128)(2,1)S(1)}, bf16[512,512]{1,0:T(8,128)(2,1)S(1)}) custom-call(bf16[17,3,16,512]{3,2,1,0:T(8,128)(2,1)S(1)} %get-tuple-element.100.refs_0_, bf16[17,3,16,512]{3,2,1,0:T(8,128)(2,1)S(1)} %collective-permute-done.27.refs_1_, bf16[17,3,16,512]{3,2,1,0:T(8,128)(2,1)S(1)} %collective-permute-done.28.refs_2_, ...), custom_call_target="tpu_custom_call" | custom-call | bytes 16777216 | tf_op jit(solution)/shard_map/shift/pallas_call | solution.py:494
  142.4 2.9 %collective-permute-done.24.refs_1_ = bf16[128,896]{1,0:T(8,128)(2,1)S(1)} collective-permute-done((bf16[128,896]{1,0:T(8,128)(2,1)S(1)}, bf16[128,896]{1,0:T(8,128)(2,1)S(1)}, u32[]{:S(2)}, u32[]{:S(2)}) %collective-permute-start.24) | collective-permute-done | bytes 229408 | tf_op jit(solution)/shard_map/ppermute | solution.py:44
  145.3 6.3 %collective-permute-done.26.refs_3_ = bf16[128,896]{1,0:T(8,128)(2,1)S(1)} collective-permute-done((bf16[128,896]{1,0:T(8,128)(2,1)S(1)}, bf16[128,896]{1,0:T(8,128)(2,1)S(1)}, u32[]{:S(2)}, u32[]{:S(2)}) %collective-permute-start.26) | collective-permute-done | bytes 229408 | tf_op jit(solution)/shard_map/ppermute | solution.py:44
  151.6 1.9 %weight_grad.5 = (f32[1,4,64,512]{3,2,1,0:T(8,128)S(1)}, bf16[1,4,64,512]{3,2,1,0:T(8,128)(2,1)S(1)}) custom-call(bf16[128,896]{1,0:T(8,128)(2,1)S(1)} %get-tuple-element.96.refs_0_, bf16[128,896]{1,0:T(8,128)(2,1)S(1)} %collective-permute-done.24.refs_1_, bf16[128,896]{1,0:T(8,128)(2,1)S(1)} %collective-permute-done.25.refs_2_, ...), custom_call_target="tpu_custom_call" | custom-call | flops 1207959552 | bytes 5242880 | tf_op jit(solution)/shard_map/weight_grad/pallas_call | solution.py:522
  154.2 1.5 weight_grad.4
  155.7 1.5 collective-permute-start.32
  157.2 1.1 weight_grad.3
  158.9 1.0 collective-permute-done.33.got
  160.0 0.8 final.3.refs_0_
  160.8 1.3 collective-permute-done.32.got
  162.1 0.8 final.4.refs_0_
  163.5 0.7 final.5
  (50 shorter events, 8.9 us)
Async XLA Ops:
  0.0 16.2 %copy-start = (f32[1024,512]{1,0:T(8,128)S(1)}, f32[1024,512]{1,0:T(8,128)}, u32[]{:S(2)}) copy-start(f32[1024,512]{1,0:T(8,128)} %param.11) | copy-start | bytes 6291460
  0.0 4.2 %collective-permute-start.1 = (s32[3,77]{1,0:T(4,128)}, s32[3,77]{1,0:T(4,128)S(1)}, u32[]{:S(2)}, u32[]{:S(2)}) collective-permute-start(s32[3,77]{1,0:T(4,128)} %refs_0_.1), channel_id=1, source_target_pairs={{0,2},{1,3},{2,0},{3,1},{4,6},{5,7},{6,4},{7,5},{8,10},{9,11},{10,... | collective-permute-start | bytes 2780 | tf_op jit(solution)/shard_map/ppermute | solution.py:25
  1.6 3.8 %collective-permute-start = (s32[3,77]{1,0:T(4,128)}, s32[3,77]{1,0:T(4,128)S(1)}, u32[]{:S(2)}, u32[]{:S(2)}) collective-permute-start(s32[3,77]{1,0:T(4,128)} %refs_0_.1), channel_id=1, source_target_pairs={{0,1},{1,0},{2,3},{3,2},{4,5},{5,4},{6,7},{7,6},{8,9},{9,8},{10,11... | collective-permute-start | bytes 2780 | tf_op jit(solution)/shard_map/ppermute | solution.py:25
  3.1 4.7 %collective-permute-start.2 = (s32[3,77]{1,0:T(4,128)}, s32[3,77]{1,0:T(4,128)S(1)}, u32[]{:S(2)}, u32[]{:S(2)}) collective-permute-start(s32[3,77]{1,0:T(4,128)} %refs_0_.1), channel_id=1, source_target_pairs={{0,3},{1,2},{2,1},{3,0},{4,7},{5,6},{6,5},{7,4},{8,11},{9,10},{10,... | collective-permute-start | bytes 2780 | tf_op jit(solution)/shard_map/ppermute | solution.py:25
  7.8 0.7 copy-start.7
  8.5 4.5 %collective-permute-start.3 = (s32[12,77]{1,0:T(8,128)S(1)}, s32[12,77]{1,0:T(8,128)S(1)}, u32[]{:S(2)}, u32[]{:S(2)}) collective-permute-start(s32[12,77]{1,0:T(8,128)S(1)} %shard_map.82.ids), channel_id=1, source_target_pairs={{0,4},{1,5},{2,6},{3,7},{4,0},{5,1},{6,2},{7,3},{8,12},{9,13},{10,... | collective-permute-start | bytes 11096 | tf_op jit(solution)/shard_map/ppermute | solution.py:25
  13.0 1.4 copy-start.3
  14.4 9.9 %copy-start.6 = (bf16[512,256]{1,0:T(8,128)(2,1)S(1)}, bf16[512,256]{1,0:T(8,128)(2,1)}, u32[]{:S(2)}) copy-start(bf16[512,256]{1,0:T(8,128)(2,1)} %start.1) | copy-start | bytes 786436
  14.4 13.1 %copy-start.4 = (bf16[1,512,512]{2,1,0:T(8,128)(2,1)S(1)}, bf16[1,512,512]{2,1,0:T(8,128)(2,1)}, u32[]{:S(2)}) copy-start(bf16[1,512,512]{2,1,0:T(8,128)(2,1)} %param.13) | copy-start | bytes 1572868
  15.9 4.8 %collective-permute-start.4 = (f32[12,512]{1,0:T(8,128)S(1)}, f32[12,512]{1,0:T(8,128)S(1)}, u32[]{:S(2)}, u32[]{:S(2)}) collective-permute-start(f32[12,512]{1,0:T(8,128)S(1)} %get-tuple-element.58), channel_id=1, source_target_pairs={{0,4},{1,5},{2,6},{3,7},{4,0},{5,1},{6,2},{7,3},{8,12},{9,13},{10,... | collective-permute-start | bytes 73736 | tf_op jit(solution)/shard_map/ppermute | solution.py:25
  20.7 6.8 %collective-permute-start.5 = (f32[3,512]{1,0:T(4,128)S(1)}, f32[3,512]{1,0:T(4,128)S(1)}, u32[]{:S(2)}, u32[]{:S(2)}) collective-permute-start(f32[3,512]{1,0:T(4,128)S(1)} %get-tuple-element.60), channel_id=1, source_target_pairs={{0,1},{1,0},{2,3},{3,2},{4,5},{5,4},{6,7},{7,6},{8,9},{9,8},{10,11... | collective-permute-start | bytes 18440 | tf_op jit(solution)/shard_map/ppermute | solution.py:25
  21.3 6.2 %collective-permute-start.6 = (f32[3,512]{1,0:T(4,128)S(1)}, f32[3,512]{1,0:T(4,128)S(1)}, u32[]{:S(2)}, u32[]{:S(2)}) collective-permute-start(f32[3,512]{1,0:T(4,128)S(1)} %get-tuple-element.61), channel_id=1, source_target_pairs={{0,2},{1,3},{2,0},{3,1},{4,6},{5,7},{6,4},{7,5},{8,10},{9,11},{10,... | collective-permute-start | bytes 18440 | tf_op jit(solution)/shard_map/ppermute | solution.py:25
  21.7 5.8 %collective-permute-start.7 = (f32[3,512]{1,0:T(4,128)S(1)}, f32[3,512]{1,0:T(4,128)S(1)}, u32[]{:S(2)}, u32[]{:S(2)}) collective-permute-start(f32[3,512]{1,0:T(4,128)S(1)} %get-tuple-element.62), channel_id=1, source_target_pairs={{0,3},{1,2},{2,1},{3,0},{4,7},{5,6},{6,5},{7,4},{8,11},{9,10},{10,... | collective-permute-start | bytes 18440 | tf_op jit(solution)/shard_map/ppermute | solution.py:25
  24.3 2.3 %copy-start.1 = (bf16[1,512,9,512]{3,1,2,0:T(8,128)(2,1)S(1)}, bf16[1,512,9,512]{3,1,2,0:T(8,128)(2,1)}, u32[]{:S(2)}) copy-start(bf16[1,512,9,512]{3,1,2,0:T(8,128)(2,1)} %param.14) | copy-start | bytes 14155780
  26.7 2.3 %copy-start.2 = (bf16[1,512,9,512]{3,1,2,0:T(8,128)(2,1)S(1)}, bf16[1,512,9,512]{3,1,2,0:T(8,128)(2,1)}, u32[]{:S(2)}) copy-start(bf16[1,512,9,512]{3,1,2,0:T(8,128)(2,1)} %param.14) | copy-start | bytes 14155780
  27.5 1.5 copy-start.5
  29.6 0.7 collective-permute-start.8
  31.0 11.3 %collective-permute-start.10 = (bf16[256,512]{1,0:T(8,128)(2,1)S(1)}, bf16[256,512]{1,0:T(8,128)(2,1)S(1)}, u32[]{:S(2)}, u32[]{:S(2)}) collective-permute-start(bf16[256,512]{1,0:T(8,128)(2,1)S(1)} %get-tuple-element.69), channel_id=1, source_target_pairs={{8,16},{9,17},{10,18},{11,19},{12,20},{13,21},{14,22},{15,23}} | collective-permute-start | bytes 786440 | tf_op jit(solution)/shard_map/ppermute | solution.py:442
  32.3 10.0 %collective-permute-start.9 = (bf16[256,512]{1,0:T(8,128)(2,1)S(1)}, bf16[256,512]{1,0:T(8,128)(2,1)S(1)}, u32[]{:S(2)}, u32[]{:S(2)}) collective-permute-start(bf16[256,512]{1,0:T(8,128)(2,1)S(1)} %get-tuple-element.69), channel_id=1, source_target_pairs={{0,8},{1,9},{2,10},{3,11},{4,12},{5,13},{6,14},{7,15}} | collective-permute-start | bytes 786440 | tf_op jit(solution)/shard_map/ppermute | solution.py:443
  44.8 7.7 %collective-permute-start.12 = (bf16[256,512]{1,0:T(8,128)(2,1)S(1)}, bf16[256,512]{1,0:T(8,128)(2,1)S(1)}, u32[]{:S(2)}, u32[]{:S(2)}) collective-permute-start(bf16[256,512]{1,0:T(8,128)(2,1)S(1)} %get-tuple-element.72), channel_id=1, source_target_pairs={{8,16},{9,17},{10,18},{11,19},{12,20},{13,21},{14,22},{15,23}} | collective-permute-start | bytes 786440 | tf_op jit(solution)/shard_map/ppermute | solution.py:442
  46.1 6.4 %collective-permute-start.11 = (bf16[256,512]{1,0:T(8,128)(2,1)S(1)}, bf16[256,512]{1,0:T(8,128)(2,1)S(1)}, u32[]{:S(2)}, u32[]{:S(2)}) collective-permute-start(bf16[256,512]{1,0:T(8,128)(2,1)S(1)} %get-tuple-element.72), channel_id=1, source_target_pairs={{0,8},{16,24},{1,9},{17,25},{2,10},{18,26},{3,11},{19,27},{4,12},{... | collective-permute-start | bytes 786440 | tf_op jit(solution)/shard_map/ppermute | solution.py:443
  54.4 7.7 %collective-permute-start.14 = (bf16[256,512]{1,0:T(8,128)(2,1)S(1)}, bf16[256,512]{1,0:T(8,128)(2,1)S(1)}, u32[]{:S(2)}, u32[]{:S(2)}) collective-permute-start(bf16[256,512]{1,0:T(8,128)(2,1)S(1)} %get-tuple-element.76), channel_id=1, source_target_pairs={{8,16},{9,17},{10,18},{11,19},{12,20},{13,21},{14,22},{15,23}} | collective-permute-start | bytes 786440 | tf_op jit(solution)/shard_map/ppermute | solution.py:442
  55.7 6.4 %collective-permute-start.13 = (bf16[256,512]{1,0:T(8,128)(2,1)S(1)}, bf16[256,512]{1,0:T(8,128)(2,1)S(1)}, u32[]{:S(2)}, u32[]{:S(2)}) collective-permute-start(bf16[256,512]{1,0:T(8,128)(2,1)S(1)} %get-tuple-element.76), channel_id=1, source_target_pairs={{16,24},{17,25},{18,26},{19,27},{20,28},{21,29},{22,30},{23,31}} | collective-permute-start | bytes 786440 | tf_op jit(solution)/shard_map/ppermute | solution.py:443
  64.0 2.4 %collective-permute-start.15 = (bf16[256,512]{1,0:T(8,128)(2,1)S(1)}, bf16[256,512]{1,0:T(8,128)(2,1)S(1)}, u32[]{:S(2)}, u32[]{:S(2)}) collective-permute-start(bf16[256,512]{1,0:T(8,128)(2,1)S(1)} %get-tuple-element.80), channel_id=1, source_target_pairs={{16,24},{17,25},{18,26},{19,27},{20,28},{21,29},{22,30},{23,31}} | collective-permute-start | bytes 786440 | tf_op jit(solution)/shard_map/ppermute | solution.py:443
  67.2 6.4 %collective-permute-start.16 = (bf16[256,512]{1,0:T(8,128)(2,1)S(1)}, bf16[256,512]{1,0:T(8,128)(2,1)S(1)}, u32[]{:S(2)}, u32[]{:S(2)}) collective-permute-start(bf16[256,512]{1,0:T(8,128)(2,1)S(1)} %get-tuple-element.85), channel_id=1, source_target_pairs={{24,16},{25,17},{26,18},{27,19},{28,20},{29,21},{30,22},{31,23}} | collective-permute-start | bytes 786440 | tf_op jit(solution)/shard_map/ppermute | solution.py:443
  75.6 5.2 %collective-permute-start.18 = (bf16[256,512]{1,0:T(8,128)(2,1)S(1)}, bf16[256,512]{1,0:T(8,128)(2,1)S(1)}, u32[]{:S(2)}, u32[]{:S(2)}) collective-permute-start(bf16[256,512]{1,0:T(8,128)(2,1)S(1)} %get-tuple-element.87), channel_id=1, source_target_pairs={{16,8},{17,9},{18,10},{19,11},{20,12},{21,13},{22,14},{23,15}} | collective-permute-start | bytes 786440 | tf_op jit(solution)/shard_map/ppermute | solution.py:442
  76.9 3.9 %collective-permute-start.17 = (bf16[256,512]{1,0:T(8,128)(2,1)S(1)}, bf16[256,512]{1,0:T(8,128)(2,1)S(1)}, u32[]{:S(2)}, u32[]{:S(2)}) collective-permute-start(bf16[256,512]{1,0:T(8,128)(2,1)S(1)} %get-tuple-element.87), channel_id=1, source_target_pairs={{24,16},{25,17},{26,18},{27,19},{28,20},{29,21},{30,22},{31,23}} | collective-permute-start | bytes 786440 | tf_op jit(solution)/shard_map/ppermute | solution.py:443
  78.2 21.4 %collective-permute-start.28 = (bf16[17,3,16,512]{3,2,1,0:T(8,128)(2,1)S(1)}, bf16[17,3,16,512]{3,2,1,0:T(8,128)(2,1)S(1)}, u32[]{:S(2)}, u32[]{:S(2)}) collective-permute-start(bf16[17,3,16,512]{3,2,1,0:T(8,128)(2,1)S(1)} %get-tuple-element.100.refs_0_), channel_id=1, source_target_pairs={{0,2},{1,3},{2,0},{3,1},{4,6},{5,7},{6,4},{7,5},{8,10},{9,11},{10,... | collective-permute-start | bytes 2506760 | tf_op jit(solution)/shard_map/ppermute | solution.py:44
  82.8 7.7 %collective-permute-start.20 = (bf16[256,512]{1,0:T(8,128)(2,1)S(1)}, bf16[256,512]{1,0:T(8,128)(2,1)S(1)}, u32[]{:S(2)}, u32[]{:S(2)}) collective-permute-start(bf16[256,512]{1,0:T(8,128)(2,1)S(1)} %get-tuple-element.89), channel_id=1, source_target_pairs={{16,8},{17,9},{18,10},{19,11},{20,12},{21,13},{22,14},{23,15}} | collective-permute-start | bytes 786440 | tf_op jit(solution)/shard_map/ppermute | solution.py:442
  86.6 3.9 %collective-permute-start.19 = (bf16[256,512]{1,0:T(8,128)(2,1)S(1)}, bf16[256,512]{1,0:T(8,128)(2,1)S(1)}, u32[]{:S(2)}, u32[]{:S(2)}) collective-permute-start(bf16[256,512]{1,0:T(8,128)(2,1)S(1)} %get-tuple-element.89), channel_id=1, source_target_pairs={{8,0},{24,16},{9,1},{25,17},{10,2},{26,18},{11,3},{27,19},{12,4},{... | collective-permute-start | bytes 786440 | tf_op jit(solution)/shard_map/ppermute | solution.py:443
  87.9 28.5 %collective-permute-start.29 = (bf16[17,3,16,512]{3,2,1,0:T(8,128)(2,1)S(1)}, bf16[17,3,16,512]{3,2,1,0:T(8,128)(2,1)S(1)}, u32[]{:S(2)}, u32[]{:S(2)}) collective-permute-start(bf16[17,3,16,512]{3,2,1,0:T(8,128)(2,1)S(1)} %get-tuple-element.100.refs_0_), channel_id=1, source_target_pairs={{0,6},{1,7},{2,4},{3,5},{4,2},{5,3},{6,0},{7,1},{8,11},{9,10},{10,... | collective-permute-start | bytes 2506760 | tf_op jit(solution)/shard_map/ppermute | solution.py:44
  92.4 7.8 %collective-permute-start.22 = (bf16[256,512]{1,0:T(8,128)(2,1)S(1)}, bf16[256,512]{1,0:T(8,128)(2,1)S(1)}, u32[]{:S(2)}, u32[]{:S(2)}) collective-permute-start(bf16[256,512]{1,0:T(8,128)(2,1)S(1)} %get-tuple-element.91), channel_id=1, source_target_pairs={{16,8},{17,9},{18,10},{19,11},{20,12},{21,13},{22,14},{23,15}} | collective-permute-start | bytes 786440 | tf_op jit(solution)/shard_map/ppermute | solution.py:442
  96.3 4.0 %collective-permute-start.21 = (bf16[256,512]{1,0:T(8,128)(2,1)S(1)}, bf16[256,512]{1,0:T(8,128)(2,1)S(1)}, u32[]{:S(2)}, u32[]{:S(2)}) collective-permute-start(bf16[256,512]{1,0:T(8,128)(2,1)S(1)} %get-tuple-element.91), channel_id=1, source_target_pairs={{8,0},{9,1},{10,2},{11,3},{12,4},{13,5},{14,6},{15,7}} | collective-permute-start | bytes 786440 | tf_op jit(solution)/shard_map/ppermute | solution.py:443
  97.0 43.5 %collective-permute-start.27 = (bf16[17,3,16,512]{3,2,1,0:T(8,128)(2,1)S(1)}, bf16[17,3,16,512]{3,2,1,0:T(8,128)(2,1)S(1)}, u32[]{:S(2)}, u32[]{:S(2)}) collective-permute-start(bf16[17,3,16,512]{3,2,1,0:T(8,128)(2,1)S(1)} %get-tuple-element.100.refs_0_), channel_id=1, source_target_pairs={{0,4},{1,5},{2,6},{3,7},{4,0},{5,1},{6,2},{7,3},{8,9},{9,8},{10,11... | collective-permute-start | bytes 2506760 | tf_op jit(solution)/shard_map/ppermute | solution.py:44
  99.6 40.9 %collective-permute-start.30 = (bf16[17,3,16,512]{3,2,1,0:T(8,128)(2,1)S(1)}, bf16[17,3,16,512]{3,2,1,0:T(8,128)(2,1)S(1)}, u32[]{:S(2)}, u32[]{:S(2)}) collective-permute-start(bf16[17,3,16,512]{3,2,1,0:T(8,128)(2,1)S(1)} %collective-permute-done.28.refs_2_), channel_id=1, source_target_pairs={{24,25},{25,24},{26,27},{27,26},{28,29},{29,28},{30,31},{31,30}} | collective-permute-start | bytes 2506760 | tf_op jit(solution)/shard_map/ppermute | solution.py:44
  100.3 0.7 collective-permute-start.23
  102.4 43.0 %collective-permute-start.24 = (bf16[128,896]{1,0:T(8,128)(2,1)S(1)}, bf16[128,896]{1,0:T(8,128)(2,1)S(1)}, u32[]{:S(2)}, u32[]{:S(2)}) collective-permute-start(bf16[128,896]{1,0:T(8,128)(2,1)S(1)} %get-tuple-element.97), channel_id=1, source_target_pairs={{0,4},{1,5},{2,6},{3,7},{4,0},{5,1},{6,2},{7,3},{8,9},{9,8},{10,11... | collective-permute-start | bytes 688136 | tf_op jit(solution)/shard_map/ppermute | solution.py:44
  103.2 42.2 %collective-permute-start.25 = (bf16[128,896]{1,0:T(8,128)(2,1)S(1)}, bf16[128,896]{1,0:T(8,128)(2,1)S(1)}, u32[]{:S(2)}, u32[]{:S(2)}) collective-permute-start(bf16[128,896]{1,0:T(8,128)(2,1)S(1)} %get-tuple-element.98), channel_id=1, source_target_pairs={{0,2},{1,3},{2,0},{3,1},{4,6},{5,7},{6,4},{7,5},{8,10},{9,11},{10,... | collective-permute-start | bytes 688136 | tf_op jit(solution)/shard_map/ppermute | solution.py:44
  116.4 35.2 %collective-permute-start.26 = (bf16[128,896]{1,0:T(8,128)(2,1)S(1)}, bf16[128,896]{1,0:T(8,128)(2,1)S(1)}, u32[]{:S(2)}, u32[]{:S(2)}) collective-permute-start(bf16[128,896]{1,0:T(8,128)(2,1)S(1)} %get-tuple-element.99), channel_id=1, source_target_pairs={{0,6},{1,7},{2,4},{3,5},{4,2},{5,3},{6,0},{7,1},{8,11},{9,10},{10,... | collective-permute-start | bytes 688136 | tf_op jit(solution)/shard_map/ppermute | solution.py:44
  153.5 6.4 %collective-permute-start.33 = (bf16[1,4,64,512]{3,2,1,0:T(8,128)(2,1)S(1)}, bf16[1,4,64,512]{3,2,1,0:T(8,128)(2,1)S(1)}, u32[]{:S(2)}, u32[]{:S(2)}) collective-permute-start(bf16[1,4,64,512]{3,2,1,0:T(8,128)(2,1)S(1)} %get-tuple-element.108), channel_id=1, source_target_pairs={{0,1},{1,0},{2,3},{3,2},{4,5},{5,4},{6,7},{7,6},{8,12},{9,13},{10,... | collective-permute-start | bytes 786440 | tf_op jit(solution)/shard_map/ppermute | solution.py:44
  155.7 6.4 %collective-permute-start.32 = (bf16[1,3,64,512]{3,2,1,0:T(8,128)(2,1)S(1)}, bf16[1,3,64,512]{3,2,1,0:T(8,128)(2,1)S(1)}, u32[]{:S(2)}, u32[]{:S(2)}) collective-permute-start(bf16[1,3,64,512]{3,2,1,0:T(8,128)(2,1)S(1)} %get-tuple-element.106), channel_id=1, source_target_pairs={{0,1},{1,0},{2,3},{3,2},{4,5},{5,4},{6,7},{7,6},{8,12},{9,13},{10,... | collective-permute-start | bytes 589832 | tf_op jit(solution)/shard_map/ppermute | solution.py:44
  158.3 5.2 %collective-permute-start.31 = (bf16[1,2,64,512]{3,2,1,0:T(8,128)(2,1)S(1)}, bf16[1,2,64,512]{3,2,1,0:T(8,128)(2,1)S(1)}, u32[]{:S(2)}, u32[]{:S(2)}) collective-permute-start(bf16[1,2,64,512]{3,2,1,0:T(8,128)(2,1)S(1)} %get-tuple-element.104), channel_id=1, source_target_pairs={{0,1},{1,0},{2,3},{3,2},{4,5},{5,4},{6,7},{7,6},{8,12},{9,13},{10,... | collective-permute-start | bytes 393224 | tf_op jit(solution)/shard_map/ppermute | solution.py:44
